TPU v7x, 256 devices: a whole 4x4x8 slice. The times are simulated.
256 devices in a mesh: feat: 64 (over x, y_hi, z), tgt: 4 (over y_lo, core).
Axes of the slice: x: 4, y: 4 (y_hi: 2, y_lo: 2; y = y_hi * 2 + y_lo), z: 8, core: 2. Of those that a mesh axis runs over, the one named last changes fastest.
Arguments:
- sources: bfloat16 [4, 128, 2304], P('tgt'), may hold values from -6 to 6
- targets: bfloat16 [4, 128, 2304], P('tgt', 'feat'), may hold values from -6 to 6
- enc_weight: bfloat16 [4, 2304, 16384], P('tgt', None, 'feat'), may hold values from -0.125 to 0.125
- enc_bias: float32 [4, 16384], P('tgt', 'feat'), may hold values from -5 to 5
- dec_weight: bfloat16 [4, 4, 16384, 2304], P('tgt', None, 'feat'), may hold values from -0.046875 to 0.046875
- pair_mask: int32 [4, 4], replicated, may hold values from 0 to 1, as said below
Outputs:
- error: bfloat16 [4, 128, 2304], P('tgt', 'feat')
- latent_grad: bfloat16 [4, 128, 16384], P('tgt', None, 'feat')
Inputs may be any that keep to these rules, and one draw needn't show every extreme that they name: pair_mask[t, s] is 0 wherever s > t and 1 wherever s == t.
All inputs are finite; a program needn't handle non-finite values.
Results may differ from a plain program's by a relative error of at most 0.0055.
Values may be sent and summed in bfloat16 or wider, within the bound.
No kernel may reach another device: no remote copies, remote signals or barrier semaphores. Data moves between devices by JAX's collectives and lax.ppermute only.
A program may use at most 64 MiB of HBM per device.

v0:
```python
import jax
import jax.numpy as jnp
from jax import lax
from jax.sharding import PartitionSpec as P


def per_device(sources, targets, enc_weight, enc_bias, dec_weight, pair_mask):
    layer_count = dec_weight.shape[1]
    width = sources.shape[2]
    rows_local = targets.shape[1]
    pre = jnp.dot(sources[0], enc_weight[0], preferred_element_type=jnp.float32) + enc_bias[0]
    latent = jnp.maximum(pre, 0.0).astype(jnp.bfloat16)
    latent_all = lax.all_gather(latent[None], "tgt", axis=0, tiled=True)
    owner = lax.axis_index("tgt")
    mask_row = lax.dynamic_index_in_dim(pair_mask, owner, 0, keepdims=False)
    total = jnp.zeros((rows_local * lax.axis_size("feat"), width), jnp.float32)
    for recon_source in range(layer_count):
        rows = latent_all[recon_source]
        recon_weight = mask_row[recon_source].astype(jnp.float32)
        total = total + recon_weight * jnp.dot(
            rows, dec_weight[0, recon_source], preferred_element_type=jnp.float32
        )
    share = lax.psum_scatter(total, "feat", scatter_dimension=0, tiled=True)
    err_local = (share - targets[0].astype(jnp.float32)).astype(jnp.bfloat16)
    err_full = lax.all_gather(err_local, "feat", axis=0, tiled=True)
    terms = []
    for source in range(layer_count):
        weight = mask_row[source].astype(jnp.float32)
        term = weight * lax.dot_general(
            err_full,
            dec_weight[0, source],
            (((1,), (1,)), ((), ())),
            preferred_element_type=jnp.float32,
        )
        terms.append(term)
    stacked = jnp.stack(terms)
    grads = lax.psum_scatter(stacked, "tgt", scatter_dimension=0, tiled=True)
    return (err_local[None], grads.astype(jnp.bfloat16))


def solution(mesh):
    in_specs = (
        P("tgt", None, None),
        P("tgt", "feat", None),
        P("tgt", None, "feat"),
        P("tgt", "feat"),
        P("tgt", None, "feat", None),
        P(),
    )
    out_specs = (P("tgt", "feat", None), P("tgt", None, "feat"))
    return jax.shard_map(
        per_device, mesh=mesh, in_specs=in_specs, out_specs=out_specs, check_vma=False
    )
```

profile of v0, /device:TPU:1, one launch (start us, length us, event | category | flops | bytes accessed | tf_op | source)
XLA Modules:
  0.0 911.5 jit_solution(5537049860476209958)
XLA Ops:
  7.2 0.0 copy-start
  7.2 0.0 all-reduce.3.cloned.1.call-start
  7.2 0.8 constant_dynamic-slice_fusion
  8.0 0.7 fusion.65
  9.2 0.0 copy-done
  9.2 1.4 fusion.47
  10.7 8.8 all-gather
  21.5 0.0 copy-start.1
  21.5 1.8 convolution_multiply_fusion.3
  23.2 1.6 fusion.2
  24.8 0.0 copy-done.1
  24.9 0.3 fusion.1
  25.2 1.4 fusion
  26.6 0.0 copy-start.4
  26.6 0.0 copy-start.3
  26.6 0.0 all-reduce.3.cloned.1.call-update
  26.6 0.0 reduce-scatter.2.cloned.1.call-start
  26.6 0.6 copy-done.4
  27.2 0.6 dynamic-slice
  28.5 633.8 %all-reduce.3.cloned.1.call-done = f32[128,2304]{1,0:T(8,128)} async-done(((f32[128,2304]{1,0:T(8,128)}), f32[128,2304]{1,0:T(8,128)}) %all-reduce.3.cloned.1.call-update) | async-done | bytes 1179664
  662.3 0.0 copy-done.3
  662.3 0.9 fusion.64
  663.2 0.0 copy-start.2
  663.2 155.4 %all-gather.1 = bf16[64,2,2304]{2,1,0:T(2,128)(2,1)S(1)} all-gather(bf16[1,2,2304]{2,1,0:T(2,128)(2,1)S(1)} %fusion.64), channel_id=1, replica_groups=mesh['feat'=64,'tgt'=4] {'feat'}, dimensions={0}, use_global_device_ids=true | all-gather | bytes 599040 | tf_op jit(solution)/shard_map/all_gather | solution.py:25
  818.6 0.2 reshape.29
  818.8 1.8 fusion.26
  820.6 0.0 copy-done.2
  820.6 1.8 fusion.32
  822.4 1.8 fusion.38
  824.3 1.8 fusion.44
  826.1 0.8 pad_maximum_fusion
  826.9 0.0 reduce-scatter.2.cloned.1.call-update
  827.0 76.1 %reduce-scatter.2.cloned.1.call-done = f32[1,128,256]{2,1,0:T(8,128)} async-done(((f32[4,128,256]{2,1,0:T(8,128)}), f32[1,128,256]{2,1,0:T(8,128)}) %reduce-scatter.2.cloned.1.call-update) | async-done | bytes 131088 | tf_op jit(solution)/shard_map/reduce_scatter | solution.py:37
  903.1 1.5 convert_element_type.55
Async XLA Ops:
  7.2 2.1 copy-start
  7.2 655.1 %all-reduce.3.cloned.1.call-start = ((), (), s32[]{:S(2)}) async-start(), calls=%async_computation.2 | async-start | bytes 2359296
  21.5 3.4 copy-start.1
  26.6 0.7 copy-start.4
  26.6 635.7 %copy-start.3 = (bf16[1,2,2304]{2,1,0:T(2,128)(2,1)S(1)}, bf16[1,2,2304]{2,1,0:T(2,128)(2,1)}, u32[]{:S(2)}) copy-start(bf16[1,2,2304]{2,1,0:T(2,128)(2,1)} %param.7) | copy-start | bytes 27652
  26.6 876.5 %reduce-scatter.2.cloned.1.call-start = ((), (), s32[]{:S(2)}) async-start(), calls=%async_computation.1 | async-start | bytes 655360 | tf_op jit(solution)/shard_map/reduce_scatter | solution.py:37
  663.2 157.5 %copy-start.2 = (bf16[1,2,2304]{2,1,0:T(2,128)(2,1)}, bf16[1,2,2304]{2,1,0:T(2,128)(2,1)S(1)}, u32[]{:S(2)}) copy-start(bf16[1,2,2304]{2,1,0:T(2,128)(2,1)S(1)} %fusion.64) | copy-start | bytes 27652
Sparse Core Ops, SparseCore 0:
  26.7 635.5 all-reduce.2
  827.1 75.9 reduce-scatter.1
where the time goes:
time: 912 us; the launch traced here: 911 us
  waiting for transfers between devices  710 us (78%)
  blocking collectives  164 us (18%)
  between operations  17.4 us (2%)
  matrix products  13.7 us (2%)
    unnamed x3, waiting for transfers between devices  634 us
    all_gather x1, blocking collectives, per_device(): err_full = lax.all_gather(err_local, 'feat', axis=0, tiled=True)  155 us
    reduce_scatter x1, waiting for transfers between devices, per_device(): grads = lax.psum_scatter(stacked, 'tgt', scatter_dimension=0, tiled=True)  76.1 us
  transfers between devices with their start and end apart: 2, of which 2 were waited for; matrix products, arithmetic and copies ran while one was open for 0% of the time, Pallas kernels for 0%

commit v1 on v0

v1 whole, which is shorter than its diff:
```python
import jax
import jax.numpy as jnp
from jax import lax
from jax.sharding import Mesh, PartitionSpec as P

X, YH, ZH, ZL, TG = 4, 2, 4, 2, 4
NEAR = ("x", "yh", "zl")
FEAT = ("x", "yh", "zh", "zl")
DOT = dict(preferred_element_type=jnp.float32)


def per_device(sources, targets, enc_weight, enc_bias, dec_weight, pair_mask):
    tok, width = sources.shape[1], sources.shape[2]
    feats = enc_weight.shape[2]
    owner = lax.axis_index("tgt")
    spot = lax.axis_index(FEAT)
    rows_local = targets.shape[1]
    group = X * YH * ZL
    rows = tok // group
    mask_row = lax.dynamic_index_in_dim(pair_mask, owner, 0, keepdims=False)

    pre = jnp.dot(sources[0], enc_weight[0], **DOT) + enc_bias[0]
    latent = jnp.maximum(pre, 0.0).astype(jnp.bfloat16)
    dec = dec_weight[0]

    def weight(index):
        return lax.dynamic_index_in_dim(mask_row, index, 0, keepdims=False)

    def slab(index):
        return lax.dynamic_index_in_dim(dec, index, 0, keepdims=False)

    got = {}
    for flip in (2, 3, 1):
        pairs = [(s, s ^ flip) for s in range(TG) if s < (s ^ flip)]
        got[flip] = lax.ppermute(latent, "tgt", pairs)
    got[0] = latent
    total = None
    for flip in (0, 1, 2, 3):
        peer = owner ^ flip
        keep = weight(peer).astype(jnp.float32)
        part = keep * jnp.dot(got[flip], slab(peer), **DOT)
        total = part if total is None else total + part

    row_ids = lax.broadcasted_iota(jnp.int32, (tok, rows_local), 0)
    col_ids = lax.broadcasted_iota(jnp.int32, (tok, rows_local), 1)
    place = (row_ids == spot * rows_local + col_ids).astype(jnp.bfloat16)
    total = total - jnp.dot(place, targets[0], **DOT)

    shares = total.astype(jnp.bfloat16).reshape(group, rows, width)
    shares = lax.all_to_all(shares, NEAR, 0, 0, tiled=True)
    near = jnp.sum(shares.astype(jnp.float32), axis=0)
    spread = jnp.broadcast_to(near[None], (ZH, rows, width))
    spread = lax.all_to_all(spread, "zh", 0, 0, tiled=True)
    err = jnp.sum(spread, axis=0).astype(jnp.bfloat16)
    copies = jnp.broadcast_to(err[None], (group, rows, width))
    err_full = lax.all_to_all(copies, NEAR, 0, 0, tiled=True).reshape(tok, width)
    err_local = lax.dynamic_slice_in_dim(err_full, spot * rows_local, rows_local, 0)

    grad = None
    for flip in (2, 3, 1, 0):
        peer = owner ^ flip
        keep = weight(peer).astype(jnp.float32)
        term = keep * lax.dot_general(err_full, slab(peer), (((1,), (1,)), ((), ())), **DOT)
        if flip:
            pairs = [(t, t ^ flip) for t in range(TG) if t > (t ^ flip)]
            term = lax.ppermute(term, "tgt", pairs)
        grad = term if grad is None else grad + term
    return (err_local[None], grad.astype(jnp.bfloat16)[None])


def solution(mesh):
    grid = Mesh(
        mesh.devices.reshape(X, YH, ZH, ZL, TG), ("x", "yh", "zh", "zl", "tgt")
    )
    in_specs = (
        P("tgt", None, None),
        P("tgt", FEAT, None),
        P("tgt", None, FEAT),
        P("tgt", FEAT),
        P("tgt", None, FEAT, None),
        P(),
    )
    out_specs = (P("tgt", FEAT, None), P("tgt", None, FEAT))
    return jax.shard_map(
        per_device, mesh=grid, in_specs=in_specs, out_specs=out_specs, check_vma=False
    )
```

time: 912 us -> 91.7 us (0.10)
  waiting for transfers between devices: 710 us -> 14.2 us
  blocking collectives: 164 us -> 36.2 us
  starting transfers between devices: 0.08 us -> 19.8 us
  between operations: 17.4 us -> 3.85 us
    unnamed x3 -> x0, waiting for transfers between devices: 634 us -> none
    all_gather x2 -> x0, blocking collectives: 164 us -> none  [the longest x1 155 us: per_device(): err_full = lax.all_gather(err_local, 'feat', axis=0, tiled=True)]
    reduce_scatter x1 -> x0, waiting for transfers between devices: 76.1 us -> none  [per_device(): grads = lax.psum_scatter(stacked, 'tgt', scatter_dimension=0, tiled=True)]
    all_to_all x0 -> x2, blocking collectives: none -> 36.2 us  [the longest x1 19.6 us: per_device(): shares = lax.all_to_all(shares, NEAR, 0, 0, tiled=True)]
    ppermute x0 -> x6, starting transfers between devices: none -> 16.2 us  [the longest x3 9.01 us: per_device(): term = lax.ppermute(term, 'tgt', pairs)]
    all_to_all x0 -> x1, waiting for transfers between devices: none -> 9.26 us  [per_device(): lax.all_to_all(copies, NEAR, 0, 0, tiled=True).reshape(tok, width)]
  transfers between devices with their start and end apart: 2 -> 7, of which waited for: 2 -> 3; matrix products, arithmetic and copies ran while one was open for 0% -> 10% of each run, Pallas kernels for 0% -> 0%
where the time goes in v1:
time: 91.7 us; the launch traced here: 91.1 us
  blocking collectives  36.2 us (39%)
  starting transfers between devices  19.8 us (22%)
  waiting for transfers between devices  14.2 us (15%)
  matrix products  13.5 us (15%)
  between operations  3.85 us (4%)
  local copies, waits for them, and re-layouts  3.43 us (4%)
    all_to_all x1, blocking collectives, per_device(): shares = lax.all_to_all(shares, NEAR, 0, 0, tiled=True)  19.6 us
    all_to_all x1, blocking collectives, per_device(): spread = lax.all_to_all(spread, 'zh', 0, 0, tiled=True)  16.7 us
    all_to_all x1, waiting for transfers between devices, per_device(): lax.all_to_all(copies, NEAR, 0, 0, tiled=True).reshape(tok, width)  9.26 us
    ppermute x3, starting transfers between devices, per_device(): term = lax.ppermute(term, 'tgt', pairs)  9.01 us
    dot_general x4, matrix products, per_device(): lax.dot_general(err_full, slab(peer), (((1,), (1,)), ((), ())), **DOT)  7.89 us
    ppermute x3, starting transfers between devices, per_device(): got[flip] = lax.ppermute(latent, 'tgt', pairs)  7.16 us
    ppermute x3, waiting for transfers between devices, per_device(): term = lax.ppermute(term, 'tgt', pairs)  4.91 us
    dot_general x4, matrix products, per_device(): part = keep * jnp.dot(got[flip], slab(peer), **DOT)  3.93 us
  transfers between devices with their start and end apart: 7, of which 3 were waited for; matrix products, arithmetic and copies ran while one was open for 10% of the time, Pallas kernels for 0%

profile of v1, /device:TPU:1, one launch (start us, length us, event | category | flops | bytes accessed | tf_op | source)
XLA Modules:
  0.0 91.1 jit_solution(1452593758517675358)
XLA Ops:
  0.6 0.0 copy-start
  0.6 0.0 copy-start.3
  0.7 1.3 %copy-done = bf16[1,2304,256]{2,1,0:T(8,128)(2,1)S(1)} copy-done((bf16[1,2304,256]{2,1,0:T(8,128)(2,1)S(1)}, bf16[1,2304,256]{2,1,0:T(8,128)(2,1)}, u32[]{:S(2)}) %copy-start) | copy-done | bytes 1179672
  1.9 1.4 %fusion.38 = bf16[128,256]{1,0:T(8,128)(2,1)S(1)} fusion(bf16[1,2304,256]{2,1,0:T(8,128)(2,1)S(1)} %copy-done, bf16[1,128,2304]{2,1,0:T(8,128)(2,1)} %param.6, f32[256]{0:T(256)} %bitcast.70), kind=kOutput, calls=%fused_computation.31 | convolution fusion | flops 151093248 | bytes 1836032 | tf_op jit(solution)/shard_map/dot_general | solution.py:22
  3.3 4.6 %collective-permute-start.2 = (bf16[128,256]{1,0:T(8,128)(2,1)S(1)}, bf16[128,256]{1,0:T(8,128)(2,1)S(1)}, u32[]{:S(2)}, u32[]{:S(2)}) collective-permute-start(bf16[128,256]{1,0:T(8,128)(2,1)S(1)} %fusion.38), channel_id=1, source_target_pairs={{0,3},{1,2},{4,7},{5,6},{8,11},{9,10},{12,15},{13,14},{16,19},{17,... | collective-permute-start | bytes 196616 | tf_op jit(solution)/shard_map/ppermute | solution.py:35
  7.9 1.3 %collective-permute-start.1 = (bf16[128,256]{1,0:T(8,128)(2,1)S(1)}, bf16[128,256]{1,0:T(8,128)(2,1)S(1)}, u32[]{:S(2)}, u32[]{:S(2)}) collective-permute-start(bf16[128,256]{1,0:T(8,128)(2,1)S(1)} %fusion.38), channel_id=1, source_target_pairs={{0,2},{1,3},{4,6},{5,7},{8,10},{9,11},{12,14},{13,15},{16,18},{17,... | collective-permute-start | bytes 196616 | tf_op jit(solution)/shard_map/ppermute | solution.py:35
  9.2 1.3 %collective-permute-start = (bf16[128,256]{1,0:T(8,128)(2,1)S(1)}, bf16[128,256]{1,0:T(8,128)(2,1)S(1)}, u32[]{:S(2)}, u32[]{:S(2)}) collective-permute-start(bf16[128,256]{1,0:T(8,128)(2,1)S(1)} %fusion.38), channel_id=1, source_target_pairs={{0,1},{2,3},{4,5},{6,7},{8,9},{10,11},{12,13},{14,15},{16,17},{18,... | collective-permute-start | bytes 196616 | tf_op jit(solution)/shard_map/ppermute | solution.py:35
  10.6 0.0 copy-done.3
  10.6 0.7 fusion.68
  11.9 0.0 copy-start.2
  11.9 1.6 %convolution_multiply_fusion.3 = f32[128,2304]{1,0:T(8,128)S(1)} fusion(bf16[128,256]{1,0:T(8,128)(2,1)S(1)} %fusion.38, bf16[1,4,256,2304]{3,2,1,0:T(8,128)(2,1)} %param.10, s32[]{:T(128)S(6)} %select_n.39, f32[]{:T(128)} %bitcast), kind=kOutput, calls=%fused_computation.7 | convolution fusion | flops 151289856 | bytes 2425348 | tf_op jit(solution)/shard_map/dot_general | solution.py:41
  13.5 0.0 copy-done.2
  13.6 0.0 copy-start.1
  13.6 0.3 fusion.53
  16.1 0.0 collective-permute-done
  16.2 1.6 %fusion.3 = f32[128,2304]{1,0:T(8,128)S(1)} fusion(f32[128,2304]{1,0:T(8,128)S(1)} %convolution_multiply_fusion.3, bf16[128,256]{1,0:T(8,128)(2,1)S(1)} %collective-permute-done, bf16[1,4,256,2304]{3,2,1,0:T(8,128)(2,1)} %param.10, s32[]{:T(128)S(6)} %select_n.41, f32[]{:T(128)} %bitcast.5), kind=kOutput, calls=%fused_computation.6 | convolution fusion | flops 151584768 | bytes 3604996 | tf_op jit(solution)/shard_map/dot_general | solution.py:41
  17.8 0.0 collective-permute-done.2
  17.8 0.0 copy-done.1
  17.8 0.3 convolution_multiply_fusion
  18.1 0.0 collective-permute-done.1
  18.2 0.4 fusion.5
  18.5 19.6 %all_to_all.15 = bf16[16,8,2304]{2,1,0:T(8,128)(2,1)S(1)} all-to-all(bf16[16,8,2304]{2,1,0:T(8,128)(2,1)S(1)} %fusion.5), channel_id=1, replica_groups=mesh['x'=4,'yh'=2,'zh'=4,'zl'=2,'tgt'=4] {'x','yh','zl'}, dimensions={0} | all-to-all | bytes 1179648 | tf_op jit(solution)/shard_map/all_to_all | solution.py:50
  38.1 0.1 convert_reduce_fusion
  38.2 16.7 %all_to_all.16 = f32[4,8,2304]{2,1,0:T(8,128)S(1)} all-to-all(f32[4,8,2304]{2,1,0:T(8,128)S(1)} %broadcast_in_dim.8), channel_id=1, replica_groups=mesh['x'=4,'yh'=2,'zh'=4,'zl'=2,'tgt'=4] {'zh'}, dimensions={0} | all-to-all | bytes 589824 | tf_op jit(solution)/shard_map/all_to_all | solution.py:53
  54.9 0.8 broadcast_in_dim.9
  55.8 3.6 %all-to-all-start.2 = ((bf16[16,8,2304]{2,1,0:T(8,128)(2,1)}), bf16[16,8,2304]{2,1,0:T(8,128)(2,1)S(1)}, u32[]{:S(2)}, u32[]{:S(2)}) async-start(bf16[16,8,2304]{2,1,0:T(8,128)(2,1)} %broadcast_in_dim.9), calls=%async_computation.2 | async-start | bytes 1179648 | tf_op jit(solution)/shard_map/all_to_all | solution.py:56
  59.3 9.3 %all-to-all-done.2 = bf16[16,8,2304]{2,1,0:T(8,128)(2,1)S(1)} async-done(((bf16[16,8,2304]{2,1,0:T(8,128)(2,1)}), bf16[16,8,2304]{2,1,0:T(8,128)(2,1)S(1)}, u32[]{:S(2)}, u32[]{:S(2)}) %all-to-all-start.2) | async-done | bytes 589856 | tf_op jit(solution)/shard_map/all_to_all | solution.py:56
  68.6 1.8 %fusion.29 = f32[128,256]{1,0:T(8,128)S(1)} fusion(bf16[1,4,256,2304]{3,2,1,0:T(8,128)(2,1)} %param.10, s32[]{:T(128)S(6)} %select_n.41, f32[]{:T(128)} %bitcast.5, bf16[16,8,2304]{2,1,0:T(8,128)(2,1)S(1)} %all-to-all-done.2), kind=kOutput, calls=%fused_computation.28 | convolution fusion | flops 151027712 | bytes 1901060 | tf_op jit(solution)/shard_map/dot_general | solution.py:63
  70.4 6.4 %collective-permute-start.5 = (f32[128,256]{1,0:T(8,128)S(1)}, f32[128,256]{1,0:T(8,128)S(1)}, u32[]{:S(2)}, u32[]{:S(2)}) collective-permute-start(f32[128,256]{1,0:T(8,128)S(1)} %fusion.29), channel_id=1, source_target_pairs={{1,0},{3,2},{5,4},{7,6},{9,8},{11,10},{13,12},{15,14},{17,16},{19,... | collective-permute-start | bytes 393224 | tf_op jit(solution)/shard_map/ppermute | solution.py:66
  76.8 1.8 %fusion.35 = f32[128,256]{1,0:T(8,128)S(1)} fusion(bf16[1,4,256,2304]{3,2,1,0:T(8,128)(2,1)} %param.10, s32[]{:T(128)S(6)} %select_n.45, f32[]{:T(128)} %bitcast.9, bf16[16,8,2304]{2,1,0:T(8,128)(2,1)S(1)} %all-to-all-done.2), kind=kOutput, calls=%fused_computation.30 | convolution fusion | flops 151027712 | bytes 1901060 | tf_op jit(solution)/shard_map/dot_general | solution.py:63
  78.7 1.3 %collective-permute-start.4 = (f32[128,256]{1,0:T(8,128)S(1)}, f32[128,256]{1,0:T(8,128)S(1)}, u32[]{:S(2)}, u32[]{:S(2)}) collective-permute-start(f32[128,256]{1,0:T(8,128)S(1)} %fusion.35), channel_id=1, source_target_pairs={{2,1},{3,0},{6,5},{7,4},{10,9},{11,8},{14,13},{15,12},{18,17},{19,... | collective-permute-start | bytes 393224 | tf_op jit(solution)/shard_map/ppermute | solution.py:66
  80.0 1.8 %fusion.32 = f32[128,256]{1,0:T(8,128)S(1)} fusion(bf16[1,4,256,2304]{3,2,1,0:T(8,128)(2,1)} %param.10, s32[]{:T(128)S(6)} %select_n.43, f32[]{:T(128)} %bitcast.7, bf16[16,8,2304]{2,1,0:T(8,128)(2,1)S(1)} %all-to-all-done.2), kind=kOutput, calls=%fused_computation.29 | convolution fusion | flops 151027712 | bytes 1901060 | tf_op jit(solution)/shard_map/dot_general | solution.py:63
  81.8 1.3 %collective-permute-start.3 = (f32[128,256]{1,0:T(8,128)S(1)}, f32[128,256]{1,0:T(8,128)S(1)}, u32[]{:S(2)}, u32[]{:S(2)}) collective-permute-start(f32[128,256]{1,0:T(8,128)S(1)} %fusion.32), channel_id=1, source_target_pairs={{2,0},{3,1},{6,4},{7,5},{10,8},{11,9},{14,12},{15,13},{18,16},{19,... | collective-permute-start | bytes 393224 | tf_op jit(solution)/shard_map/ppermute | solution.py:66
  83.1 0.6 dynamic-slice_bitcast_fusion
  83.7 0.0 collective-permute-done.5
  83.7 1.3 %collective-permute-done.4 = f32[128,256]{1,0:T(8,128)S(1)} collective-permute-done((f32[128,256]{1,0:T(8,128)S(1)}, f32[128,256]{1,0:T(8,128)S(1)}, u32[]{:S(2)}, u32[]{:S(2)}) %collective-permute-start.4) | collective-permute-done | bytes 131104 | tf_op jit(solution)/shard_map/ppermute | solution.py:66
  85.0 3.6 %collective-permute-done.3 = f32[128,256]{1,0:T(8,128)S(1)} collective-permute-done((f32[128,256]{1,0:T(8,128)S(1)}, f32[128,256]{1,0:T(8,128)S(1)}, u32[]{:S(2)}, u32[]{:S(2)}) %collective-permute-start.3) | collective-permute-done | bytes 131104 | tf_op jit(solution)/shard_map/ppermute | solution.py:66
  88.6 2.5 %fusion.50 = bf16[1,128,256]{2,1,0:T(8,128)(2,1)} fusion(f32[128,256]{1,0:T(8,128)S(1)} %collective-permute-done.5, f32[128,256]{1,0:T(8,128)S(1)} %collective-permute-done.3, f32[128,256]{1,0:T(8,128)S(1)} %collective-permute-done.4, bf16[1,4,256,2304]{3,2,1,0:T(8,128)(2,1)} %param.10, s32[]{:T(128)S(6)} %select_n.39, f32[]{:T(128)} %bitcast, ...), kind=kOutput, calls=%fused_computation.42 | convolution fusion | flops 151158784 | bytes 2228740 | tf_op jit(solution)/shard_map/dot_general | solution.py:63
  (3 shorter events, 0.0 us)
Async XLA Ops:
  0.6 1.3 %copy-start = (bf16[1,2304,256]{2,1,0:T(8,128)(2,1)S(1)}, bf16[1,2304,256]{2,1,0:T(8,128)(2,1)}, u32[]{:S(2)}) copy-start(bf16[1,2304,256]{2,1,0:T(8,128)(2,1)} %param.8) | copy-start | bytes 3538948
  0.6 9.9 %copy-start.3 = (s32[4,4]{1,0:T(4,128)S(1)}, s32[4,4]{1,0:T(4,128)}, u32[]{:S(2)}) copy-start(s32[4,4]{1,0:T(4,128)} %param.11) | copy-start | bytes 196
  3.3 14.5 %collective-permute-start.2 = (bf16[128,256]{1,0:T(8,128)(2,1)S(1)}, bf16[128,256]{1,0:T(8,128)(2,1)S(1)}, u32[]{:S(2)}, u32[]{:S(2)}) collective-permute-start(bf16[128,256]{1,0:T(8,128)(2,1)S(1)} %fusion.38), channel_id=1, source_target_pairs={{0,3},{1,2},{4,7},{5,6},{8,11},{9,10},{12,15},{13,14},{16,19},{17,... | collective-permute-start | bytes 196616 | tf_op jit(solution)/shard_map/ppermute | solution.py:35
  7.9 10.2 %collective-permute-start.1 = (bf16[128,256]{1,0:T(8,128)(2,1)S(1)}, bf16[128,256]{1,0:T(8,128)(2,1)S(1)}, u32[]{:S(2)}, u32[]{:S(2)}) collective-permute-start(bf16[128,256]{1,0:T(8,128)(2,1)S(1)} %fusion.38), channel_id=1, source_target_pairs={{0,2},{1,3},{4,6},{5,7},{8,10},{9,11},{12,14},{13,15},{16,18},{17,... | collective-permute-start | bytes 196616 | tf_op jit(solution)/shard_map/ppermute | solution.py:35
  9.2 7.0 %collective-permute-start = (bf16[128,256]{1,0:T(8,128)(2,1)S(1)}, bf16[128,256]{1,0:T(8,128)(2,1)S(1)}, u32[]{:S(2)}, u32[]{:S(2)}) collective-permute-start(bf16[128,256]{1,0:T(8,128)(2,1)S(1)} %fusion.38), channel_id=1, source_target_pairs={{0,1},{2,3},{4,5},{6,7},{8,9},{10,11},{12,13},{14,15},{16,17},{18,... | collective-permute-start | bytes 196616 | tf_op jit(solution)/shard_map/ppermute | solution.py:35
  11.9 1.6 %copy-start.2 = (bf16[1,2,2304]{2,1,0:T(2,128)(2,1)S(1)}, bf16[1,2,2304]{2,1,0:T(2,128)(2,1)}, u32[]{:S(2)}) copy-start(bf16[1,2,2304]{2,1,0:T(2,128)(2,1)} %param.7) | copy-start | bytes 27652
  13.6 4.2 %copy-start.1 = (bf16[1,4,256,2304]{3,2,1,0:T(8,128)(2,1)S(1)}, bf16[1,4,256,2304]{3,2,1,0:T(8,128)(2,1)}, u32[]{:S(2)}) copy-start(bf16[1,4,256,2304]{3,2,1,0:T(8,128)(2,1)} %param.10) | copy-start | bytes 14155780
  55.8 12.8 %all-to-all-start.2 = ((bf16[16,8,2304]{2,1,0:T(8,128)(2,1)}), bf16[16,8,2304]{2,1,0:T(8,128)(2,1)S(1)}, u32[]{:S(2)}, u32[]{:S(2)}) async-start(bf16[16,8,2304]{2,1,0:T(8,128)(2,1)} %broadcast_in_dim.9), calls=%async_computation.2 | async-start | bytes 1179648 | tf_op jit(solution)/shard_map/all_to_all | solution.py:56
  70.4 13.3 %collective-permute-start.5 = (f32[128,256]{1,0:T(8,128)S(1)}, f32[128,256]{1,0:T(8,128)S(1)}, u32[]{:S(2)}, u32[]{:S(2)}) collective-permute-start(f32[128,256]{1,0:T(8,128)S(1)} %fusion.29), channel_id=1, source_target_pairs={{1,0},{3,2},{5,4},{7,6},{9,8},{11,10},{13,12},{15,14},{17,16},{19,... | collective-permute-start | bytes 393224 | tf_op jit(solution)/shard_map/ppermute | solution.py:66
  78.7 6.4 %collective-permute-start.4 = (f32[128,256]{1,0:T(8,128)S(1)}, f32[128,256]{1,0:T(8,128)S(1)}, u32[]{:S(2)}, u32[]{:S(2)}) collective-permute-start(f32[128,256]{1,0:T(8,128)S(1)} %fusion.35), channel_id=1, source_target_pairs={{2,1},{3,0},{6,5},{7,4},{10,9},{11,8},{14,13},{15,12},{18,17},{19,... | collective-permute-start | bytes 393224 | tf_op jit(solution)/shard_map/ppermute | solution.py:66
  81.8 6.8 %collective-permute-start.3 = (f32[128,256]{1,0:T(8,128)S(1)}, f32[128,256]{1,0:T(8,128)S(1)}, u32[]{:S(2)}, u32[]{:S(2)}) collective-permute-start(f32[128,256]{1,0:T(8,128)S(1)} %fusion.32), channel_id=1, source_target_pairs={{2,0},{3,1},{6,4},{7,5},{10,8},{11,9},{14,12},{15,13},{18,16},{19,... | collective-permute-start | bytes 393224 | tf_op jit(solution)/shard_map/ppermute | solution.py:66

commit v2 on v1

v2 whole, which is shorter than its diff:
```python
import jax
import jax.numpy as jnp
from jax import lax
from jax.experimental import pallas as pl
from jax.experimental.pallas import tpu as pltpu
from jax.sharding import Mesh, PartitionSpec as P

X, YH, ZH, ZL, TG = 4, 2, 4, 2, 4
NEAR = ("x", "yh", "zl")
FEAT = ("x", "yh", "zh", "zl")
GROUP = X * YH * ZL
DOT = dict(preferred_element_type=jnp.float32)
BF, F32 = jnp.bfloat16, jnp.float32
VMEM = pl.BlockSpec(memory_space=pltpu.VMEM)
ANY = pl.BlockSpec(memory_space=pl.ANY)
SMEM = pl.BlockSpec(memory_space=pltpu.SMEM)
LIMIT = 24 * 1024 * 1024
FLIPS = (1, 2, 3)


def cost(flops, moved):
    return pl.CostEstimate(flops=flops, bytes_accessed=moved, transcendentals=0)


def spot_of():
    index = lax.axis_index("x")
    for name, size in (("yh", YH), ("zh", ZH), ("zl", ZL)):
        index = index * size + lax.axis_index(name)
    return index


def encode_kernel(sources, weight, bias, latent, src, wts, shift, sems):
    chunks = wts.shape[0]
    depth = wts.shape[1]
    last = pltpu.make_async_copy(bias, shift, sems.at[chunks + 1])
    last.start()
    copies = [pltpu.make_async_copy(sources, src, sems.at[chunks])]
    for i in range(chunks):
        part = weight.at[pl.ds(i * depth, depth), :]
        copies.append(pltpu.make_async_copy(part, wts.at[i], sems.at[i]))
    for copy in copies:
        copy.start()
    copies[0].wait()
    total = None
    for i in range(chunks):
        copies[i + 1].wait()
        part = jnp.dot(src[:, pl.ds(i * depth, depth)], wts[i], **DOT)
        total = part if total is None else total + part
    last.wait()
    latent[...] = jnp.maximum(total + shift[...], 0.0).astype(BF)


def load_kernel(dec, held, sem):
    copy = pltpu.make_async_copy(dec, held, sem)
    copy.start()
    copy.wait()


def decode_kernel(mask, l0, l1, l2, l3, targets, dec, out):
    owner = lax.axis_index("tgt")
    base = spot_of() * targets.shape[0]
    tok, width = out.shape
    step = 256
    rows = []
    for flip, ref in enumerate((l0, l1, l2, l3)):
        peer = owner ^ flip
        rows.append((peer, ref[...] * mask[owner, peer].astype(F32).astype(BF)))
    row_ids = lax.broadcasted_iota(jnp.int32, (tok, 1), 0)
    for start in range(0, width, step):
        cols = pl.ds(start, step)
        total = None
        for peer, latent in rows:
            part = jnp.dot(latent, dec[peer, :, cols], **DOT)
            total = part if total is None else total + part
        for r in range(targets.shape[0]):
            own = targets[r : r + 1, cols].astype(F32)
            total = total - jnp.where(row_ids == base + r, own, 0.0)
        out[:, cols] = total.astype(BF)


def gather_sum_kernel(shares, out):
    total = shares[0].astype(F32)
    for i in range(1, shares.shape[0]):
        total = total + shares[i].astype(F32)
    out[...] = total.astype(out.dtype)


def spread_kernel(s0, s1, s2, s3, out):
    total = (s0[...].astype(F32) + s1[...].astype(F32)) + (
        s2[...].astype(F32) + s3[...].astype(F32)
    )
    err = total.astype(BF)
    for i in range(out.shape[0]):
        out[i] = err


def grad_kernel(mask, err, dec, g0, g1, g2, g3):
    owner = lax.axis_index("tgt")
    for flip, ref in ((3, g3), (2, g2), (1, g1), (0, g0)):
        peer = owner ^ flip
        keep = mask[owner, peer].astype(F32)
        term = lax.dot_general(err[...], dec[peer], (((1,), (1,)), ((), ())), **DOT)
        ref[...] = (keep * term).astype(ref.dtype)


def pick_kernel(err, out):
    base = spot_of() * out.shape[0]
    block = pl.multiple_of(base // 16 * 16, 16)
    value = err[pl.ds(block, 16), :].astype(F32)
    row_ids = lax.broadcasted_iota(jnp.int32, (16, 1), 0) + block
    for r in range(out.shape[0]):
        row = jnp.sum(jnp.where(row_ids == base + r, value, 0.0), axis=0, keepdims=True)
        out[r : r + 1, :] = row.astype(out.dtype)


def in_hbm(value):
    return pltpu.with_memory_space_constraint(value, pltpu.HBM)


def call(kernel, outs, specs, flops=0, moved=0, scratch=(), out_spec=VMEM):
    return pl.pallas_call(
        kernel,
        out_shape=outs,
        in_specs=specs,
        out_specs=jax.tree.map(lambda _: out_spec, outs),
        scratch_shapes=scratch,
        cost_estimate=cost(flops, moved),
        compiler_params=pltpu.CompilerParams(vmem_limit_bytes=LIMIT),
    )


def per_device(sources, targets, enc_weight, enc_bias, dec_weight, pair_mask):
    tok, width = sources.shape[1], sources.shape[2]
    feats = enc_weight.shape[2]
    rows_local = targets.shape[1]
    rows = tok // GROUP
    shape = jax.ShapeDtypeStruct

    chunks = 6
    latent = call(
        encode_kernel,
        shape((tok, feats), BF),
        [ANY, ANY, ANY],
        2 * tok * feats * width,
        2 * feats * width,
        scratch=[
            pltpu.VMEM((tok, width), BF),
            pltpu.VMEM((chunks, width // chunks, feats), BF),
            pltpu.VMEM((1, feats), F32),
            pltpu.SemaphoreType.DMA((chunks + 2,)),
        ],
    )(in_hbm(sources[0]), in_hbm(enc_weight[0]), in_hbm(enc_bias))
    dec = call(
        load_kernel,
        shape((TG, feats, width), BF),
        [ANY],
        0,
        2 * TG * feats * width,
        scratch=[pltpu.SemaphoreType.DMA],
        out_spec=ANY,
    )(in_hbm(dec_weight[0]))

    got = [latent]
    for flip in FLIPS:
        pairs = [(s, s ^ flip) for s in range(TG) if s < (s ^ flip)]
        got.append(lax.ppermute(latent, "tgt", pairs))
    flops = 2 * TG * tok * feats * width
    shares = call(
        decode_kernel,
        shape((tok, width), BF),
        [SMEM] + [VMEM] * 6,
        flops,
    )(pair_mask, *got, targets[0], dec)

    shares = shares.reshape(GROUP, rows, width)
    shares = lax.all_to_all(shares, NEAR, 0, 0, tiled=True)
    near = call(gather_sum_kernel, shape((rows, width), BF), [VMEM])(shares)
    parts = [near]
    for flip in FLIPS:
        parts.append(lax.ppermute(near, "zh", [(s, s ^ flip) for s in range(ZH)]))
    copies = call(spread_kernel, shape((GROUP, rows, width), BF), [VMEM] * 4)(*parts)
    err_full = lax.all_to_all(copies, NEAR, 0, 0, tiled=True).reshape(tok, width)

    terms = call(
        grad_kernel,
        [shape((tok, feats), F32)] + [shape((tok, feats), BF)] * 3,
        [SMEM] + [VMEM] * 2,
        flops,
    )(pair_mask, err_full, dec)
    err_local = call(pick_kernel, shape((rows_local, width), BF), [VMEM])(err_full)
    grad = terms[0]
    for flip in (3, 2, 1):
        pairs = [(t, t ^ flip) for t in range(TG) if t > (t ^ flip)]
        grad = grad + lax.ppermute(terms[flip], "tgt", pairs).astype(F32)
    return (err_local[None], grad.astype(BF)[None])


def solution(mesh):
    grid = Mesh(
        mesh.devices.reshape(X, YH, ZH, ZL, TG), ("x", "yh", "zh", "zl", "tgt")
    )
    in_specs = (
        P("tgt", None, None),
        P("tgt", FEAT, None),
        P("tgt", None, FEAT),
        P("tgt", FEAT),
        P("tgt", None, FEAT, None),
        P(),
    )
    out_specs = (P("tgt", FEAT, None), P("tgt", None, FEAT))
    return jax.shard_map(
        per_device, mesh=grid, in_specs=in_specs, out_specs=out_specs, check_vma=False
    )
```

time: 91.7 us -> 72.9 us (0.79)
  matrix products: 13.5 us -> 0 us
  Pallas kernels: 0 us -> 8.8 us
  waiting for transfers between devices: 14.2 us -> 6.17 us
  starting transfers between devices: 19.8 us -> 23.6 us
  blocking collectives: 36.2 us -> 32.6 us
  local copies, waits for them, and re-layouts: 3.43 us -> 0.01 us
  between operations: 3.85 us -> 0.78 us
    dot_general x10 -> x0, matrix products: 13.5 us -> none  [the longest x4 7.89 us: per_device(): lax.dot_general(err_full, slab(peer), (((1,), (1,)), ((), ())), **DOT)]
    all_to_all x1 -> x0, waiting for transfers between devices: 9.26 us -> none  [per_device(): lax.all_to_all(copies, NEAR, 0, 0, tiled=True).reshape(tok, width)]
    pallas_call x0 -> x7, Pallas kernels: none -> 8.8 us  [the longest x1 2.36 us: per_device(): call(load_kernel, shape((TG, feats, width), BF), [ANY], 0, 2 * TG * feats...]
    ppermute x6 -> x9, starting transfers between devices: 16.2 us -> 23.6 us  [the longest x3 9.06 us: per_device(): grad = grad + lax.ppermute(terms[flip], 'tgt', pairs).astype(F32)]
    all_to_all x1, blocking collectives: 16.7 us -> 13 us  [per_device(): lax.all_to_all(copies, NEAR, 0, 0, tiled=True).reshape(tok, width)]
    all_to_all x1 -> x0, starting transfers between devices: 3.58 us -> none  [per_device(): lax.all_to_all(copies, NEAR, 0, 0, tiled=True).reshape(tok, width)]
    broadcast_in_dim x3 -> x0, local copies, waits for them, and re-layouts: 1.49 us -> none  [the longest x1 0.85 us: per_device(): copies = jnp.broadcast_to(err[None], (group, rows, width))]
    unnamed x8 -> x4, local copies, waits for them, and re-layouts: 1.28 us -> 0.01 us
  transfers between devices with their start and end apart: 7 -> 9, of which waited for: 3 -> 2; matrix products, arithmetic and copies ran while one was open for 10% -> 0% of each run, Pallas kernels for 0% -> 4%
where the time goes in v2:
time: 72.9 us; the launch traced here: 72.6 us
  blocking collectives  32.6 us (45%)
  starting transfers between devices  23.6 us (32%)
  Pallas kernels  8.8 us (12%)
  waiting for transfers between devices  6.17 us (8%)
  between operations  0.78 us (1%)
    all_to_all x1, blocking collectives, per_device(): shares = lax.all_to_all(shares, NEAR, 0, 0, tiled=True)  19.5 us
    all_to_all x1, blocking collectives, per_device(): lax.all_to_all(copies, NEAR, 0, 0, tiled=True).reshape(tok, width)  13 us
    ppermute x3, starting transfers between devices, per_device(): grad = grad + lax.ppermute(terms[flip], 'tgt', pairs).astype(F32)  9.06 us
    ppermute x3, starting transfers between devices, per_device(): parts.append(lax.ppermute(near, 'zh', [(s, s ^ flip) for s in range(ZH)]))  7.39 us
    ppermute x3, starting transfers between devices, per_device(): got.append(lax.ppermute(latent, 'tgt', pairs))  7.17 us
    ppermute x3, waiting for transfers between devices, per_device(): parts.append(lax.ppermute(near, 'zh', [(s, s ^ flip) for s in range(ZH)]))  4.75 us
    pallas_call x1, Pallas kernels, per_device(): call(load_kernel, shape((TG, feats, width), BF), [ANY], 0, 2 * TG * feats...  2.36 us
    pallas_call x1, Pallas kernels, per_device(): call(grad_kernel, [shape((tok, feats), F32)] + [shape((tok, feats), BF)]...  2.2 us
  transfers between devices with their start and end apart: 9, of which 2 were waited for; matrix products, arithmetic and copies ran while one was open for 0% of the time, Pallas kernels for 4%

profile of v2, /device:TPU:1, one launch (start us, length us, event | category | flops | bytes accessed | tf_op | source)
XLA Modules:
  0.0 72.6 jit_solution(14314407284546887417)
XLA Ops:
  0.6 2.0 %shard_map.77.l0 = bf16[128,256]{1,0:T(8,128)(2,1)S(1)} custom-call(bf16[128,2304]{1,0:T(8,128)(2,1)} %bitcast.15, bf16[2304,256]{1,0:T(8,128)(2,1)} %bitcast.14, f32[1,256]{1,0:T(1,128)} %bias.1), custom_call_target="tpu_custom_call" | custom-call | flops 150994944 | bytes 1179648 | tf_op jit(solution)/shard_map/pallas_call | solution.py:140
  2.7 4.6 %collective-permute-start.2 = (bf16[128,256]{1,0:T(8,128)(2,1)S(1)}, bf16[128,256]{1,0:T(8,128)(2,1)S(1)}, u32[]{:S(2)}, u32[]{:S(2)}) collective-permute-start(bf16[128,256]{1,0:T(8,128)(2,1)S(1)} %shard_map.77.l0), channel_id=1, source_target_pairs={{0,3},{1,2},{4,7},{5,6},{8,11},{9,10},{12,15},{13,14},{16,19},{17,... | collective-permute-start | bytes 196616 | tf_op jit(solution)/shard_map/ppermute | solution.py:166
  7.2 1.3 %collective-permute-start.1 = (bf16[128,256]{1,0:T(8,128)(2,1)S(1)}, bf16[128,256]{1,0:T(8,128)(2,1)S(1)}, u32[]{:S(2)}, u32[]{:S(2)}) collective-permute-start(bf16[128,256]{1,0:T(8,128)(2,1)S(1)} %shard_map.77.l0), channel_id=1, source_target_pairs={{0,2},{1,3},{4,6},{5,7},{8,10},{9,11},{12,14},{13,15},{16,18},{17,... | collective-permute-start | bytes 196616 | tf_op jit(solution)/shard_map/ppermute | solution.py:166
  8.5 1.3 %collective-permute-start = (bf16[128,256]{1,0:T(8,128)(2,1)S(1)}, bf16[128,256]{1,0:T(8,128)(2,1)S(1)}, u32[]{:S(2)}, u32[]{:S(2)}) collective-permute-start(bf16[128,256]{1,0:T(8,128)(2,1)S(1)} %shard_map.77.l0), channel_id=1, source_target_pairs={{0,1},{2,3},{4,5},{6,7},{8,9},{10,11},{12,13},{14,15},{16,17},{18,... | collective-permute-start | bytes 196616 | tf_op jit(solution)/shard_map/ppermute | solution.py:166
  9.8 0.0 copy-start
  9.9 0.0 copy-start.1
  9.9 2.4 %shard_map.78.dec = bf16[4,256,2304]{2,1,0:T(8,128)(2,1)S(1)} custom-call(bf16[4,256,2304]{2,1,0:T(8,128)(2,1)} %bitcast.13), custom_call_target="tpu_custom_call" | custom-call | bytes 4718592 | tf_op jit(solution)/shard_map/pallas_call | solution.py:153
  12.2 0.0 collective-permute-done.2.l3
  12.2 0.0 collective-permute-done.1.l2
  12.3 0.0 collective-permute-done.l1
  12.3 0.0 copy-done
  12.3 0.0 copy-done.1
  12.3 1.4 %shard_map.79 = bf16[128,2304]{1,0:T(8,128)(2,1)S(1)} custom-call(s32[4,4]{1,0:T(4,128)S(1)} %copy-done.1, bf16[128,256]{1,0:T(8,128)(2,1)S(1)} %shard_map.77.l0, bf16[128,256]{1,0:T(8,128)(2,1)S(1)} %collective-permute-done.l1, bf16[128,256]{1,0:T(8,128)(2,1)S(1)} %collective-permute-done.1.l2, bf16[128,256]{1,0:T(8,128)(2,1)S(1)} %collective-permute-done.2.l3, ...), custom_call_target="tpu_custom_call" | custom-call | flops 603979776 | tf_op jit(solution)/shard_map/pallas_call | solution.py:168
  13.7 19.5 %all_to_all.10.shares = bf16[16,8,2304]{2,1,0:T(8,128)(2,1)S(1)} all-to-all(bf16[16,8,2304]{2,1,0:T(8,128)(2,1)S(1)} %bitcast.11), channel_id=1, replica_groups=mesh['x'=4,'yh'=2,'zh'=4,'zl'=2,'tgt'=4] {'x','yh','zl'}, dimensions={0} | all-to-all | bytes 1179648 | tf_op jit(solution)/shard_map/all_to_all | solution.py:176
  33.2 0.1 shard_map.80.s0
  33.3 5.2 %collective-permute-start.5 = (bf16[8,2304]{1,0:T(8,128)(2,1)S(1)}, bf16[8,2304]{1,0:T(8,128)(2,1)S(1)}, u32[]{:S(2)}, u32[]{:S(2)}) collective-permute-start(bf16[8,2304]{1,0:T(8,128)(2,1)S(1)} %shard_map.80.s0), channel_id=1, source_target_pairs={{0,24},{8,16},{16,8},{24,0},{1,25},{9,17},{17,9},{25,1},{2,26},{10... | collective-permute-start | bytes 110600 | tf_op jit(solution)/shard_map/ppermute | solution.py:180
  38.5 1.2 %collective-permute-start.4 = (bf16[8,2304]{1,0:T(8,128)(2,1)S(1)}, bf16[8,2304]{1,0:T(8,128)(2,1)S(1)}, u32[]{:S(2)}, u32[]{:S(2)}) collective-permute-start(bf16[8,2304]{1,0:T(8,128)(2,1)S(1)} %shard_map.80.s0), channel_id=1, source_target_pairs={{0,16},{8,24},{16,0},{24,8},{1,17},{9,25},{17,1},{25,9},{2,18},{10... | collective-permute-start | bytes 110600 | tf_op jit(solution)/shard_map/ppermute | solution.py:180
  39.7 1.0 %collective-permute-start.3 = (bf16[8,2304]{1,0:T(8,128)(2,1)S(1)}, bf16[8,2304]{1,0:T(8,128)(2,1)S(1)}, u32[]{:S(2)}, u32[]{:S(2)}) collective-permute-start(bf16[8,2304]{1,0:T(8,128)(2,1)S(1)} %shard_map.80.s0), channel_id=1, source_target_pairs={{0,8},{8,0},{16,24},{24,16},{1,9},{9,1},{17,25},{25,17},{2,10},{10... | collective-permute-start | bytes 110600 | tf_op jit(solution)/shard_map/ppermute | solution.py:180
  40.7 0.0 collective-permute-done.5.s3
  40.7 4.7 %collective-permute-done.4.s2 = bf16[8,2304]{1,0:T(8,128)(2,1)S(1)} collective-permute-done((bf16[8,2304]{1,0:T(8,128)(2,1)S(1)}, bf16[8,2304]{1,0:T(8,128)(2,1)S(1)}, u32[]{:S(2)}, u32[]{:S(2)}) %collective-permute-start.4) | collective-permute-done | bytes 36896 | tf_op jit(solution)/shard_map/ppermute | solution.py:180
  45.5 0.0 collective-permute-done.3.s1
  45.5 13.0 %all_to_all.11 = bf16[16,8,2304]{2,1,0:T(8,128)(2,1)S(1)} all-to-all(bf16[16,8,2304]{2,1,0:T(8,128)(2,1)S(1)} %shard_map.81), channel_id=1, replica_groups=mesh['x'=4,'yh'=2,'zh'=4,'zl'=2,'tgt'=4] {'x','yh','zl'}, dimensions={0} | all-to-all | bytes 1179648 | tf_op jit(solution)/shard_map/all_to_all | solution.py:182
  58.5 2.2 %shard_map.83 = (f32[128,256]{1,0:T(8,128)S(1)}, bf16[128,256]{1,0:T(8,128)(2,1)S(1)}, bf16[128,256]{1,0:T(8,128)(2,1)S(1)}, bf16[128,256]{1,0:T(8,128)(2,1)S(1)}) custom-call(s32[4,4]{1,0:T(4,128)S(1)} %copy-done.1, bf16[128,2304]{1,0:T(8,128)(2,1)S(1)} %bitcast.9, bf16[4,256,2304]{2,1,0:T(8,128)(2,1)S(1)} %shard_map.78.dec), custom_call_target="tpu_custom_call" | custom-call | flops 603979776 | tf_op jit(solution)/shard_map/pallas_call | solution.py:184
  60.7 1.3 %collective-permute-start.6 = (bf16[128,256]{1,0:T(8,128)(2,1)S(1)}, bf16[128,256]{1,0:T(8,128)(2,1)S(1)}, u32[]{:S(2)}, u32[]{:S(2)}) collective-permute-start(bf16[128,256]{1,0:T(8,128)(2,1)S(1)} %get-tuple-element.7), channel_id=1, source_target_pairs={{2,1},{3,0},{6,5},{7,4},{10,9},{11,8},{14,13},{15,12},{18,17},{19,... | collective-permute-start | bytes 196616 | tf_op jit(solution)/shard_map/ppermute | solution.py:194
  62.0 1.3 %collective-permute-start.7 = (bf16[128,256]{1,0:T(8,128)(2,1)S(1)}, bf16[128,256]{1,0:T(8,128)(2,1)S(1)}, u32[]{:S(2)}, u32[]{:S(2)}) collective-permute-start(bf16[128,256]{1,0:T(8,128)(2,1)S(1)} %get-tuple-element.8), channel_id=1, source_target_pairs={{2,0},{3,1},{6,4},{7,5},{10,8},{11,9},{14,12},{15,13},{18,16},{19,... | collective-permute-start | bytes 196616 | tf_op jit(solution)/shard_map/ppermute | solution.py:194
  63.3 6.5 %collective-permute-start.8 = (bf16[128,256]{1,0:T(8,128)(2,1)S(1)}, bf16[128,256]{1,0:T(8,128)(2,1)S(1)}, u32[]{:S(2)}, u32[]{:S(2)}) collective-permute-start(bf16[128,256]{1,0:T(8,128)(2,1)S(1)} %get-tuple-element.9), channel_id=1, source_target_pairs={{1,0},{3,2},{5,4},{7,6},{9,8},{11,10},{13,12},{15,14},{17,16},{19,... | collective-permute-start | bytes 196616 | tf_op jit(solution)/shard_map/ppermute | solution.py:194
  69.8 0.7 shard_map.82
  70.5 0.0 collective-permute-done.6
  70.5 1.4 %collective-permute-done.7 = bf16[128,256]{1,0:T(8,128)(2,1)S(1)} collective-permute-done((bf16[128,256]{1,0:T(8,128)(2,1)S(1)}, bf16[128,256]{1,0:T(8,128)(2,1)S(1)}, u32[]{:S(2)}, u32[]{:S(2)}) %collective-permute-start.7) | collective-permute-done | bytes 65568 | tf_op jit(solution)/shard_map/ppermute | solution.py:194
  71.9 0.0 collective-permute-done.8
  71.9 0.7 fusion
  (1 shorter events, 0.0 us)
Async XLA Ops:
  2.7 9.6 %collective-permute-start.2 = (bf16[128,256]{1,0:T(8,128)(2,1)S(1)}, bf16[128,256]{1,0:T(8,128)(2,1)S(1)}, u32[]{:S(2)}, u32[]{:S(2)}) collective-permute-start(bf16[128,256]{1,0:T(8,128)(2,1)S(1)} %shard_map.77.l0), channel_id=1, source_target_pairs={{0,3},{1,2},{4,7},{5,6},{8,11},{9,10},{12,15},{13,14},{16,19},{17,... | collective-permute-start | bytes 196616 | tf_op jit(solution)/shard_map/ppermute | solution.py:166
  7.2 5.0 %collective-permute-start.1 = (bf16[128,256]{1,0:T(8,128)(2,1)S(1)}, bf16[128,256]{1,0:T(8,128)(2,1)S(1)}, u32[]{:S(2)}, u32[]{:S(2)}) collective-permute-start(bf16[128,256]{1,0:T(8,128)(2,1)S(1)} %shard_map.77.l0), channel_id=1, source_target_pairs={{0,2},{1,3},{4,6},{5,7},{8,10},{9,11},{12,14},{13,15},{16,18},{17,... | collective-permute-start | bytes 196616 | tf_op jit(solution)/shard_map/ppermute | solution.py:166
  8.5 3.7 %collective-permute-start = (bf16[128,256]{1,0:T(8,128)(2,1)S(1)}, bf16[128,256]{1,0:T(8,128)(2,1)S(1)}, u32[]{:S(2)}, u32[]{:S(2)}) collective-permute-start(bf16[128,256]{1,0:T(8,128)(2,1)S(1)} %shard_map.77.l0), channel_id=1, source_target_pairs={{0,1},{2,3},{4,5},{6,7},{8,9},{10,11},{12,13},{14,15},{16,17},{18,... | collective-permute-start | bytes 196616 | tf_op jit(solution)/shard_map/ppermute | solution.py:166
  9.8 2.4 %copy-start = (bf16[1,2,2304]{2,1,0:T(2,128)(2,1)S(1)}, bf16[1,2,2304]{2,1,0:T(2,128)(2,1)}, u32[]{:S(2)}) copy-start(bf16[1,2,2304]{2,1,0:T(2,128)(2,1)} %param.7) | copy-start | bytes 27652
  9.9 2.4 %copy-start.1 = (s32[4,4]{1,0:T(4,128)S(1)}, s32[4,4]{1,0:T(4,128)}, u32[]{:S(2)}) copy-start(s32[4,4]{1,0:T(4,128)} %mask.3) | copy-start | bytes 196
  33.3 7.4 %collective-permute-start.5 = (bf16[8,2304]{1,0:T(8,128)(2,1)S(1)}, bf16[8,2304]{1,0:T(8,128)(2,1)S(1)}, u32[]{:S(2)}, u32[]{:S(2)}) collective-permute-start(bf16[8,2304]{1,0:T(8,128)(2,1)S(1)} %shard_map.80.s0), channel_id=1, source_target_pairs={{0,24},{8,16},{16,8},{24,0},{1,25},{9,17},{17,9},{25,1},{2,26},{10... | collective-permute-start | bytes 110600 | tf_op jit(solution)/shard_map/ppermute | solution.py:180
  38.5 6.9 %collective-permute-start.4 = (bf16[8,2304]{1,0:T(8,128)(2,1)S(1)}, bf16[8,2304]{1,0:T(8,128)(2,1)S(1)}, u32[]{:S(2)}, u32[]{:S(2)}) collective-permute-start(bf16[8,2304]{1,0:T(8,128)(2,1)S(1)} %shard_map.80.s0), channel_id=1, source_target_pairs={{0,16},{8,24},{16,0},{24,8},{1,17},{9,25},{17,1},{25,9},{2,18},{10... | collective-permute-start | bytes 110600 | tf_op jit(solution)/shard_map/ppermute | solution.py:180
  39.7 5.8 %collective-permute-start.3 = (bf16[8,2304]{1,0:T(8,128)(2,1)S(1)}, bf16[8,2304]{1,0:T(8,128)(2,1)S(1)}, u32[]{:S(2)}, u32[]{:S(2)}) collective-permute-start(bf16[8,2304]{1,0:T(8,128)(2,1)S(1)} %shard_map.80.s0), channel_id=1, source_target_pairs={{0,8},{8,0},{16,24},{24,16},{1,9},{9,1},{17,25},{25,17},{2,10},{10... | collective-permute-start | bytes 110600 | tf_op jit(solution)/shard_map/ppermute | solution.py:180
  60.7 9.8 %collective-permute-start.6 = (bf16[128,256]{1,0:T(8,128)(2,1)S(1)}, bf16[128,256]{1,0:T(8,128)(2,1)S(1)}, u32[]{:S(2)}, u32[]{:S(2)}) collective-permute-start(bf16[128,256]{1,0:T(8,128)(2,1)S(1)} %get-tuple-element.7), channel_id=1, source_target_pairs={{2,1},{3,0},{6,5},{7,4},{10,9},{11,8},{14,13},{15,12},{18,17},{19,... | collective-permute-start | bytes 196616 | tf_op jit(solution)/shard_map/ppermute | solution.py:194
  62.0 9.9 %collective-permute-start.7 = (bf16[128,256]{1,0:T(8,128)(2,1)S(1)}, bf16[128,256]{1,0:T(8,128)(2,1)S(1)}, u32[]{:S(2)}, u32[]{:S(2)}) collective-permute-start(bf16[128,256]{1,0:T(8,128)(2,1)S(1)} %get-tuple-element.8), channel_id=1, source_target_pairs={{2,0},{3,1},{6,4},{7,5},{10,8},{11,9},{14,12},{15,13},{18,16},{19,... | collective-permute-start | bytes 196616 | tf_op jit(solution)/shard_map/ppermute | solution.py:194
  63.3 8.6 %collective-permute-start.8 = (bf16[128,256]{1,0:T(8,128)(2,1)S(1)}, bf16[128,256]{1,0:T(8,128)(2,1)S(1)}, u32[]{:S(2)}, u32[]{:S(2)}) collective-permute-start(bf16[128,256]{1,0:T(8,128)(2,1)S(1)} %get-tuple-element.9), channel_id=1, source_target_pairs={{1,0},{3,2},{5,4},{7,6},{9,8},{11,10},{13,12},{15,14},{17,16},{19,... | collective-permute-start | bytes 196616 | tf_op jit(solution)/shard_map/ppermute | solution.py:194

commit v3 on v2

--- a/solution.py
+++ b/solution.py
@@ -1,3 +1,5 @@
+import functools
+
 import jax
 import jax.numpy as jnp
 from jax import lax
@@ -13,7 +15,6 @@
 BF, F32 = jnp.bfloat16, jnp.float32
 VMEM = pl.BlockSpec(memory_space=pltpu.VMEM)
 ANY = pl.BlockSpec(memory_space=pl.ANY)
-SMEM = pl.BlockSpec(memory_space=pltpu.SMEM)
 LIMIT = 24 * 1024 * 1024
 FLIPS = (1, 2, 3)
 
@@ -50,31 +51,44 @@
     latent[...] = jnp.maximum(total + shift[...], 0.0).astype(BF)
 
 
-def load_kernel(dec, held, sem):
-    copy = pltpu.make_async_copy(dec, held, sem)
-    copy.start()
-    copy.wait()
-
-
-def decode_kernel(mask, l0, l1, l2, l3, targets, dec, out):
+def load_kernel(mask, latent, dec, held, own, keep, flags, sems):
+    owner = lax.axis_index("tgt")
+    first = pltpu.make_async_copy(mask, flags, sems.at[TG])
+    first.start()
+    copies = []
+    for flip in range(TG):
+        peer = owner ^ flip
+        copies.append(pltpu.make_async_copy(dec.at[peer], held.at[peer], sems.at[flip]))
+    for copy in copies:
+        copy.start()
+    first.wait()
+    for flip in range(TG):
+        value = flags[owner, owner ^ flip].astype(F32)
+        keep[flip] = jnp.full(keep.shape[1:], value, F32)
+    copies[0].wait()
+    rows = latent[...] * keep[0, 0:1, :].astype(BF)
+    own[...] = jnp.dot(rows, held[owner], **DOT)
+    for copy in copies[1:]:
+        copy.wait()
+
+
+def decode_kernel(keep, own, l1, l2, l3, targets, dec, out):
     owner = lax.axis_index("tgt")
     base = spot_of() * targets.shape[0]
     tok, width = out.shape
     step = 256
     rows = []
-    for flip, ref in enumerate((l0, l1, l2, l3)):
-        peer = owner ^ flip
-        rows.append((peer, ref[...] * mask[owner, peer].astype(F32).astype(BF)))
+    for flip, ref in zip(FLIPS, (l1, l2, l3)):
+        rows.append((owner ^ flip, ref[...] * keep[flip, 0:1, :].astype(BF)))
     row_ids = lax.broadcasted_iota(jnp.int32, (tok, 1), 0)
     for start in range(0, width, step):
         cols = pl.ds(start, step)
-        total = None
+        total = own[:, cols]
         for peer, latent in rows:
-            part = jnp.dot(latent, dec[peer, :, cols], **DOT)
-            total = part if total is None else total + part
+            total = total + jnp.dot(latent, dec[peer, :, cols], **DOT)
         for r in range(targets.shape[0]):
-            own = targets[r : r + 1, cols].astype(F32)
-            total = total - jnp.where(row_ids == base + r, own, 0.0)
+            line = targets[r : r + 1, cols].astype(F32)
+            total = total - jnp.where(row_ids == base + r, line, 0.0)
         out[:, cols] = total.astype(BF)
 
 
@@ -94,13 +108,10 @@
         out[i] = err
 
 
-def grad_kernel(mask, err, dec, g0, g1, g2, g3):
-    owner = lax.axis_index("tgt")
-    for flip, ref in ((3, g3), (2, g2), (1, g1), (0, g0)):
-        peer = owner ^ flip
-        keep = mask[owner, peer].astype(F32)
-        term = lax.dot_general(err[...], dec[peer], (((1,), (1,)), ((), ())), **DOT)
-        ref[...] = (keep * term).astype(ref.dtype)
+def grad_kernel(flip, keep, err, dec, out):
+    peer = lax.axis_index("tgt") ^ flip
+    term = lax.dot_general(err[...], dec[peer], (((1,), (1,)), ((), ())), **DOT)
+    out[...] = (keep[flip, 0:1, :] * term).astype(out.dtype)
 
 
 def pick_kernel(err, out):
@@ -113,6 +124,11 @@
         out[r : r + 1, :] = row.astype(out.dtype)
 
 
+def swap(value, name, flip):
+    size = lax.axis_size(name)
+    return lax.ppermute(value, name, [(i, i ^ flip) for i in range(size)])
+
+
 def in_hbm(value):
     return pltpu.with_memory_space_constraint(value, pltpu.HBM)
 
@@ -122,7 +138,7 @@
         kernel,
         out_shape=outs,
         in_specs=specs,
-        out_specs=jax.tree.map(lambda _: out_spec, outs),
+        out_specs=out_spec,
         scratch_shapes=scratch,
         cost_estimate=cost(flops, moved),
         compiler_params=pltpu.CompilerParams(vmem_limit_bytes=LIMIT),
@@ -136,7 +152,7 @@
     rows = tok // GROUP
     shape = jax.ShapeDtypeStruct
 
-    chunks = 6
+    chunks = 3
     latent = call(
         encode_kernel,
         shape((tok, feats), BF),
@@ -150,48 +166,49 @@
             pltpu.SemaphoreType.DMA((chunks + 2,)),
         ],
     )(in_hbm(sources[0]), in_hbm(enc_weight[0]), in_hbm(enc_bias))
-    dec = call(
+    got = {flip: swap(latent, "tgt", flip) for flip in FLIPS}
+    flops = 2 * tok * feats * width
+    dec, own, keep = call(
         load_kernel,
-        shape((TG, feats, width), BF),
-        [ANY],
-        0,
+        [
+            shape((TG, feats, width), BF),
+            shape((tok, width), F32),
+            shape((TG, 8, feats), F32),
+        ],
+        [ANY, VMEM, ANY],
+        flops,
         2 * TG * feats * width,
-        scratch=[pltpu.SemaphoreType.DMA],
-        out_spec=ANY,
-    )(in_hbm(dec_weight[0]))
-
-    got = [latent]
-    for flip in FLIPS:
-        pairs = [(s, s ^ flip) for s in range(TG) if s < (s ^ flip)]
-        got.append(lax.ppermute(latent, "tgt", pairs))
-    flops = 2 * TG * tok * feats * width
+        scratch=[pltpu.SMEM((TG, TG), jnp.int32), pltpu.SemaphoreType.DMA((TG + 1,))],
+        out_spec=[VMEM] * 3,
+    )(in_hbm(pair_mask), latent, in_hbm(dec_weight[0]))
     shares = call(
         decode_kernel,
         shape((tok, width), BF),
-        [SMEM] + [VMEM] * 6,
-        flops,
-    )(pair_mask, *got, targets[0], dec)
+        [VMEM] * 7,
+        3 * flops,
+    )(keep, own, got[1], got[2], got[3], targets[0], dec)
 
     shares = shares.reshape(GROUP, rows, width)
     shares = lax.all_to_all(shares, NEAR, 0, 0, tiled=True)
     near = call(gather_sum_kernel, shape((rows, width), BF), [VMEM])(shares)
-    parts = [near]
-    for flip in FLIPS:
-        parts.append(lax.ppermute(near, "zh", [(s, s ^ flip) for s in range(ZH)]))
+    parts = [near] * ZH
+    for flip in (1, 3, 2):
+        parts[flip] = swap(near, "zh", flip)
     copies = call(spread_kernel, shape((GROUP, rows, width), BF), [VMEM] * 4)(*parts)
     err_full = lax.all_to_all(copies, NEAR, 0, 0, tiled=True).reshape(tok, width)
 
-    terms = call(
-        grad_kernel,
-        [shape((tok, feats), F32)] + [shape((tok, feats), BF)] * 3,
-        [SMEM] + [VMEM] * 2,
-        flops,
-    )(pair_mask, err_full, dec)
+    def term(flip, kind):
+        kernel = functools.partial(grad_kernel, flip)
+        specs = [VMEM] * 3
+        return call(kernel, shape((tok, feats), kind), specs, flops)(
+            keep, err_full, dec
+        )
+
+    back = {flip: swap(term(flip, BF), "tgt", flip) for flip in (3, 2, 1)}
+    grad = term(0, F32)
     err_local = call(pick_kernel, shape((rows_local, width), BF), [VMEM])(err_full)
-    grad = terms[0]
-    for flip in (3, 2, 1):
-        pairs = [(t, t ^ flip) for t in range(TG) if t > (t ^ flip)]
-        grad = grad + lax.ppermute(terms[flip], "tgt", pairs).astype(F32)
+    for flip in FLIPS:
+        grad = grad + back[flip].astype(F32)
     return (err_local[None], grad.astype(BF)[None])
 
 

time: 72.9 us -> 67.7 us (0.929)
  starting transfers between devices: 23.6 us -> 17.6 us
  waiting for transfers between devices: 6.17 us -> 8.34 us
  Pallas kernels: 8.8 us -> 7.94 us
    ppermute x9, starting transfers between devices: 23.6 us -> 17.6 us  [swap(): return lax.ppermute(value, name, [(i, i ^ flip) for i in range(size)])]
    ppermute x9, waiting for transfers between devices: 6.17 us -> 8.34 us  [swap(): return lax.ppermute(value, name, [(i, i ^ flip) for i in range(size)])]
    pallas_call x3 -> x6, Pallas kernels: 5.96 us -> 5.24 us  [the longest x1 2.38 us: per_device(): call(load_kernel, [shape((TG, feats, width), BF), shape((tok, width), F32...]
  transfers between devices with their start and end apart: 9 -> 9, of which waited for: 2 -> 4; matrix products, arithmetic and copies ran while one was open for 0% -> 0% of each run, Pallas kernels for 4% -> 5%
where the time goes in v3:
time: 67.7 us; the launch traced here: 67.4 us
  blocking collectives  32.2 us (48%)
  starting transfers between devices  17.6 us (26%)
  waiting for transfers between devices  8.34 us (12%)
  Pallas kernels  7.94 us (12%)
  between operations  0.7 us (1%)
    all_to_all x1, blocking collectives, per_device(): shares = lax.all_to_all(shares, NEAR, 0, 0, tiled=True)  19.1 us
    ppermute x9, starting transfers between devices, swap(): return lax.ppermute(value, name, [(i, i ^ flip) for i in range(size)])  17.6 us
    all_to_all x1, blocking collectives, per_device(): lax.all_to_all(copies, NEAR, 0, 0, tiled=True).reshape(tok, width)  13.1 us
    ppermute x9, waiting for transfers between devices, swap(): return lax.ppermute(value, name, [(i, i ^ flip) for i in range(size)])  8.34 us
    pallas_call x1, Pallas kernels, per_device(): call(load_kernel, [shape((TG, feats, width), BF), shape((tok, width), F32...  2.38 us
    pallas_call x4, Pallas kernels, term(): call(kernel, shape((tok, feats), kind), specs, flops)(keep, err_full, dec)  2.16 us
    pallas_call x1, Pallas kernels, per_device(): call(encode_kernel, shape((tok, feats), BF), [ANY, ANY, ANY], 2 * tok * f...  1.9 us
  transfers between devices with their start and end apart: 9, of which 4 were waited for; matrix products, arithmetic and copies ran while one was open for 0% of the time, Pallas kernels for 5%

profile of v3, /device:TPU:1, one launch (start us, length us, event | category | flops | bytes accessed | tf_op | source)
XLA Modules:
  0.0 67.4 jit_solution(12306867940199371637)
XLA Ops:
  0.6 0.0 copy-start
  0.6 1.9 %shard_map.77.latent = bf16[128,256]{1,0:T(8,128)(2,1)S(1)} custom-call(bf16[128,2304]{1,0:T(8,128)(2,1)} %bitcast.18, bf16[2304,256]{1,0:T(8,128)(2,1)} %bitcast.17, f32[1,256]{1,0:T(1,128)} %bias.1), custom_call_target="tpu_custom_call" | custom-call | flops 150994944 | bytes 1179648 | tf_op jit(solution)/shard_map/pallas_call | solution.py:156
  2.5 2.8 %collective-permute-start.2 = (bf16[128,256]{1,0:T(8,128)(2,1)S(1)}, bf16[128,256]{1,0:T(8,128)(2,1)S(1)}, u32[]{:S(2)}, u32[]{:S(2)}) collective-permute-start(bf16[128,256]{1,0:T(8,128)(2,1)S(1)} %shard_map.77.latent), channel_id=1, source_target_pairs={{0,3},{1,2},{2,1},{3,0},{4,7},{5,6},{6,5},{7,4},{8,11},{9,10},{10,... | collective-permute-start | bytes 196616 | tf_op jit(solution)/shard_map/ppermute | solution.py:129
  5.3 1.9 %collective-permute-start.1 = (bf16[128,256]{1,0:T(8,128)(2,1)S(1)}, bf16[128,256]{1,0:T(8,128)(2,1)S(1)}, u32[]{:S(2)}, u32[]{:S(2)}) collective-permute-start(bf16[128,256]{1,0:T(8,128)(2,1)S(1)} %shard_map.77.latent), channel_id=1, source_target_pairs={{0,2},{1,3},{2,0},{3,1},{4,6},{5,7},{6,4},{7,5},{8,10},{9,11},{10,... | collective-permute-start | bytes 196616 | tf_op jit(solution)/shard_map/ppermute | solution.py:129
  7.2 0.0 collective-permute-start
  7.2 2.4 %shard_map.78 = (bf16[4,256,2304]{2,1,0:T(8,128)(2,1)S(1)}, f32[128,2304]{1,0:T(8,128)S(1)}, f32[4,8,256]{2,1,0:T(8,128)S(1)}) custom-call(s32[4,4]{1,0:T(4,128)} %mask.1, bf16[128,256]{1,0:T(8,128)(2,1)S(1)} %shard_map.77.latent, bf16[4,256,2304]{2,1,0:T(8,128)(2,1)} %bitcast.16), custom_call_target="tpu_custom_call" | custom-call | flops 150994944 | bytes 4718592 | tf_op jit(solution)/shard_map/pallas_call | solution.py:171
  9.6 0.0 collective-permute-done.2.l3
  9.6 0.9 %collective-permute-done.1.l2 = bf16[128,256]{1,0:T(8,128)(2,1)S(1)} collective-permute-done((bf16[128,256]{1,0:T(8,128)(2,1)S(1)}, bf16[128,256]{1,0:T(8,128)(2,1)S(1)}, u32[]{:S(2)}, u32[]{:S(2)}) %collective-permute-start.1) | collective-permute-done | bytes 65568 | tf_op jit(solution)/shard_map/ppermute | solution.py:129
  10.5 0.0 collective-permute-done.l1
  10.5 0.0 copy-done
  10.5 0.7 %shard_map.79 = bf16[128,2304]{1,0:T(8,128)(2,1)S(1)} custom-call(f32[4,8,256]{2,1,0:T(8,128)S(1)} %get-tuple-element.5.keep, f32[128,2304]{1,0:T(8,128)S(1)} %get-tuple-element.6.own, bf16[128,256]{1,0:T(8,128)(2,1)S(1)} %collective-permute-done.l1, bf16[128,256]{1,0:T(8,128)(2,1)S(1)} %collective-permute-done.1.l2, ...), custom_call_target="tpu_custom_call" | custom-call | flops 452984832 | tf_op jit(solution)/shard_map/pallas_call | solution.py:184
  11.2 19.1 %all_to_all.10.shares = bf16[16,8,2304]{2,1,0:T(8,128)(2,1)S(1)} all-to-all(bf16[16,8,2304]{2,1,0:T(8,128)(2,1)S(1)} %bitcast.14), channel_id=1, replica_groups=mesh['x'=4,'yh'=2,'zh'=4,'zl'=2,'tgt'=4] {'x','yh','zl'}, dimensions={0} | all-to-all | bytes 1179648 | tf_op jit(solution)/shard_map/all_to_all | solution.py:192
  30.3 0.1 shard_map.80.s0
  30.4 5.2 %collective-permute-start.5 = (bf16[8,2304]{1,0:T(8,128)(2,1)S(1)}, bf16[8,2304]{1,0:T(8,128)(2,1)S(1)}, u32[]{:S(2)}, u32[]{:S(2)}) collective-permute-start(bf16[8,2304]{1,0:T(8,128)(2,1)S(1)} %shard_map.80.s0), channel_id=1, source_target_pairs={{0,24},{8,16},{16,8},{24,0},{1,25},{9,17},{17,9},{25,1},{2,26},{10... | collective-permute-start | bytes 110600 | tf_op jit(solution)/shard_map/ppermute | solution.py:129
  35.6 1.2 %collective-permute-start.4 = (bf16[8,2304]{1,0:T(8,128)(2,1)S(1)}, bf16[8,2304]{1,0:T(8,128)(2,1)S(1)}, u32[]{:S(2)}, u32[]{:S(2)}) collective-permute-start(bf16[8,2304]{1,0:T(8,128)(2,1)S(1)} %shard_map.80.s0), channel_id=1, source_target_pairs={{0,16},{8,24},{16,0},{24,8},{1,17},{9,25},{17,1},{25,9},{2,18},{10... | collective-permute-start | bytes 110600 | tf_op jit(solution)/shard_map/ppermute | solution.py:129
  36.7 1.0 %collective-permute-start.3 = (bf16[8,2304]{1,0:T(8,128)(2,1)S(1)}, bf16[8,2304]{1,0:T(8,128)(2,1)S(1)}, u32[]{:S(2)}, u32[]{:S(2)}) collective-permute-start(bf16[8,2304]{1,0:T(8,128)(2,1)S(1)} %shard_map.80.s0), channel_id=1, source_target_pairs={{0,8},{8,0},{16,24},{24,16},{1,9},{9,1},{17,25},{25,17},{2,10},{10... | collective-permute-start | bytes 110600 | tf_op jit(solution)/shard_map/ppermute | solution.py:129
  37.8 0.0 collective-permute-done.5.s3
  37.8 5.1 %collective-permute-done.4.s2 = bf16[8,2304]{1,0:T(8,128)(2,1)S(1)} collective-permute-done((bf16[8,2304]{1,0:T(8,128)(2,1)S(1)}, bf16[8,2304]{1,0:T(8,128)(2,1)S(1)}, u32[]{:S(2)}, u32[]{:S(2)}) %collective-permute-start.4) | collective-permute-done | bytes 36896 | tf_op jit(solution)/shard_map/ppermute | solution.py:129
  42.9 0.0 collective-permute-done.3.s1
  43.0 13.1 %all_to_all.11 = bf16[16,8,2304]{2,1,0:T(8,128)(2,1)S(1)} all-to-all(bf16[16,8,2304]{2,1,0:T(8,128)(2,1)S(1)} %shard_map.81), channel_id=1, replica_groups=mesh['x'=4,'yh'=2,'zh'=4,'zl'=2,'tgt'=4] {'x','yh','zl'}, dimensions={0} | all-to-all | bytes 1179648 | tf_op jit(solution)/shard_map/all_to_all | solution.py:198
  56.1 0.5 shard_map.86
  56.7 0.5 shard_map.85
  57.2 0.5 shard_map.84
  57.7 3.8 %collective-permute-start.6 = (bf16[128,256]{1,0:T(8,128)(2,1)S(1)}, bf16[128,256]{1,0:T(8,128)(2,1)S(1)}, u32[]{:S(2)}, u32[]{:S(2)}) collective-permute-start(bf16[128,256]{1,0:T(8,128)(2,1)S(1)} %shard_map.84), channel_id=1, source_target_pairs={{0,1},{1,0},{2,3},{3,2},{4,5},{5,4},{6,7},{7,6},{8,9},{9,8},{10,11... | collective-permute-start | bytes 196616 | tf_op jit(solution)/shard_map/ppermute | solution.py:129
  61.6 0.4 collective-permute-start.7
  62.0 1.3 %collective-permute-start.8 = (bf16[128,256]{1,0:T(8,128)(2,1)S(1)}, bf16[128,256]{1,0:T(8,128)(2,1)S(1)}, u32[]{:S(2)}, u32[]{:S(2)}) collective-permute-start(bf16[128,256]{1,0:T(8,128)(2,1)S(1)} %shard_map.86), channel_id=1, source_target_pairs={{0,3},{1,2},{2,1},{3,0},{4,7},{5,6},{6,5},{7,4},{8,11},{9,10},{10,... | collective-permute-start | bytes 196616 | tf_op jit(solution)/shard_map/ppermute | solution.py:129
  63.3 0.7 shard_map.82
  64.0 0.5 shard_map.83
  64.5 0.0 collective-permute-done.6
  64.5 0.6 collective-permute-done.7
  65.1 1.7 %collective-permute-done.8 = bf16[128,256]{1,0:T(8,128)(2,1)S(1)} collective-permute-done((bf16[128,256]{1,0:T(8,128)(2,1)S(1)}, bf16[128,256]{1,0:T(8,128)(2,1)S(1)}, u32[]{:S(2)}, u32[]{:S(2)}) %collective-permute-start.8) | collective-permute-done | bytes 65568 | tf_op jit(solution)/shard_map/ppermute | solution.py:129
  66.8 0.7 fusion
  (1 shorter events, 0.0 us)
Async XLA Ops:
  0.6 9.9 %copy-start = (bf16[1,2,2304]{2,1,0:T(2,128)(2,1)S(1)}, bf16[1,2,2304]{2,1,0:T(2,128)(2,1)}, u32[]{:S(2)}) copy-start(bf16[1,2,2304]{2,1,0:T(2,128)(2,1)} %param.7) | copy-start | bytes 27652
  2.5 7.0 %collective-permute-start.2 = (bf16[128,256]{1,0:T(8,128)(2,1)S(1)}, bf16[128,256]{1,0:T(8,128)(2,1)S(1)}, u32[]{:S(2)}, u32[]{:S(2)}) collective-permute-start(bf16[128,256]{1,0:T(8,128)(2,1)S(1)} %shard_map.77.latent), channel_id=1, source_target_pairs={{0,3},{1,2},{2,1},{3,0},{4,7},{5,6},{6,5},{7,4},{8,11},{9,10},{10,... | collective-permute-start | bytes 196616 | tf_op jit(solution)/shard_map/ppermute | solution.py:129
  5.3 5.2 %collective-permute-start.1 = (bf16[128,256]{1,0:T(8,128)(2,1)S(1)}, bf16[128,256]{1,0:T(8,128)(2,1)S(1)}, u32[]{:S(2)}, u32[]{:S(2)}) collective-permute-start(bf16[128,256]{1,0:T(8,128)(2,1)S(1)} %shard_map.77.latent), channel_id=1, source_target_pairs={{0,2},{1,3},{2,0},{3,1},{4,6},{5,7},{6,4},{7,5},{8,10},{9,11},{10,... | collective-permute-start | bytes 196616 | tf_op jit(solution)/shard_map/ppermute | solution.py:129
  7.2 3.3 %collective-permute-start = (bf16[128,256]{1,0:T(8,128)(2,1)S(1)}, bf16[128,256]{1,0:T(8,128)(2,1)S(1)}, u32[]{:S(2)}, u32[]{:S(2)}) collective-permute-start(bf16[128,256]{1,0:T(8,128)(2,1)S(1)} %shard_map.77.latent), channel_id=1, source_target_pairs={{0,1},{1,0},{2,3},{3,2},{4,5},{5,4},{6,7},{7,6},{8,9},{9,8},{10,11... | collective-permute-start | bytes 196616 | tf_op jit(solution)/shard_map/ppermute | solution.py:129
  30.4 7.4 %collective-permute-start.5 = (bf16[8,2304]{1,0:T(8,128)(2,1)S(1)}, bf16[8,2304]{1,0:T(8,128)(2,1)S(1)}, u32[]{:S(2)}, u32[]{:S(2)}) collective-permute-start(bf16[8,2304]{1,0:T(8,128)(2,1)S(1)} %shard_map.80.s0), channel_id=1, source_target_pairs={{0,24},{8,16},{16,8},{24,0},{1,25},{9,17},{17,9},{25,1},{2,26},{10... | collective-permute-start | bytes 110600 | tf_op jit(solution)/shard_map/ppermute | solution.py:129
  35.6 7.3 %collective-permute-start.4 = (bf16[8,2304]{1,0:T(8,128)(2,1)S(1)}, bf16[8,2304]{1,0:T(8,128)(2,1)S(1)}, u32[]{:S(2)}, u32[]{:S(2)}) collective-permute-start(bf16[8,2304]{1,0:T(8,128)(2,1)S(1)} %shard_map.80.s0), channel_id=1, source_target_pairs={{0,16},{8,24},{16,0},{24,8},{1,17},{9,25},{17,1},{25,9},{2,18},{10... | collective-permute-start | bytes 110600 | tf_op jit(solution)/shard_map/ppermute | solution.py:129
  36.7 6.2 %collective-permute-start.3 = (bf16[8,2304]{1,0:T(8,128)(2,1)S(1)}, bf16[8,2304]{1,0:T(8,128)(2,1)S(1)}, u32[]{:S(2)}, u32[]{:S(2)}) collective-permute-start(bf16[8,2304]{1,0:T(8,128)(2,1)S(1)} %shard_map.80.s0), channel_id=1, source_target_pairs={{0,8},{8,0},{16,24},{24,16},{1,9},{9,1},{17,25},{25,17},{2,10},{10... | collective-permute-start | bytes 110600 | tf_op jit(solution)/shard_map/ppermute | solution.py:129
  57.7 6.8 %collective-permute-start.6 = (bf16[128,256]{1,0:T(8,128)(2,1)S(1)}, bf16[128,256]{1,0:T(8,128)(2,1)S(1)}, u32[]{:S(2)}, u32[]{:S(2)}) collective-permute-start(bf16[128,256]{1,0:T(8,128)(2,1)S(1)} %shard_map.84), channel_id=1, source_target_pairs={{0,1},{1,0},{2,3},{3,2},{4,5},{5,4},{6,7},{7,6},{8,9},{9,8},{10,11... | collective-permute-start | bytes 196616 | tf_op jit(solution)/shard_map/ppermute | solution.py:129
  61.6 3.5 %collective-permute-start.7 = (bf16[128,256]{1,0:T(8,128)(2,1)S(1)}, bf16[128,256]{1,0:T(8,128)(2,1)S(1)}, u32[]{:S(2)}, u32[]{:S(2)}) collective-permute-start(bf16[128,256]{1,0:T(8,128)(2,1)S(1)} %shard_map.85), channel_id=1, source_target_pairs={{0,2},{1,3},{2,0},{3,1},{4,6},{5,7},{6,4},{7,5},{8,10},{9,11},{10,... | collective-permute-start | bytes 196616 | tf_op jit(solution)/shard_map/ppermute | solution.py:129
  62.0 4.8 %collective-permute-start.8 = (bf16[128,256]{1,0:T(8,128)(2,1)S(1)}, bf16[128,256]{1,0:T(8,128)(2,1)S(1)}, u32[]{:S(2)}, u32[]{:S(2)}) collective-permute-start(bf16[128,256]{1,0:T(8,128)(2,1)S(1)} %shard_map.86), channel_id=1, source_target_pairs={{0,3},{1,2},{2,1},{3,0},{4,7},{5,6},{6,5},{7,4},{8,11},{9,10},{10,... | collective-permute-start | bytes 196616 | tf_op jit(solution)/shard_map/ppermute | solution.py:129

commit v4 on v3

--- a/solution.py
+++ b/solution.py
@@ -6,6 +6,7 @@
 from jax.experimental import pallas as pl
 from jax.experimental.pallas import tpu as pltpu
 from jax.sharding import Mesh, PartitionSpec as P
+
 
 X, YH, ZH, ZL, TG = 4, 2, 4, 2, 4
 NEAR = ("x", "yh", "zl")
@@ -16,7 +17,6 @@
 VMEM = pl.BlockSpec(memory_space=pltpu.VMEM)
 ANY = pl.BlockSpec(memory_space=pl.ANY)
 LIMIT = 24 * 1024 * 1024
-FLIPS = (1, 2, 3)
 
 
 def cost(flops, moved):
@@ -72,20 +72,30 @@
         copy.wait()
 
 
-def decode_kernel(keep, own, l1, l2, l3, targets, dec, out):
+def decode_pair_kernel(keep, own, l1, l2, dec, out):
     owner = lax.axis_index("tgt")
-    base = spot_of() * targets.shape[0]
-    tok, width = out.shape
     step = 256
     rows = []
-    for flip, ref in zip(FLIPS, (l1, l2, l3)):
+    for flip, ref in ((1, l1), (2, l2)):
         rows.append((owner ^ flip, ref[...] * keep[flip, 0:1, :].astype(BF)))
-    row_ids = lax.broadcasted_iota(jnp.int32, (tok, 1), 0)
-    for start in range(0, width, step):
+    for start in range(0, out.shape[1], step):
         cols = pl.ds(start, step)
         total = own[:, cols]
         for peer, latent in rows:
             total = total + jnp.dot(latent, dec[peer, :, cols], **DOT)
+        out[:, cols] = total
+
+
+def decode_last_kernel(keep, most, l3, targets, dec, out):
+    peer = lax.axis_index("tgt") ^ 3
+    base = spot_of() * targets.shape[0]
+    tok, width = out.shape
+    step = 256
+    latent = l3[...] * keep[3, 0:1, :].astype(BF)
+    row_ids = lax.broadcasted_iota(jnp.int32, (tok, 1), 0)
+    for start in range(0, width, step):
+        cols = pl.ds(start, step)
+        total = most[:, cols] + jnp.dot(latent, dec[peer, :, cols], **DOT)
         for r in range(targets.shape[0]):
             line = targets[r : r + 1, cols].astype(F32)
             total = total - jnp.where(row_ids == base + r, line, 0.0)
@@ -112,6 +122,10 @@
     peer = lax.axis_index("tgt") ^ flip
     term = lax.dot_general(err[...], dec[peer], (((1,), (1,)), ((), ())), **DOT)
     out[...] = (keep[flip, 0:1, :] * term).astype(out.dtype)
+
+
+def join_kernel(a, b, out):
+    out[...] = (a[...] + b[...]).astype(out.dtype)
 
 
 def pick_kernel(err, out):
@@ -166,9 +180,10 @@
             pltpu.SemaphoreType.DMA((chunks + 2,)),
         ],
     )(in_hbm(sources[0]), in_hbm(enc_weight[0]), in_hbm(enc_bias))
-    got = {flip: swap(latent, "tgt", flip) for flip in FLIPS}
+    l2 = swap(latent, "tgt", 2)
+    l1 = swap(latent, "tgt", 1)
     flops = 2 * tok * feats * width
-    dec, own, keep = call(
+    load = call(
         load_kernel,
         [
             shape((TG, feats, width), BF),
@@ -180,19 +195,21 @@
         2 * TG * feats * width,
         scratch=[pltpu.SMEM((TG, TG), jnp.int32), pltpu.SemaphoreType.DMA((TG + 1,))],
         out_spec=[VMEM] * 3,
-    )(in_hbm(pair_mask), latent, in_hbm(dec_weight[0]))
-    shares = call(
-        decode_kernel,
-        shape((tok, width), BF),
-        [VMEM] * 7,
-        3 * flops,
-    )(keep, own, got[1], got[2], got[3], targets[0], dec)
+    )
+    dec, own, keep = load(in_hbm(pair_mask), latent, in_hbm(dec_weight[0]))
+    l3 = swap(l2, "tgt", 1)
+    most = call(decode_pair_kernel, shape((tok, width), F32), [VMEM] * 5, 2 * flops)(
+        keep, own, l1, l2, dec
+    )
+    shares = call(decode_last_kernel, shape((tok, width), BF), [VMEM] * 5, flops)(
+        keep, most, l3, targets[0], dec
+    )
 
     shares = shares.reshape(GROUP, rows, width)
     shares = lax.all_to_all(shares, NEAR, 0, 0, tiled=True)
     near = call(gather_sum_kernel, shape((rows, width), BF), [VMEM])(shares)
     parts = [near] * ZH
-    for flip in (1, 3, 2):
+    for flip in (2, 3, 1):
         parts[flip] = swap(near, "zh", flip)
     copies = call(spread_kernel, shape((GROUP, rows, width), BF), [VMEM] * 4)(*parts)
     err_full = lax.all_to_all(copies, NEAR, 0, 0, tiled=True).reshape(tok, width)
@@ -204,11 +221,16 @@
             keep, err_full, dec
         )
 
-    back = {flip: swap(term(flip, BF), "tgt", flip) for flip in (3, 2, 1)}
-    grad = term(0, F32)
+    diag = term(3, F32)
+    diag = swap(diag, "tgt", 1)
+    far = term(2, F32)
+    far = call(join_kernel, shape((tok, feats), BF), [VMEM] * 2)(far, diag)
+    far = swap(far, "tgt", 2)
+    near = term(1, F32)
+    near = swap(near, "tgt", 1)
+    own = term(0, F32)
     err_local = call(pick_kernel, shape((rows_local, width), BF), [VMEM])(err_full)
-    for flip in FLIPS:
-        grad = grad + back[flip].astype(F32)
+    grad = own + near + far.astype(F32)
     return (err_local[None], grad.astype(BF)[None])
 
 

time: 67.7 us -> 68.5 us (1.012)
  blocking collectives: 32.2 us -> 33.3 us
  waiting for transfers between devices: 8.34 us -> 7.27 us
    all_to_all x1, blocking collectives: 13.1 us -> 14.6 us  [per_device(): lax.all_to_all(copies, NEAR, 0, 0, tiled=True).reshape(tok, width)]
    ppermute x9, waiting for transfers between devices: 8.34 us -> 7.27 us  [swap(): return lax.ppermute(value, name, [(i, i ^ flip) for i in range(size)])]
    pallas_call x2 -> x4, Pallas kernels: 3.09 us -> 3.29 us  [the longest x1 2.38 us: per_device(): dec, own, keep = load(in_hbm(pair_mask), latent, in_hbm(dec_weight[0]))]
  transfers between devices with their start and end apart: 9 -> 9, of which waited for: 4 -> 4; matrix products, arithmetic and copies ran while one was open for 0% -> 0% of each run, Pallas kernels for 5% -> 8%
where the time goes in v4:
time: 68.5 us; the launch traced here: 68.3 us
  blocking collectives  33.3 us (49%)
  starting transfers between devices  18 us (26%)
  Pallas kernels  8.15 us (12%)
  waiting for transfers between devices  7.27 us (11%)
  between operations  0.72 us (1%)
    all_to_all x1, blocking collectives, per_device(): shares = lax.all_to_all(shares, NEAR, 0, 0, tiled=True)  18.7 us
    ppermute x9, starting transfers between devices, swap(): return lax.ppermute(value, name, [(i, i ^ flip) for i in range(size)])  18 us
    all_to_all x1, blocking collectives, per_device(): lax.all_to_all(copies, NEAR, 0, 0, tiled=True).reshape(tok, width)  14.6 us
    ppermute x9, waiting for transfers between devices, swap(): return lax.ppermute(value, name, [(i, i ^ flip) for i in range(size)])  7.27 us
    pallas_call x1, Pallas kernels, per_device(): dec, own, keep = load(in_hbm(pair_mask), latent, in_hbm(dec_weight[0]))  2.38 us
    pallas_call x4, Pallas kernels, term(): call(kernel, shape((tok, feats), kind), specs, flops)(keep, err_full, dec)  2.17 us
    pallas_call x1, Pallas kernels, per_device(): call(encode_kernel, shape((tok, feats), BF), [ANY, ANY, ANY], 2 * tok * f...  1.89 us
  transfers between devices with their start and end apart: 9, of which 4 were waited for; matrix products, arithmetic and copies ran while one was open for 0% of the time, Pallas kernels for 8%

profile of v4, /device:TPU:1, one launch (start us, length us, event | category | flops | bytes accessed | tf_op | source)
XLA Modules:
  0.0 68.3 jit_solution(9469947196921843617)
XLA Ops:
  0.6 1.9 %shard_map.77.latent = bf16[128,256]{1,0:T(8,128)(2,1)S(1)} custom-call(bf16[128,2304]{1,0:T(8,128)(2,1)} %bitcast.18, bf16[2304,256]{1,0:T(8,128)(2,1)} %bitcast.17, f32[1,256]{1,0:T(1,128)} %bias.1), custom_call_target="tpu_custom_call" | custom-call | flops 150994944 | bytes 1179648 | tf_op jit(solution)/shard_map/pallas_call | solution.py:170
  2.5 2.2 %collective-permute-start.1 = (bf16[128,256]{1,0:T(8,128)(2,1)S(1)}, bf16[128,256]{1,0:T(8,128)(2,1)S(1)}, u32[]{:S(2)}, u32[]{:S(2)}) collective-permute-start(bf16[128,256]{1,0:T(8,128)(2,1)S(1)} %shard_map.77.latent), channel_id=1, source_target_pairs={{0,2},{1,3},{2,0},{3,1},{4,6},{5,7},{6,4},{7,5},{8,10},{9,11},{10,... | collective-permute-start | bytes 196616 | tf_op jit(solution)/shard_map/ppermute | solution.py:143
  4.7 1.2 %collective-permute-start = (bf16[128,256]{1,0:T(8,128)(2,1)S(1)}, bf16[128,256]{1,0:T(8,128)(2,1)S(1)}, u32[]{:S(2)}, u32[]{:S(2)}) collective-permute-start(bf16[128,256]{1,0:T(8,128)(2,1)S(1)} %shard_map.77.latent), channel_id=1, source_target_pairs={{0,1},{1,0},{2,3},{3,2},{4,5},{5,4},{6,7},{7,6},{8,9},{9,8},{10,11... | collective-permute-start | bytes 196616 | tf_op jit(solution)/shard_map/ppermute | solution.py:143
  5.9 0.5 collective-permute-done.1.l2
  6.4 3.7 %collective-permute-start.2 = (bf16[128,256]{1,0:T(8,128)(2,1)S(1)}, bf16[128,256]{1,0:T(8,128)(2,1)S(1)}, u32[]{:S(2)}, u32[]{:S(2)}) collective-permute-start(bf16[128,256]{1,0:T(8,128)(2,1)S(1)} %collective-permute-done.1.l2), channel_id=1, source_target_pairs={{0,1},{1,0},{2,3},{3,2},{4,5},{5,4},{6,7},{7,6},{8,9},{9,8},{10,11... | collective-permute-start | bytes 196616 | tf_op jit(solution)/shard_map/ppermute | solution.py:143
  10.1 2.4 %shard_map.78 = (bf16[4,256,2304]{2,1,0:T(8,128)(2,1)S(1)}, f32[128,2304]{1,0:T(8,128)S(1)}, f32[4,8,256]{2,1,0:T(8,128)S(1)}) custom-call(s32[4,4]{1,0:T(4,128)} %mask.1, bf16[128,256]{1,0:T(8,128)(2,1)S(1)} %shard_map.77.latent, bf16[4,256,2304]{2,1,0:T(8,128)(2,1)} %bitcast.16), custom_call_target="tpu_custom_call" | custom-call | flops 150994944 | bytes 4718592 | tf_op jit(solution)/shard_map/pallas_call | solution.py:199
  12.5 0.0 collective-permute-done.l1
  12.5 0.0 copy-start
  12.5 0.5 shard_map.79.most
  13.0 0.0 collective-permute-done.2.l3
  13.0 0.2 copy-done
  13.2 0.4 shard_map.80
  13.6 18.7 %all_to_all.10.shares = bf16[16,8,2304]{2,1,0:T(8,128)(2,1)S(1)} all-to-all(bf16[16,8,2304]{2,1,0:T(8,128)(2,1)S(1)} %bitcast.14), channel_id=1, replica_groups=mesh['x'=4,'yh'=2,'zh'=4,'zl'=2,'tgt'=4] {'x','yh','zl'}, dimensions={0} | all-to-all | bytes 1179648 | tf_op jit(solution)/shard_map/all_to_all | solution.py:209
  32.3 0.1 shard_map.81.s0
  32.4 3.1 %collective-permute-start.3 = (bf16[8,2304]{1,0:T(8,128)(2,1)S(1)}, bf16[8,2304]{1,0:T(8,128)(2,1)S(1)}, u32[]{:S(2)}, u32[]{:S(2)}) collective-permute-start(bf16[8,2304]{1,0:T(8,128)(2,1)S(1)} %shard_map.81.s0), channel_id=1, source_target_pairs={{0,8},{8,0},{16,24},{24,16},{1,9},{9,1},{17,25},{25,17},{2,10},{10... | collective-permute-start | bytes 110600 | tf_op jit(solution)/shard_map/ppermute | solution.py:143
  35.5 4.2 %collective-permute-start.4 = (bf16[8,2304]{1,0:T(8,128)(2,1)S(1)}, bf16[8,2304]{1,0:T(8,128)(2,1)S(1)}, u32[]{:S(2)}, u32[]{:S(2)}) collective-permute-start(bf16[8,2304]{1,0:T(8,128)(2,1)S(1)} %shard_map.81.s0), channel_id=1, source_target_pairs={{0,16},{8,24},{16,0},{24,8},{1,17},{9,25},{17,1},{25,9},{2,18},{10... | collective-permute-start | bytes 110600 | tf_op jit(solution)/shard_map/ppermute | solution.py:143
  39.7 0.0 collective-permute-start.5
  39.7 0.0 collective-permute-done.3.s1
  39.7 2.5 %collective-permute-done.4.s2 = bf16[8,2304]{1,0:T(8,128)(2,1)S(1)} collective-permute-done((bf16[8,2304]{1,0:T(8,128)(2,1)S(1)}, bf16[8,2304]{1,0:T(8,128)(2,1)S(1)}, u32[]{:S(2)}, u32[]{:S(2)}) %collective-permute-start.4) | collective-permute-done | bytes 36896 | tf_op jit(solution)/shard_map/ppermute | solution.py:143
  42.2 2.7 %collective-permute-done.5.s3 = bf16[8,2304]{1,0:T(8,128)(2,1)S(1)} collective-permute-done((bf16[8,2304]{1,0:T(8,128)(2,1)S(1)}, bf16[8,2304]{1,0:T(8,128)(2,1)S(1)}, u32[]{:S(2)}, u32[]{:S(2)}) %collective-permute-start.5) | collective-permute-done | bytes 36896 | tf_op jit(solution)/shard_map/ppermute | solution.py:143
  45.0 14.6 %all_to_all.11 = bf16[16,8,2304]{2,1,0:T(8,128)(2,1)S(1)} all-to-all(bf16[16,8,2304]{2,1,0:T(8,128)(2,1)S(1)} %shard_map.82), channel_id=1, replica_groups=mesh['x'=4,'yh'=2,'zh'=4,'zl'=2,'tgt'=4] {'x','yh','zl'}, dimensions={0} | all-to-all | bytes 1179648 | tf_op jit(solution)/shard_map/all_to_all | solution.py:215
  59.6 0.5 shard_map.87
  60.2 3.0 %collective-permute-start.7 = (f32[128,256]{1,0:T(8,128)S(1)}, f32[128,256]{1,0:T(8,128)S(1)}, u32[]{:S(2)}, u32[]{:S(2)}) collective-permute-start(f32[128,256]{1,0:T(8,128)S(1)} %shard_map.87), channel_id=1, source_target_pairs={{0,1},{1,0},{2,3},{3,2},{4,5},{5,4},{6,7},{7,6},{8,9},{9,8},{10,11... | collective-permute-start | bytes 393224 | tf_op jit(solution)/shard_map/ppermute | solution.py:143
  63.2 0.5 shard_map.85
  63.7 0.1 collective-permute-start.6
  63.8 0.5 shard_map.86.a
  64.4 0.0 collective-permute-done.7.b
  64.4 0.5 collective-permute-start.8
  64.9 0.7 shard_map.83
  65.6 0.5 shard_map.84
  66.1 0.0 collective-permute-done.6
  66.1 1.5 %collective-permute-done.8 = bf16[128,256]{1,0:T(8,128)(2,1)S(1)} collective-permute-done((bf16[128,256]{1,0:T(8,128)(2,1)S(1)}, bf16[128,256]{1,0:T(8,128)(2,1)S(1)}, u32[]{:S(2)}, u32[]{:S(2)}) %collective-permute-start.8) | collective-permute-done | bytes 65568 | tf_op jit(solution)/shard_map/ppermute | solution.py:143
  67.6 0.7 fusion
  (2 shorter events, 0.1 us)
Async XLA Ops:
  2.5 3.9 %collective-permute-start.1 = (bf16[128,256]{1,0:T(8,128)(2,1)S(1)}, bf16[128,256]{1,0:T(8,128)(2,1)S(1)}, u32[]{:S(2)}, u32[]{:S(2)}) collective-permute-start(bf16[128,256]{1,0:T(8,128)(2,1)S(1)} %shard_map.77.latent), channel_id=1, source_target_pairs={{0,2},{1,3},{2,0},{3,1},{4,6},{5,7},{6,4},{7,5},{8,10},{9,11},{10,... | collective-permute-start | bytes 196616 | tf_op jit(solution)/shard_map/ppermute | solution.py:143
  4.7 7.7 %collective-permute-start = (bf16[128,256]{1,0:T(8,128)(2,1)S(1)}, bf16[128,256]{1,0:T(8,128)(2,1)S(1)}, u32[]{:S(2)}, u32[]{:S(2)}) collective-permute-start(bf16[128,256]{1,0:T(8,128)(2,1)S(1)} %shard_map.77.latent), channel_id=1, source_target_pairs={{0,1},{1,0},{2,3},{3,2},{4,5},{5,4},{6,7},{7,6},{8,9},{9,8},{10,11... | collective-permute-start | bytes 196616 | tf_op jit(solution)/shard_map/ppermute | solution.py:143
  6.4 6.6 %collective-permute-start.2 = (bf16[128,256]{1,0:T(8,128)(2,1)S(1)}, bf16[128,256]{1,0:T(8,128)(2,1)S(1)}, u32[]{:S(2)}, u32[]{:S(2)}) collective-permute-start(bf16[128,256]{1,0:T(8,128)(2,1)S(1)} %collective-permute-done.1.l2), channel_id=1, source_target_pairs={{0,1},{1,0},{2,3},{3,2},{4,5},{5,4},{6,7},{7,6},{8,9},{9,8},{10,11... | collective-permute-start | bytes 196616 | tf_op jit(solution)/shard_map/ppermute | solution.py:143
  12.5 0.7 %copy-start = (bf16[1,2,2304]{2,1,0:T(2,128)(2,1)S(1)}, bf16[1,2,2304]{2,1,0:T(2,128)(2,1)}, u32[]{:S(2)}) copy-start(bf16[1,2,2304]{2,1,0:T(2,128)(2,1)} %param.7) | copy-start | bytes 27652
  32.4 7.3 %collective-permute-start.3 = (bf16[8,2304]{1,0:T(8,128)(2,1)S(1)}, bf16[8,2304]{1,0:T(8,128)(2,1)S(1)}, u32[]{:S(2)}, u32[]{:S(2)}) collective-permute-start(bf16[8,2304]{1,0:T(8,128)(2,1)S(1)} %shard_map.81.s0), channel_id=1, source_target_pairs={{0,8},{8,0},{16,24},{24,16},{1,9},{9,1},{17,25},{25,17},{2,10},{10... | collective-permute-start | bytes 110600 | tf_op jit(solution)/shard_map/ppermute | solution.py:143
  35.5 6.8 %collective-permute-start.4 = (bf16[8,2304]{1,0:T(8,128)(2,1)S(1)}, bf16[8,2304]{1,0:T(8,128)(2,1)S(1)}, u32[]{:S(2)}, u32[]{:S(2)}) collective-permute-start(bf16[8,2304]{1,0:T(8,128)(2,1)S(1)} %shard_map.81.s0), channel_id=1, source_target_pairs={{0,16},{8,24},{16,0},{24,8},{1,17},{9,25},{17,1},{25,9},{2,18},{10... | collective-permute-start | bytes 110600 | tf_op jit(solution)/shard_map/ppermute | solution.py:143
  39.7 5.3 %collective-permute-start.5 = (bf16[8,2304]{1,0:T(8,128)(2,1)S(1)}, bf16[8,2304]{1,0:T(8,128)(2,1)S(1)}, u32[]{:S(2)}, u32[]{:S(2)}) collective-permute-start(bf16[8,2304]{1,0:T(8,128)(2,1)S(1)} %shard_map.81.s0), channel_id=1, source_target_pairs={{0,24},{8,16},{16,8},{24,0},{1,25},{9,17},{17,9},{25,1},{2,26},{10... | collective-permute-start | bytes 110600 | tf_op jit(solution)/shard_map/ppermute | solution.py:143
  60.2 4.2 %collective-permute-start.7 = (f32[128,256]{1,0:T(8,128)S(1)}, f32[128,256]{1,0:T(8,128)S(1)}, u32[]{:S(2)}, u32[]{:S(2)}) collective-permute-start(f32[128,256]{1,0:T(8,128)S(1)} %shard_map.87), channel_id=1, source_target_pairs={{0,1},{1,0},{2,3},{3,2},{4,5},{5,4},{6,7},{7,6},{8,9},{9,8},{10,11... | collective-permute-start | bytes 393224 | tf_op jit(solution)/shard_map/ppermute | solution.py:143
  63.7 2.4 %collective-permute-start.6 = (f32[128,256]{1,0:T(8,128)S(1)}, f32[128,256]{1,0:T(8,128)S(1)}, u32[]{:S(2)}, u32[]{:S(2)}) collective-permute-start(f32[128,256]{1,0:T(8,128)S(1)} %shard_map.85), channel_id=1, source_target_pairs={{0,1},{1,0},{2,3},{3,2},{4,5},{5,4},{6,7},{7,6},{8,9},{9,8},{10,11... | collective-permute-start | bytes 393224 | tf_op jit(solution)/shard_map/ppermute | solution.py:143
  64.4 3.2 %collective-permute-start.8 = (bf16[128,256]{1,0:T(8,128)(2,1)S(1)}, bf16[128,256]{1,0:T(8,128)(2,1)S(1)}, u32[]{:S(2)}, u32[]{:S(2)}) collective-permute-start(bf16[128,256]{1,0:T(8,128)(2,1)S(1)} %shard_map.88), channel_id=1, source_target_pairs={{0,2},{1,3},{2,0},{3,1},{4,6},{5,7},{6,4},{7,5},{8,10},{9,11},{10,... | collective-permute-start | bytes 196616 | tf_op jit(solution)/shard_map/ppermute | solution.py:143

commit v5 on v4

--- a/solution.py
+++ b/solution.py
@@ -17,6 +17,7 @@
 VMEM = pl.BlockSpec(memory_space=pltpu.VMEM)
 ANY = pl.BlockSpec(memory_space=pl.ANY)
 LIMIT = 24 * 1024 * 1024
+FLIPS = (1, 2, 3)
 
 
 def cost(flops, moved):
@@ -30,16 +31,18 @@
     return index
 
 
-def encode_kernel(sources, weight, bias, latent, src, wts, shift, sems):
+def encode_kernel(sources, weight, bias, dec, latent, mine, src, wts, shift, sems):
     chunks = wts.shape[0]
     depth = wts.shape[1]
-    last = pltpu.make_async_copy(bias, shift, sems.at[chunks + 1])
-    last.start()
     copies = [pltpu.make_async_copy(sources, src, sems.at[chunks])]
     for i in range(chunks):
         part = weight.at[pl.ds(i * depth, depth), :]
         copies.append(pltpu.make_async_copy(part, wts.at[i], sems.at[i]))
-    for copy in copies:
+    late = [
+        pltpu.make_async_copy(bias, shift, sems.at[chunks + 1]),
+        pltpu.make_async_copy(dec.at[lax.axis_index("tgt")], mine, sems.at[chunks + 2]),
+    ]
+    for copy in copies + late:
         copy.start()
     copies[0].wait()
     total = None
@@ -47,47 +50,47 @@
         copies[i + 1].wait()
         part = jnp.dot(src[:, pl.ds(i * depth, depth)], wts[i], **DOT)
         total = part if total is None else total + part
-    last.wait()
+    late[0].wait()
     latent[...] = jnp.maximum(total + shift[...], 0.0).astype(BF)
-
-
-def load_kernel(mask, latent, dec, held, own, keep, flags, sems):
+    late[1].wait()
+
+
+def load_kernel(mask, latent, mine, dec, held, own, keep, flags, sems):
     owner = lax.axis_index("tgt")
-    first = pltpu.make_async_copy(mask, flags, sems.at[TG])
+    first = pltpu.make_async_copy(mask, flags, sems.at[0])
     first.start()
     copies = []
-    for flip in range(TG):
+    for flip in FLIPS:
         peer = owner ^ flip
-        copies.append(pltpu.make_async_copy(dec.at[peer], held.at[peer], sems.at[flip]))
+        copies.append(
+            pltpu.make_async_copy(dec.at[peer], held.at[flip - 1], sems.at[flip])
+        )
     for copy in copies:
         copy.start()
     first.wait()
     for flip in range(TG):
         value = flags[owner, owner ^ flip].astype(F32)
         keep[flip] = jnp.full(keep.shape[1:], value, F32)
-    copies[0].wait()
     rows = latent[...] * keep[0, 0:1, :].astype(BF)
-    own[...] = jnp.dot(rows, held[owner], **DOT)
-    for copy in copies[1:]:
+    own[...] = jnp.dot(rows, mine[...], **DOT)
+    for copy in copies:
         copy.wait()
 
 
 def decode_pair_kernel(keep, own, l1, l2, dec, out):
-    owner = lax.axis_index("tgt")
     step = 256
     rows = []
     for flip, ref in ((1, l1), (2, l2)):
-        rows.append((owner ^ flip, ref[...] * keep[flip, 0:1, :].astype(BF)))
+        rows.append((flip - 1, ref[...] * keep[flip, 0:1, :].astype(BF)))
     for start in range(0, out.shape[1], step):
         cols = pl.ds(start, step)
         total = own[:, cols]
-        for peer, latent in rows:
-            total = total + jnp.dot(latent, dec[peer, :, cols], **DOT)
+        for slab, latent in rows:
+            total = total + jnp.dot(latent, dec[slab, :, cols], **DOT)
         out[:, cols] = total
 
 
 def decode_last_kernel(keep, most, l3, targets, dec, out):
-    peer = lax.axis_index("tgt") ^ 3
     base = spot_of() * targets.shape[0]
     tok, width = out.shape
     step = 256
@@ -95,7 +98,7 @@
     row_ids = lax.broadcasted_iota(jnp.int32, (tok, 1), 0)
     for start in range(0, width, step):
         cols = pl.ds(start, step)
-        total = most[:, cols] + jnp.dot(latent, dec[peer, :, cols], **DOT)
+        total = most[:, cols] + jnp.dot(latent, dec[2, :, cols], **DOT)
         for r in range(targets.shape[0]):
             line = targets[r : r + 1, cols].astype(F32)
             total = total - jnp.where(row_ids == base + r, line, 0.0)
@@ -109,18 +112,19 @@
     out[...] = total.astype(out.dtype)
 
 
-def spread_kernel(s0, s1, s2, s3, out):
-    total = (s0[...].astype(F32) + s1[...].astype(F32)) + (
-        s2[...].astype(F32) + s3[...].astype(F32)
-    )
-    err = total.astype(BF)
+def pair_kernel(a, b, out):
+    out[...] = a[...].astype(F32) + b[...].astype(F32)
+
+
+def spread_kernel(a, b, out):
+    err = (a[...] + b[...]).astype(BF)
     for i in range(out.shape[0]):
         out[i] = err
 
 
 def grad_kernel(flip, keep, err, dec, out):
-    peer = lax.axis_index("tgt") ^ flip
-    term = lax.dot_general(err[...], dec[peer], (((1,), (1,)), ((), ())), **DOT)
+    slab = dec[flip - 1] if flip else dec[...]
+    term = lax.dot_general(err[...], slab, (((1,), (1,)), ((), ())), **DOT)
     out[...] = (keep[flip, 0:1, :] * term).astype(out.dtype)
 
 
@@ -167,36 +171,38 @@
     shape = jax.ShapeDtypeStruct
 
     chunks = 3
-    latent = call(
+    slabs = in_hbm(dec_weight[0])
+    latent, mine = call(
         encode_kernel,
-        shape((tok, feats), BF),
-        [ANY, ANY, ANY],
+        [shape((tok, feats), BF), shape((feats, width), BF)],
+        [ANY] * 4,
         2 * tok * feats * width,
         2 * feats * width,
         scratch=[
             pltpu.VMEM((tok, width), BF),
             pltpu.VMEM((chunks, width // chunks, feats), BF),
             pltpu.VMEM((1, feats), F32),
-            pltpu.SemaphoreType.DMA((chunks + 2,)),
+            pltpu.SemaphoreType.DMA((chunks + 3,)),
         ],
-    )(in_hbm(sources[0]), in_hbm(enc_weight[0]), in_hbm(enc_bias))
+        out_spec=[VMEM] * 2,
+    )(in_hbm(sources[0]), in_hbm(enc_weight[0]), in_hbm(enc_bias), slabs)
     l2 = swap(latent, "tgt", 2)
     l1 = swap(latent, "tgt", 1)
     flops = 2 * tok * feats * width
     load = call(
         load_kernel,
         [
-            shape((TG, feats, width), BF),
+            shape((TG - 1, feats, width), BF),
             shape((tok, width), F32),
             shape((TG, 8, feats), F32),
         ],
-        [ANY, VMEM, ANY],
+        [ANY, VMEM, VMEM, ANY],
         flops,
         2 * TG * feats * width,
-        scratch=[pltpu.SMEM((TG, TG), jnp.int32), pltpu.SemaphoreType.DMA((TG + 1,))],
+        scratch=[pltpu.SMEM((TG, TG), jnp.int32), pltpu.SemaphoreType.DMA((TG,))],
         out_spec=[VMEM] * 3,
     )
-    dec, own, keep = load(in_hbm(pair_mask), latent, in_hbm(dec_weight[0]))
+    dec, own, keep = load(in_hbm(pair_mask), latent, mine, slabs)
     l3 = swap(l2, "tgt", 1)
     most = call(decode_pair_kernel, shape((tok, width), F32), [VMEM] * 5, 2 * flops)(
         keep, own, l1, l2, dec
@@ -208,17 +214,17 @@
     shares = shares.reshape(GROUP, rows, width)
     shares = lax.all_to_all(shares, NEAR, 0, 0, tiled=True)
     near = call(gather_sum_kernel, shape((rows, width), BF), [VMEM])(shares)
-    parts = [near] * ZH
-    for flip in (2, 3, 1):
-        parts[flip] = swap(near, "zh", flip)
-    copies = call(spread_kernel, shape((GROUP, rows, width), BF), [VMEM] * 4)(*parts)
+    other = swap(near, "zh", 1)
+    pair = call(pair_kernel, shape((rows, width), F32), [VMEM] * 2)(near, other)
+    other = swap(pair, "zh", 3)
+    copies = call(spread_kernel, shape((GROUP, rows, width), BF), [VMEM] * 2)(pair, other)
     err_full = lax.all_to_all(copies, NEAR, 0, 0, tiled=True).reshape(tok, width)
 
     def term(flip, kind):
         kernel = functools.partial(grad_kernel, flip)
         specs = [VMEM] * 3
         return call(kernel, shape((tok, feats), kind), specs, flops)(
-            keep, err_full, dec
+            keep, err_full, dec if flip else mine
         )
 
     diag = term(3, F32)

time: 68.5 us -> 66.8 us (0.975)
  waiting for transfers between devices: 7.27 us -> 5.43 us
  starting transfers between devices: 18 us -> 19.2 us
  blocking collectives: 33.3 us -> 32.6 us
    ppermute x9 -> x8, waiting for transfers between devices: 7.27 us -> 5.43 us  [swap(): return lax.ppermute(value, name, [(i, i ^ flip) for i in range(size)])]
    ppermute x9 -> x8, starting transfers between devices: 18 us -> 19.2 us  [swap(): return lax.ppermute(value, name, [(i, i ^ flip) for i in range(size)])]
    all_to_all x1, blocking collectives: 14.6 us -> 13.9 us  [per_device(): lax.all_to_all(copies, NEAR, 0, 0, tiled=True).reshape(tok, width)]
    pallas_call x7 -> x8, Pallas kernels: 6.48 us -> 6.1 us  [the longest x4 2.15 us: term(): call(kernel, shape((tok, feats), kind), specs, flops)]
  transfers between devices with their start and end apart: 9 -> 8, of which waited for: 4 -> 4; matrix products, arithmetic and copies ran while one was open for 0% -> 0% of each run, Pallas kernels for 8% -> 7%
where the time goes in v5:
time: 66.8 us; the launch traced here: 66.5 us
  blocking collectives  32.6 us (49%)
  starting transfers between devices  19.2 us (29%)
  Pallas kernels  7.75 us (12%)
  waiting for transfers between devices  5.43 us (8%)
  between operations  0.73 us (1%)
    ppermute x8, starting transfers between devices, swap(): return lax.ppermute(value, name, [(i, i ^ flip) for i in range(size)])  19.2 us
    all_to_all x1, blocking collectives, per_device(): shares = lax.all_to_all(shares, NEAR, 0, 0, tiled=True)  18.7 us
    all_to_all x1, blocking collectives, per_device(): lax.all_to_all(copies, NEAR, 0, 0, tiled=True).reshape(tok, width)  13.9 us
    ppermute x8, waiting for transfers between devices, swap(): return lax.ppermute(value, name, [(i, i ^ flip) for i in range(size)])  5.43 us
    pallas_call x4, Pallas kernels, term(): call(kernel, shape((tok, feats), kind), specs, flops)  2.15 us
    pallas_call x1, Pallas kernels, per_device(): dec, own, keep = load(in_hbm(pair_mask), latent, mine, slabs)  2.01 us
    pallas_call x1, Pallas kernels, per_device(): call(encode_kernel, [shape((tok, feats), BF), shape((feats, width), BF)],...  1.88 us
  transfers between devices with their start and end apart: 8, of which 4 were waited for; matrix products, arithmetic and copies ran while one was open for 0% of the time, Pallas kernels for 7%

profile of v5, /device:TPU:1, one launch (start us, length us, event | category | flops | bytes accessed | tf_op | source)
XLA Modules:
  0.0 66.5 jit_solution(14172000889160774767)
XLA Ops:
  0.6 1.9 %shard_map.77 = (bf16[128,256]{1,0:T(8,128)(2,1)S(1)}, bf16[256,2304]{1,0:T(8,128)(2,1)S(1)}) custom-call(bf16[128,2304]{1,0:T(8,128)(2,1)} %bitcast.19, bf16[2304,256]{1,0:T(8,128)(2,1)} %bitcast.18, f32[1,256]{1,0:T(1,128)} %bias.1, bf16[4,256,2304]{2,1,0:T(8,128)(2,1)} %bitcast.16), custom_call_target="tpu_custom_call" | custom-call | flops 150994944 | bytes 1179648 | tf_op jit(solution)/shard_map/pallas_call | solution.py:175
  2.5 2.2 %collective-permute-start.1 = (bf16[128,256]{1,0:T(8,128)(2,1)S(1)}, bf16[128,256]{1,0:T(8,128)(2,1)S(1)}, u32[]{:S(2)}, u32[]{:S(2)}) collective-permute-start(bf16[128,256]{1,0:T(8,128)(2,1)S(1)} %get-tuple-element.7.latent), channel_id=1, source_target_pairs={{0,2},{1,3},{2,0},{3,1},{4,6},{5,7},{6,4},{7,5},{8,10},{9,11},{10,... | collective-permute-start | bytes 196616 | tf_op jit(solution)/shard_map/ppermute | solution.py:147
  4.7 1.2 %collective-permute-start = (bf16[128,256]{1,0:T(8,128)(2,1)S(1)}, bf16[128,256]{1,0:T(8,128)(2,1)S(1)}, u32[]{:S(2)}, u32[]{:S(2)}) collective-permute-start(bf16[128,256]{1,0:T(8,128)(2,1)S(1)} %get-tuple-element.7.latent), channel_id=1, source_target_pairs={{0,1},{1,0},{2,3},{3,2},{4,5},{5,4},{6,7},{7,6},{8,9},{9,8},{10,11... | collective-permute-start | bytes 196616 | tf_op jit(solution)/shard_map/ppermute | solution.py:147
  5.9 0.5 collective-permute-done.1.l2
  6.4 3.7 %collective-permute-start.2 = (bf16[128,256]{1,0:T(8,128)(2,1)S(1)}, bf16[128,256]{1,0:T(8,128)(2,1)S(1)}, u32[]{:S(2)}, u32[]{:S(2)}) collective-permute-start(bf16[128,256]{1,0:T(8,128)(2,1)S(1)} %collective-permute-done.1.l2), channel_id=1, source_target_pairs={{0,1},{1,0},{2,3},{3,2},{4,5},{5,4},{6,7},{7,6},{8,9},{9,8},{10,11... | collective-permute-start | bytes 196616 | tf_op jit(solution)/shard_map/ppermute | solution.py:147
  10.1 2.0 %shard_map.78 = (bf16[3,256,2304]{2,1,0:T(8,128)(2,1)S(1)}, f32[128,2304]{1,0:T(8,128)S(1)}, f32[4,8,256]{2,1,0:T(8,128)S(1)}) custom-call(s32[4,4]{1,0:T(4,128)} %mask.1, bf16[128,256]{1,0:T(8,128)(2,1)S(1)} %get-tuple-element.7.latent, bf16[256,2304]{1,0:T(8,128)(2,1)S(1)} %get-tuple-element.8.mine.dec, bf16[4,256,2304]{2,1,0:T(8,128)(2,1)} %bitcast.17), custom_call_target="tpu_custom_call" | custom-call | flops 150994944 | bytes 4718592 | tf_op jit(solution)/shard_map/pallas_call | solution.py:205
  12.1 0.0 collective-permute-done.l1
  12.1 0.0 copy-start
  12.1 0.5 shard_map.79.most
  12.6 0.0 collective-permute-done.2.l3
  12.6 0.2 copy-done
  12.8 0.4 shard_map.80
  13.2 18.7 %all_to_all.10.shares = bf16[16,8,2304]{2,1,0:T(8,128)(2,1)S(1)} all-to-all(bf16[16,8,2304]{2,1,0:T(8,128)(2,1)S(1)} %bitcast.14), channel_id=1, replica_groups=mesh['x'=4,'yh'=2,'zh'=4,'zl'=2,'tgt'=4] {'x','yh','zl'}, dimensions={0} | all-to-all | bytes 1179648 | tf_op jit(solution)/shard_map/all_to_all | solution.py:215
  31.9 0.1 shard_map.81.a
  32.0 3.1 %collective-permute-start.3 = (bf16[8,2304]{1,0:T(8,128)(2,1)S(1)}, bf16[8,2304]{1,0:T(8,128)(2,1)S(1)}, u32[]{:S(2)}, u32[]{:S(2)}) collective-permute-start(bf16[8,2304]{1,0:T(8,128)(2,1)S(1)} %shard_map.81.a), channel_id=1, source_target_pairs={{0,8},{8,0},{16,24},{24,16},{1,9},{9,1},{17,25},{25,17},{2,10},{10... | collective-permute-start | bytes 110600 | tf_op jit(solution)/shard_map/ppermute | solution.py:147
  35.1 1.4 %collective-permute-done.3.b = bf16[8,2304]{1,0:T(8,128)(2,1)S(1)} collective-permute-done((bf16[8,2304]{1,0:T(8,128)(2,1)S(1)}, bf16[8,2304]{1,0:T(8,128)(2,1)S(1)}, u32[]{:S(2)}, u32[]{:S(2)}) %collective-permute-start.3) | collective-permute-done | bytes 36896 | tf_op jit(solution)/shard_map/ppermute | solution.py:147
  36.5 4.6 %collective-permute-start.4 = (f32[8,2304]{1,0:T(8,128)S(1)}, f32[8,2304]{1,0:T(8,128)S(1)}, u32[]{:S(2)}, u32[]{:S(2)}) collective-permute-start(f32[8,2304]{1,0:T(8,128)S(1)} %shard_map.82.a), channel_id=1, source_target_pairs={{0,24},{8,16},{16,8},{24,0},{1,25},{9,17},{17,9},{25,1},{2,26},{10... | collective-permute-start | bytes 221192 | tf_op jit(solution)/shard_map/ppermute | solution.py:147
  41.0 2.1 %collective-permute-done.4.b = f32[8,2304]{1,0:T(8,128)S(1)} collective-permute-done((f32[8,2304]{1,0:T(8,128)S(1)}, f32[8,2304]{1,0:T(8,128)S(1)}, u32[]{:S(2)}, u32[]{:S(2)}) %collective-permute-start.4) | collective-permute-done | bytes 73760 | tf_op jit(solution)/shard_map/ppermute | solution.py:147
  43.2 13.9 %all_to_all.11 = bf16[16,8,2304]{2,1,0:T(8,128)(2,1)S(1)} all-to-all(bf16[16,8,2304]{2,1,0:T(8,128)(2,1)S(1)} %shard_map.83), channel_id=1, replica_groups=mesh['x'=4,'yh'=2,'zh'=4,'zl'=2,'tgt'=4] {'x','yh','zl'}, dimensions={0} | all-to-all | bytes 1179648 | tf_op jit(solution)/shard_map/all_to_all | solution.py:221
  57.0 0.5 shard_map.88
  57.6 3.9 %collective-permute-start.6 = (f32[128,256]{1,0:T(8,128)S(1)}, f32[128,256]{1,0:T(8,128)S(1)}, u32[]{:S(2)}, u32[]{:S(2)}) collective-permute-start(f32[128,256]{1,0:T(8,128)S(1)} %shard_map.88), channel_id=1, source_target_pairs={{0,1},{1,0},{2,3},{3,2},{4,5},{5,4},{6,7},{7,6},{8,9},{9,8},{10,11... | collective-permute-start | bytes 393224 | tf_op jit(solution)/shard_map/ppermute | solution.py:147
  61.5 0.5 shard_map.86
  62.0 0.1 collective-permute-start.5
  62.1 0.5 shard_map.87.a
  62.7 0.0 collective-permute-done.6.b
  62.7 0.5 collective-permute-start.7
  63.2 0.7 %shard_map.84 = bf16[2,2304]{1,0:T(2,128)(2,1)} custom-call(bf16[128,2304]{1,0:T(8,128)(2,1)S(1)} %bitcast.12), custom_call_target="tpu_custom_call" | custom-call | tf_op jit(solution)/shard_map/pallas_call | solution.py:238
  63.8 0.5 shard_map.85
  64.4 0.0 collective-permute-done.5
  64.4 1.5 %collective-permute-done.7 = bf16[128,256]{1,0:T(8,128)(2,1)S(1)} collective-permute-done((bf16[128,256]{1,0:T(8,128)(2,1)S(1)}, bf16[128,256]{1,0:T(8,128)(2,1)S(1)}, u32[]{:S(2)}, u32[]{:S(2)}) %collective-permute-start.7) | collective-permute-done | bytes 65568 | tf_op jit(solution)/shard_map/ppermute | solution.py:147
  65.9 0.7 fusion
  (3 shorter events, 0.1 us)
Async XLA Ops:
  2.5 3.9 %collective-permute-start.1 = (bf16[128,256]{1,0:T(8,128)(2,1)S(1)}, bf16[128,256]{1,0:T(8,128)(2,1)S(1)}, u32[]{:S(2)}, u32[]{:S(2)}) collective-permute-start(bf16[128,256]{1,0:T(8,128)(2,1)S(1)} %get-tuple-element.7.latent), channel_id=1, source_target_pairs={{0,2},{1,3},{2,0},{3,1},{4,6},{5,7},{6,4},{7,5},{8,10},{9,11},{10,... | collective-permute-start | bytes 196616 | tf_op jit(solution)/shard_map/ppermute | solution.py:147
  4.7 7.4 %collective-permute-start = (bf16[128,256]{1,0:T(8,128)(2,1)S(1)}, bf16[128,256]{1,0:T(8,128)(2,1)S(1)}, u32[]{:S(2)}, u32[]{:S(2)}) collective-permute-start(bf16[128,256]{1,0:T(8,128)(2,1)S(1)} %get-tuple-element.7.latent), channel_id=1, source_target_pairs={{0,1},{1,0},{2,3},{3,2},{4,5},{5,4},{6,7},{7,6},{8,9},{9,8},{10,11... | collective-permute-start | bytes 196616 | tf_op jit(solution)/shard_map/ppermute | solution.py:147
  6.4 6.2 %collective-permute-start.2 = (bf16[128,256]{1,0:T(8,128)(2,1)S(1)}, bf16[128,256]{1,0:T(8,128)(2,1)S(1)}, u32[]{:S(2)}, u32[]{:S(2)}) collective-permute-start(bf16[128,256]{1,0:T(8,128)(2,1)S(1)} %collective-permute-done.1.l2), channel_id=1, source_target_pairs={{0,1},{1,0},{2,3},{3,2},{4,5},{5,4},{6,7},{7,6},{8,9},{9,8},{10,11... | collective-permute-start | bytes 196616 | tf_op jit(solution)/shard_map/ppermute | solution.py:147
  12.1 0.7 %copy-start = (bf16[1,2,2304]{2,1,0:T(2,128)(2,1)S(1)}, bf16[1,2,2304]{2,1,0:T(2,128)(2,1)}, u32[]{:S(2)}) copy-start(bf16[1,2,2304]{2,1,0:T(2,128)(2,1)} %param.7) | copy-start | bytes 27652
  32.0 4.4 %collective-permute-start.3 = (bf16[8,2304]{1,0:T(8,128)(2,1)S(1)}, bf16[8,2304]{1,0:T(8,128)(2,1)S(1)}, u32[]{:S(2)}, u32[]{:S(2)}) collective-permute-start(bf16[8,2304]{1,0:T(8,128)(2,1)S(1)} %shard_map.81.a), channel_id=1, source_target_pairs={{0,8},{8,0},{16,24},{24,16},{1,9},{9,1},{17,25},{25,17},{2,10},{10... | collective-permute-start | bytes 110600 | tf_op jit(solution)/shard_map/ppermute | solution.py:147
  36.5 6.6 %collective-permute-start.4 = (f32[8,2304]{1,0:T(8,128)S(1)}, f32[8,2304]{1,0:T(8,128)S(1)}, u32[]{:S(2)}, u32[]{:S(2)}) collective-permute-start(f32[8,2304]{1,0:T(8,128)S(1)} %shard_map.82.a), channel_id=1, source_target_pairs={{0,24},{8,16},{16,8},{24,0},{1,25},{9,17},{17,9},{25,1},{2,26},{10... | collective-permute-start | bytes 221192 | tf_op jit(solution)/shard_map/ppermute | solution.py:147
  57.6 5.1 %collective-permute-start.6 = (f32[128,256]{1,0:T(8,128)S(1)}, f32[128,256]{1,0:T(8,128)S(1)}, u32[]{:S(2)}, u32[]{:S(2)}) collective-permute-start(f32[128,256]{1,0:T(8,128)S(1)} %shard_map.88), channel_id=1, source_target_pairs={{0,1},{1,0},{2,3},{3,2},{4,5},{5,4},{6,7},{7,6},{8,9},{9,8},{10,11... | collective-permute-start | bytes 393224 | tf_op jit(solution)/shard_map/ppermute | solution.py:147
  62.0 2.4 %collective-permute-start.5 = (f32[128,256]{1,0:T(8,128)S(1)}, f32[128,256]{1,0:T(8,128)S(1)}, u32[]{:S(2)}, u32[]{:S(2)}) collective-permute-start(f32[128,256]{1,0:T(8,128)S(1)} %shard_map.86), channel_id=1, source_target_pairs={{0,1},{1,0},{2,3},{3,2},{4,5},{5,4},{6,7},{7,6},{8,9},{9,8},{10,11... | collective-permute-start | bytes 393224 | tf_op jit(solution)/shard_map/ppermute | solution.py:147
  62.7 3.2 %collective-permute-start.7 = (bf16[128,256]{1,0:T(8,128)(2,1)S(1)}, bf16[128,256]{1,0:T(8,128)(2,1)S(1)}, u32[]{:S(2)}, u32[]{:S(2)}) collective-permute-start(bf16[128,256]{1,0:T(8,128)(2,1)S(1)} %shard_map.89), channel_id=1, source_target_pairs={{0,2},{1,3},{2,0},{3,1},{4,6},{5,7},{6,4},{7,5},{8,10},{9,11},{10,... | collective-permute-start | bytes 196616 | tf_op jit(solution)/shard_map/ppermute | solution.py:147

commit v6 on v5

--- a/solution.py
+++ b/solution.py
@@ -112,12 +112,11 @@
     out[...] = total.astype(out.dtype)
 
 
-def pair_kernel(a, b, out):
-    out[...] = a[...].astype(F32) + b[...].astype(F32)
-
-
-def spread_kernel(a, b, out):
-    err = (a[...] + b[...]).astype(BF)
+def spread_kernel(s0, s1, s2, s3, out):
+    total = (s0[...].astype(F32) + s1[...].astype(F32)) + (
+        s2[...].astype(F32) + s3[...].astype(F32)
+    )
+    err = total.astype(BF)
     for i in range(out.shape[0]):
         out[i] = err
 
@@ -214,10 +213,10 @@
     shares = shares.reshape(GROUP, rows, width)
     shares = lax.all_to_all(shares, NEAR, 0, 0, tiled=True)
     near = call(gather_sum_kernel, shape((rows, width), BF), [VMEM])(shares)
-    other = swap(near, "zh", 1)
-    pair = call(pair_kernel, shape((rows, width), F32), [VMEM] * 2)(near, other)
-    other = swap(pair, "zh", 3)
-    copies = call(spread_kernel, shape((GROUP, rows, width), BF), [VMEM] * 2)(pair, other)
+    parts = [near] * ZH
+    for flip in (2, 3, 1):
+        parts[flip] = swap(near, "zh", flip)
+    copies = call(spread_kernel, shape((GROUP, rows, width), BF), [VMEM] * 4)(*parts)
     err_full = lax.all_to_all(copies, NEAR, 0, 0, tiled=True).reshape(tok, width)
 
     def term(flip, kind):

time: 66.8 us -> 68.1 us (1.019)
  waiting for transfers between devices: 5.43 us -> 7.28 us
  starting transfers between devices: 19.2 us -> 18 us
  blocking collectives: 32.6 us -> 33.3 us
    ppermute x8 -> x9, waiting for transfers between devices: 5.43 us -> 7.28 us  [swap(): return lax.ppermute(value, name, [(i, i ^ flip) for i in range(size)])]
    ppermute x8 -> x9, starting transfers between devices: 19.2 us -> 18 us  [swap(): return lax.ppermute(value, name, [(i, i ^ flip) for i in range(size)])]
    all_to_all x1, blocking collectives: 13.9 us -> 14.6 us  [per_device(): lax.all_to_all(copies, NEAR, 0, 0, tiled=True).reshape(tok, width)]
  transfers between devices with their start and end apart: 8 -> 9, of which waited for: 4 -> 4; matrix products, arithmetic and copies ran while one was open for 0% -> 0% of each run, Pallas kernels for 7% -> 7%
where the time goes in v6:
time: 68.1 us; the launch traced here: 67.9 us
  blocking collectives  33.3 us (49%)
  starting transfers between devices  18 us (26%)
  Pallas kernels  7.74 us (11%)
  waiting for transfers between devices  7.28 us (11%)
  between operations  0.72 us (1%)
    all_to_all x1, blocking collectives, per_device(): shares = lax.all_to_all(shares, NEAR, 0, 0, tiled=True)  18.7 us
    ppermute x9, starting transfers between devices, swap(): return lax.ppermute(value, name, [(i, i ^ flip) for i in range(size)])  18 us
    all_to_all x1, blocking collectives, per_device(): lax.all_to_all(copies, NEAR, 0, 0, tiled=True).reshape(tok, width)  14.6 us
    ppermute x9, waiting for transfers between devices, swap(): return lax.ppermute(value, name, [(i, i ^ flip) for i in range(size)])  7.28 us
    pallas_call x4, Pallas kernels, term(): call(kernel, shape((tok, feats), kind), specs, flops)  2.14 us
    pallas_call x1, Pallas kernels, per_device(): dec, own, keep = load(in_hbm(pair_mask), latent, mine, slabs)  2.01 us
    pallas_call x1, Pallas kernels, per_device(): call(encode_kernel, [shape((tok, feats), BF), shape((feats, width), BF)],...  1.88 us
  transfers between devices with their start and end apart: 9, of which 4 were waited for; matrix products, arithmetic and copies ran while one was open for 0% of the time, Pallas kernels for 7%

profile of v6, /device:TPU:1, one launch (start us, length us, event | category | flops | bytes accessed | tf_op | source)
XLA Modules:
  0.0 67.9 jit_solution(8928990784668228216)
XLA Ops:
  0.6 1.9 %shard_map.77 = (bf16[128,256]{1,0:T(8,128)(2,1)S(1)}, bf16[256,2304]{1,0:T(8,128)(2,1)S(1)}) custom-call(bf16[128,2304]{1,0:T(8,128)(2,1)} %bitcast.19, bf16[2304,256]{1,0:T(8,128)(2,1)} %bitcast.18, f32[1,256]{1,0:T(1,128)} %bias.1, bf16[4,256,2304]{2,1,0:T(8,128)(2,1)} %bitcast.16), custom_call_target="tpu_custom_call" | custom-call | flops 150994944 | bytes 1179648 | tf_op jit(solution)/shard_map/pallas_call | solution.py:174
  2.5 2.2 %collective-permute-start.1 = (bf16[128,256]{1,0:T(8,128)(2,1)S(1)}, bf16[128,256]{1,0:T(8,128)(2,1)S(1)}, u32[]{:S(2)}, u32[]{:S(2)}) collective-permute-start(bf16[128,256]{1,0:T(8,128)(2,1)S(1)} %get-tuple-element.7.latent), channel_id=1, source_target_pairs={{0,2},{1,3},{2,0},{3,1},{4,6},{5,7},{6,4},{7,5},{8,10},{9,11},{10,... | collective-permute-start | bytes 196616 | tf_op jit(solution)/shard_map/ppermute | solution.py:146
  4.7 1.2 %collective-permute-start = (bf16[128,256]{1,0:T(8,128)(2,1)S(1)}, bf16[128,256]{1,0:T(8,128)(2,1)S(1)}, u32[]{:S(2)}, u32[]{:S(2)}) collective-permute-start(bf16[128,256]{1,0:T(8,128)(2,1)S(1)} %get-tuple-element.7.latent), channel_id=1, source_target_pairs={{0,1},{1,0},{2,3},{3,2},{4,5},{5,4},{6,7},{7,6},{8,9},{9,8},{10,11... | collective-permute-start | bytes 196616 | tf_op jit(solution)/shard_map/ppermute | solution.py:146
  5.9 0.5 collective-permute-done.1.l2
  6.4 3.7 %collective-permute-start.2 = (bf16[128,256]{1,0:T(8,128)(2,1)S(1)}, bf16[128,256]{1,0:T(8,128)(2,1)S(1)}, u32[]{:S(2)}, u32[]{:S(2)}) collective-permute-start(bf16[128,256]{1,0:T(8,128)(2,1)S(1)} %collective-permute-done.1.l2), channel_id=1, source_target_pairs={{0,1},{1,0},{2,3},{3,2},{4,5},{5,4},{6,7},{7,6},{8,9},{9,8},{10,11... | collective-permute-start | bytes 196616 | tf_op jit(solution)/shard_map/ppermute | solution.py:146
  10.1 2.0 %shard_map.78 = (bf16[3,256,2304]{2,1,0:T(8,128)(2,1)S(1)}, f32[128,2304]{1,0:T(8,128)S(1)}, f32[4,8,256]{2,1,0:T(8,128)S(1)}) custom-call(s32[4,4]{1,0:T(4,128)} %mask.1, bf16[128,256]{1,0:T(8,128)(2,1)S(1)} %get-tuple-element.7.latent, bf16[256,2304]{1,0:T(8,128)(2,1)S(1)} %get-tuple-element.8.mine.dec, bf16[4,256,2304]{2,1,0:T(8,128)(2,1)} %bitcast.17), custom_call_target="tpu_custom_call" | custom-call | flops 150994944 | bytes 4718592 | tf_op jit(solution)/shard_map/pallas_call | solution.py:204
  12.1 0.0 collective-permute-done.l1
  12.1 0.0 copy-start
  12.1 0.5 shard_map.79.most
  12.6 0.0 collective-permute-done.2.l3
  12.6 0.2 copy-done
  12.8 0.4 shard_map.80
  13.2 18.7 %all_to_all.10.shares = bf16[16,8,2304]{2,1,0:T(8,128)(2,1)S(1)} all-to-all(bf16[16,8,2304]{2,1,0:T(8,128)(2,1)S(1)} %bitcast.14), channel_id=1, replica_groups=mesh['x'=4,'yh'=2,'zh'=4,'zl'=2,'tgt'=4] {'x','yh','zl'}, dimensions={0} | all-to-all | bytes 1179648 | tf_op jit(solution)/shard_map/all_to_all | solution.py:214
  31.9 0.1 shard_map.81.s0
  32.0 3.1 %collective-permute-start.3 = (bf16[8,2304]{1,0:T(8,128)(2,1)S(1)}, bf16[8,2304]{1,0:T(8,128)(2,1)S(1)}, u32[]{:S(2)}, u32[]{:S(2)}) collective-permute-start(bf16[8,2304]{1,0:T(8,128)(2,1)S(1)} %shard_map.81.s0), channel_id=1, source_target_pairs={{0,8},{8,0},{16,24},{24,16},{1,9},{9,1},{17,25},{25,17},{2,10},{10... | collective-permute-start | bytes 110600 | tf_op jit(solution)/shard_map/ppermute | solution.py:146
  35.1 4.2 %collective-permute-start.4 = (bf16[8,2304]{1,0:T(8,128)(2,1)S(1)}, bf16[8,2304]{1,0:T(8,128)(2,1)S(1)}, u32[]{:S(2)}, u32[]{:S(2)}) collective-permute-start(bf16[8,2304]{1,0:T(8,128)(2,1)S(1)} %shard_map.81.s0), channel_id=1, source_target_pairs={{0,16},{8,24},{16,0},{24,8},{1,17},{9,25},{17,1},{25,9},{2,18},{10... | collective-permute-start | bytes 110600 | tf_op jit(solution)/shard_map/ppermute | solution.py:146
  39.3 0.0 collective-permute-start.5
  39.3 0.0 collective-permute-done.3.s1
  39.3 2.6 %collective-permute-done.4.s2 = bf16[8,2304]{1,0:T(8,128)(2,1)S(1)} collective-permute-done((bf16[8,2304]{1,0:T(8,128)(2,1)S(1)}, bf16[8,2304]{1,0:T(8,128)(2,1)S(1)}, u32[]{:S(2)}, u32[]{:S(2)}) %collective-permute-start.4) | collective-permute-done | bytes 36896 | tf_op jit(solution)/shard_map/ppermute | solution.py:146
  41.9 2.7 %collective-permute-done.5.s3 = bf16[8,2304]{1,0:T(8,128)(2,1)S(1)} collective-permute-done((bf16[8,2304]{1,0:T(8,128)(2,1)S(1)}, bf16[8,2304]{1,0:T(8,128)(2,1)S(1)}, u32[]{:S(2)}, u32[]{:S(2)}) %collective-permute-start.5) | collective-permute-done | bytes 36896 | tf_op jit(solution)/shard_map/ppermute | solution.py:146
  44.7 14.6 %all_to_all.11 = bf16[16,8,2304]{2,1,0:T(8,128)(2,1)S(1)} all-to-all(bf16[16,8,2304]{2,1,0:T(8,128)(2,1)S(1)} %shard_map.82), channel_id=1, replica_groups=mesh['x'=4,'yh'=2,'zh'=4,'zl'=2,'tgt'=4] {'x','yh','zl'}, dimensions={0} | all-to-all | bytes 1179648 | tf_op jit(solution)/shard_map/all_to_all | solution.py:220
  59.3 0.5 shard_map.87
  59.8 3.0 %collective-permute-start.7 = (f32[128,256]{1,0:T(8,128)S(1)}, f32[128,256]{1,0:T(8,128)S(1)}, u32[]{:S(2)}, u32[]{:S(2)}) collective-permute-start(f32[128,256]{1,0:T(8,128)S(1)} %shard_map.87), channel_id=1, source_target_pairs={{0,1},{1,0},{2,3},{3,2},{4,5},{5,4},{6,7},{7,6},{8,9},{9,8},{10,11... | collective-permute-start | bytes 393224 | tf_op jit(solution)/shard_map/ppermute | solution.py:146
  62.8 0.5 shard_map.85
  63.3 0.1 collective-permute-start.6
  63.4 0.5 shard_map.86.a
  64.0 0.0 collective-permute-done.7.b
  64.0 0.5 collective-permute-start.8
  64.5 0.7 shard_map.83
  65.2 0.5 shard_map.84
  65.7 0.0 collective-permute-done.6
  65.7 1.5 %collective-permute-done.8 = bf16[128,256]{1,0:T(8,128)(2,1)S(1)} collective-permute-done((bf16[128,256]{1,0:T(8,128)(2,1)S(1)}, bf16[128,256]{1,0:T(8,128)(2,1)S(1)}, u32[]{:S(2)}, u32[]{:S(2)}) %collective-permute-start.8) | collective-permute-done | bytes 65568 | tf_op jit(solution)/shard_map/ppermute | solution.py:146
  67.2 0.7 fusion
  (2 shorter events, 0.1 us)
Async XLA Ops:
  2.5 3.9 %collective-permute-start.1 = (bf16[128,256]{1,0:T(8,128)(2,1)S(1)}, bf16[128,256]{1,0:T(8,128)(2,1)S(1)}, u32[]{:S(2)}, u32[]{:S(2)}) collective-permute-start(bf16[128,256]{1,0:T(8,128)(2,1)S(1)} %get-tuple-element.7.latent), channel_id=1, source_target_pairs={{0,2},{1,3},{2,0},{3,1},{4,6},{5,7},{6,4},{7,5},{8,10},{9,11},{10,... | collective-permute-start | bytes 196616 | tf_op jit(solution)/shard_map/ppermute | solution.py:146
  4.7 7.4 %collective-permute-start = (bf16[128,256]{1,0:T(8,128)(2,1)S(1)}, bf16[128,256]{1,0:T(8,128)(2,1)S(1)}, u32[]{:S(2)}, u32[]{:S(2)}) collective-permute-start(bf16[128,256]{1,0:T(8,128)(2,1)S(1)} %get-tuple-element.7.latent), channel_id=1, source_target_pairs={{0,1},{1,0},{2,3},{3,2},{4,5},{5,4},{6,7},{7,6},{8,9},{9,8},{10,11... | collective-permute-start | bytes 196616 | tf_op jit(solution)/shard_map/ppermute | solution.py:146
  6.4 6.2 %collective-permute-start.2 = (bf16[128,256]{1,0:T(8,128)(2,1)S(1)}, bf16[128,256]{1,0:T(8,128)(2,1)S(1)}, u32[]{:S(2)}, u32[]{:S(2)}) collective-permute-start(bf16[128,256]{1,0:T(8,128)(2,1)S(1)} %collective-permute-done.1.l2), channel_id=1, source_target_pairs={{0,1},{1,0},{2,3},{3,2},{4,5},{5,4},{6,7},{7,6},{8,9},{9,8},{10,11... | collective-permute-start | bytes 196616 | tf_op jit(solution)/shard_map/ppermute | solution.py:146
  12.1 0.7 %copy-start = (bf16[1,2,2304]{2,1,0:T(2,128)(2,1)S(1)}, bf16[1,2,2304]{2,1,0:T(2,128)(2,1)}, u32[]{:S(2)}) copy-start(bf16[1,2,2304]{2,1,0:T(2,128)(2,1)} %param.7) | copy-start | bytes 27652
  32.0 7.3 %collective-permute-start.3 = (bf16[8,2304]{1,0:T(8,128)(2,1)S(1)}, bf16[8,2304]{1,0:T(8,128)(2,1)S(1)}, u32[]{:S(2)}, u32[]{:S(2)}) collective-permute-start(bf16[8,2304]{1,0:T(8,128)(2,1)S(1)} %shard_map.81.s0), channel_id=1, source_target_pairs={{0,8},{8,0},{16,24},{24,16},{1,9},{9,1},{17,25},{25,17},{2,10},{10... | collective-permute-start | bytes 110600 | tf_op jit(solution)/shard_map/ppermute | solution.py:146
  35.1 6.8 %collective-permute-start.4 = (bf16[8,2304]{1,0:T(8,128)(2,1)S(1)}, bf16[8,2304]{1,0:T(8,128)(2,1)S(1)}, u32[]{:S(2)}, u32[]{:S(2)}) collective-permute-start(bf16[8,2304]{1,0:T(8,128)(2,1)S(1)} %shard_map.81.s0), channel_id=1, source_target_pairs={{0,16},{8,24},{16,0},{24,8},{1,17},{9,25},{17,1},{25,9},{2,18},{10... | collective-permute-start | bytes 110600 | tf_op jit(solution)/shard_map/ppermute | solution.py:146
  39.3 5.3 %collective-permute-start.5 = (bf16[8,2304]{1,0:T(8,128)(2,1)S(1)}, bf16[8,2304]{1,0:T(8,128)(2,1)S(1)}, u32[]{:S(2)}, u32[]{:S(2)}) collective-permute-start(bf16[8,2304]{1,0:T(8,128)(2,1)S(1)} %shard_map.81.s0), channel_id=1, source_target_pairs={{0,24},{8,16},{16,8},{24,0},{1,25},{9,17},{17,9},{25,1},{2,26},{10... | collective-permute-start | bytes 110600 | tf_op jit(solution)/shard_map/ppermute | solution.py:146
  59.8 4.2 %collective-permute-start.7 = (f32[128,256]{1,0:T(8,128)S(1)}, f32[128,256]{1,0:T(8,128)S(1)}, u32[]{:S(2)}, u32[]{:S(2)}) collective-permute-start(f32[128,256]{1,0:T(8,128)S(1)} %shard_map.87), channel_id=1, source_target_pairs={{0,1},{1,0},{2,3},{3,2},{4,5},{5,4},{6,7},{7,6},{8,9},{9,8},{10,11... | collective-permute-start | bytes 393224 | tf_op jit(solution)/shard_map/ppermute | solution.py:146
  63.3 2.4 %collective-permute-start.6 = (f32[128,256]{1,0:T(8,128)S(1)}, f32[128,256]{1,0:T(8,128)S(1)}, u32[]{:S(2)}, u32[]{:S(2)}) collective-permute-start(f32[128,256]{1,0:T(8,128)S(1)} %shard_map.85), channel_id=1, source_target_pairs={{0,1},{1,0},{2,3},{3,2},{4,5},{5,4},{6,7},{7,6},{8,9},{9,8},{10,11... | collective-permute-start | bytes 393224 | tf_op jit(solution)/shard_map/ppermute | solution.py:146
  64.0 3.2 %collective-permute-start.8 = (bf16[128,256]{1,0:T(8,128)(2,1)S(1)}, bf16[128,256]{1,0:T(8,128)(2,1)S(1)}, u32[]{:S(2)}, u32[]{:S(2)}) collective-permute-start(bf16[128,256]{1,0:T(8,128)(2,1)S(1)} %shard_map.88), channel_id=1, source_target_pairs={{0,2},{1,3},{2,0},{3,1},{4,6},{5,7},{6,4},{7,5},{8,10},{9,11},{10,... | collective-permute-start | bytes 196616 | tf_op jit(solution)/shard_map/ppermute | solution.py:146

commit v7 on v6

--- a/solution.py
+++ b/solution.py
@@ -127,8 +127,14 @@
     out[...] = (keep[flip, 0:1, :] * term).astype(out.dtype)
 
 
-def join_kernel(a, b, out):
-    out[...] = (a[...] + b[...]).astype(out.dtype)
+def turn_kernel(dec, out):
+    for flip in (2, 3):
+        out[flip - 2] = dec[flip - 1].T
+
+
+def turned_kernel(flip, keep, err, turned, out):
+    term = jnp.dot(err[...], turned[flip - 2], **DOT)
+    out[...] = (keep[flip, 0:1, :] * term).astype(out.dtype)
 
 
 def pick_kernel(err, out):
@@ -216,26 +222,26 @@
     parts = [near] * ZH
     for flip in (2, 3, 1):
         parts[flip] = swap(near, "zh", flip)
+    turned = call(turn_kernel, shape((2, width, feats), BF), [VMEM])(dec)
     copies = call(spread_kernel, shape((GROUP, rows, width), BF), [VMEM] * 4)(*parts)
     err_full = lax.all_to_all(copies, NEAR, 0, 0, tiled=True).reshape(tok, width)
 
     def term(flip, kind):
-        kernel = functools.partial(grad_kernel, flip)
-        specs = [VMEM] * 3
-        return call(kernel, shape((tok, feats), kind), specs, flops)(
-            keep, err_full, dec if flip else mine
+        far = flip > 1
+        kernel = functools.partial(turned_kernel if far else grad_kernel, flip)
+        slab = turned if far else dec if flip else mine
+        return call(kernel, shape((tok, feats), kind), [VMEM] * 3, flops)(
+            keep, err_full, slab
         )
 
-    diag = term(3, F32)
-    diag = swap(diag, "tgt", 1)
-    far = term(2, F32)
-    far = call(join_kernel, shape((tok, feats), BF), [VMEM] * 2)(far, diag)
-    far = swap(far, "tgt", 2)
-    near = term(1, F32)
-    near = swap(near, "tgt", 1)
-    own = term(0, F32)
+    back = {}
+    for flip in (3, 2, 1):
+        part = term(flip, BF)
+        back[flip] = swap(part, "tgt", flip)
+    grad = term(0, F32)
     err_local = call(pick_kernel, shape((rows_local, width), BF), [VMEM])(err_full)
-    grad = own + near + far.astype(F32)
+    for flip in FLIPS:
+        grad = grad + back[flip].astype(F32)
     return (err_local[None], grad.astype(BF)[None])
 
 

time: 68.1 us -> 75.3 us (1.11)
  blocking collectives: 33.3 us -> 18.7 us
  starting transfers between devices: 18 us -> 24.6 us
  waiting for transfers between devices: 7.28 us -> 13.1 us
  Pallas kernels: 7.74 us -> 13.5 us
  local copies, waits for them, and re-layouts: 0.2 us -> 3.3 us
    all_to_all x1 -> x0, blocking collectives: 14.6 us -> none  [per_device(): lax.all_to_all(copies, NEAR, 0, 0, tiled=True).reshape(tok, width)]
    all_to_all x0 -> x1, waiting for transfers between devices: none -> 7.24 us  [per_device(): lax.all_to_all(copies, NEAR, 0, 0, tiled=True).reshape(tok, width)]
    pallas_call x5, Pallas kernels: 2.15 us -> 6.89 us  [the longest x4 6.24 us: term(): call(kernel, shape((tok, feats), kind), [VMEM] * 3, flops)]
    all_to_all x0 -> x1, starting transfers between devices: none -> 4.25 us  [per_device(): lax.all_to_all(copies, NEAR, 0, 0, tiled=True).reshape(tok, width)]
    unnamed x2 -> x18, local copies, waits for them, and re-layouts: 0.2 us -> 3.3 us
    ppermute x9, starting transfers between devices: 18 us -> 20.3 us  [swap(): return lax.ppermute(value, name, [(i, i ^ flip) for i in range(size)])]
    ppermute x9, waiting for transfers between devices: 7.28 us -> 5.89 us  [swap(): return lax.ppermute(value, name, [(i, i ^ flip) for i in range(size)])]
    pallas_call x1, Pallas kernels: 0.67 us -> 1.74 us  [per_device(): call(pick_kernel, shape((rows_local, width), BF), [VMEM])(err_full)]
  transfers between devices with their start and end apart: 9 -> 10, of which waited for: 4 -> 5; matrix products, arithmetic and copies ran while one was open for 0% -> 0% of each run, Pallas kernels for 7% -> 9%
where the time goes in v7:
time: 75.3 us; the launch traced here: 74.7 us
  starting transfers between devices  24.6 us (33%)
  blocking collectives  18.7 us (25%)
  Pallas kernels  13.5 us (18%)
  waiting for transfers between devices  13.1 us (17%)
  local copies, waits for them, and re-layouts  3.3 us (4%)
  between operations  0.8 us (1%)
    ppermute x9, starting transfers between devices, swap(): return lax.ppermute(value, name, [(i, i ^ flip) for i in range(size)])  20.3 us
    all_to_all x1, blocking collectives, per_device(): shares = lax.all_to_all(shares, NEAR, 0, 0, tiled=True)  18.7 us
    all_to_all x1, waiting for transfers between devices, per_device(): lax.all_to_all(copies, NEAR, 0, 0, tiled=True).reshape(tok, width)  7.24 us
    pallas_call x4, Pallas kernels, term(): call(kernel, shape((tok, feats), kind), [VMEM] * 3, flops)  6.24 us
    ppermute x9, waiting for transfers between devices, swap(): return lax.ppermute(value, name, [(i, i ^ flip) for i in range(size)])  5.89 us
    all_to_all x1, starting transfers between devices, per_device(): lax.all_to_all(copies, NEAR, 0, 0, tiled=True).reshape(tok, width)  4.25 us
    unnamed x18, local copies, waits for them, and re-layouts  3.3 us
    pallas_call x1, Pallas kernels, per_device(): dec, own, keep = load(in_hbm(pair_mask), latent, mine, slabs)  2.01 us
  transfers between devices with their start and end apart: 10, of which 5 were waited for; matrix products, arithmetic and copies ran while one was open for 0% of the time, Pallas kernels for 9%

profile of v7, /device:TPU:1, one launch (start us, length us, event | category | flops | bytes accessed | tf_op | source)
XLA Modules:
  0.0 74.7 jit_solution(9926791011527164883)
XLA Ops:
  0.6 1.9 %shard_map.77 = (bf16[128,256]{1,0:T(8,128)(2,1)S(1)}, bf16[256,2304]{1,0:T(8,128)(2,1)S(1)}) custom-call(bf16[128,2304]{1,0:T(8,128)(2,1)} %bitcast.14, bf16[2304,256]{1,0:T(8,128)(2,1)} %bitcast.13, f32[1,256]{1,0:T(1,128)} %bias.1, bf16[4,256,2304]{2,1,0:T(8,128)(2,1)} %bitcast.11), custom_call_target="tpu_custom_call" | custom-call | flops 150994944 | bytes 1179648 | tf_op jit(solution)/shard_map/pallas_call | solution.py:180
  2.5 0.0 copy-start.2
  2.5 2.2 %collective-permute-start.1 = (bf16[128,256]{1,0:T(8,128)(2,1)S(1)}, bf16[128,256]{1,0:T(8,128)(2,1)S(1)}, u32[]{:S(2)}, u32[]{:S(2)}) collective-permute-start(bf16[128,256]{1,0:T(8,128)(2,1)S(1)} %get-tuple-element.7.latent), channel_id=1, source_target_pairs={{0,2},{1,3},{2,0},{3,1},{4,6},{5,7},{6,4},{7,5},{8,10},{9,11},{10,... | collective-permute-start | bytes 196616 | tf_op jit(solution)/shard_map/ppermute | solution.py:152
  4.7 1.2 %collective-permute-start = (bf16[128,256]{1,0:T(8,128)(2,1)S(1)}, bf16[128,256]{1,0:T(8,128)(2,1)S(1)}, u32[]{:S(2)}, u32[]{:S(2)}) collective-permute-start(bf16[128,256]{1,0:T(8,128)(2,1)S(1)} %get-tuple-element.7.latent), channel_id=1, source_target_pairs={{0,1},{1,0},{2,3},{3,2},{4,5},{5,4},{6,7},{7,6},{8,9},{9,8},{10,11... | collective-permute-start | bytes 196616 | tf_op jit(solution)/shard_map/ppermute | solution.py:152
  5.9 0.5 collective-permute-done.1.l2
  6.4 3.7 %collective-permute-start.2 = (bf16[128,256]{1,0:T(8,128)(2,1)S(1)}, bf16[128,256]{1,0:T(8,128)(2,1)S(1)}, u32[]{:S(2)}, u32[]{:S(2)}) collective-permute-start(bf16[128,256]{1,0:T(8,128)(2,1)S(1)} %collective-permute-done.1.l2), channel_id=1, source_target_pairs={{0,1},{1,0},{2,3},{3,2},{4,5},{5,4},{6,7},{7,6},{8,9},{9,8},{10,11... | collective-permute-start | bytes 196616 | tf_op jit(solution)/shard_map/ppermute | solution.py:152
  10.1 2.0 %shard_map.78 = (bf16[3,256,2304]{2,1,0:T(8,128)(2,1)S(1)}, f32[128,2304]{1,0:T(8,128)S(1)}, f32[4,8,256]{2,1,0:T(8,128)S(1)}) custom-call(s32[4,4]{1,0:T(4,128)} %mask.1, bf16[128,256]{1,0:T(8,128)(2,1)S(1)} %get-tuple-element.7.latent, bf16[256,2304]{1,0:T(8,128)(2,1)S(1)} %get-tuple-element.8.mine.dec, bf16[4,256,2304]{2,1,0:T(8,128)(2,1)} %bitcast.12), custom_call_target="tpu_custom_call" | custom-call | flops 150994944 | bytes 4718592 | tf_op jit(solution)/shard_map/pallas_call | solution.py:210
  12.1 0.0 copy-done.2
  12.1 0.0 copy-start.5
  12.1 0.0 collective-permute-done.l1
  12.1 0.0 copy-start.8
  12.2 0.5 shard_map.79.most
  12.6 0.0 collective-permute-done.2.l3
  12.7 0.1 copy-done.5
  12.7 0.1 copy-done.8
  12.8 0.4 shard_map.80
  13.3 18.7 %all_to_all.10.shares = bf16[16,8,2304]{2,1,0:T(8,128)(2,1)S(1)} all-to-all(bf16[16,8,2304]{2,1,0:T(8,128)(2,1)S(1)} %bitcast.9), channel_id=1, replica_groups=mesh['x'=4,'yh'=2,'zh'=4,'zl'=2,'tgt'=4] {'x','yh','zl'}, dimensions={0} | all-to-all | bytes 1179648 | tf_op jit(solution)/shard_map/all_to_all | solution.py:220
  32.0 0.1 shard_map.81.s0
  32.1 3.1 %collective-permute-start.3 = (bf16[8,2304]{1,0:T(8,128)(2,1)S(1)}, bf16[8,2304]{1,0:T(8,128)(2,1)S(1)}, u32[]{:S(2)}, u32[]{:S(2)}) collective-permute-start(bf16[8,2304]{1,0:T(8,128)(2,1)S(1)} %shard_map.81.s0), channel_id=1, source_target_pairs={{0,8},{8,0},{16,24},{24,16},{1,9},{9,1},{17,25},{25,17},{2,10},{10... | collective-permute-start | bytes 110600 | tf_op jit(solution)/shard_map/ppermute | solution.py:152
  35.1 4.2 %collective-permute-start.4 = (bf16[8,2304]{1,0:T(8,128)(2,1)S(1)}, bf16[8,2304]{1,0:T(8,128)(2,1)S(1)}, u32[]{:S(2)}, u32[]{:S(2)}) collective-permute-start(bf16[8,2304]{1,0:T(8,128)(2,1)S(1)} %shard_map.81.s0), channel_id=1, source_target_pairs={{0,16},{8,24},{16,0},{24,8},{1,17},{9,25},{17,1},{25,9},{2,18},{10... | collective-permute-start | bytes 110600 | tf_op jit(solution)/shard_map/ppermute | solution.py:152
  39.3 0.0 collective-permute-start.5
  39.3 0.0 collective-permute-done.3.s1
  39.4 2.5 %collective-permute-done.4.s2 = bf16[8,2304]{1,0:T(8,128)(2,1)S(1)} collective-permute-done((bf16[8,2304]{1,0:T(8,128)(2,1)S(1)}, bf16[8,2304]{1,0:T(8,128)(2,1)S(1)}, u32[]{:S(2)}, u32[]{:S(2)}) %collective-permute-start.4) | collective-permute-done | bytes 36896 | tf_op jit(solution)/shard_map/ppermute | solution.py:152
  41.9 2.7 %collective-permute-done.5.s3 = bf16[8,2304]{1,0:T(8,128)(2,1)S(1)} collective-permute-done((bf16[8,2304]{1,0:T(8,128)(2,1)S(1)}, bf16[8,2304]{1,0:T(8,128)(2,1)S(1)}, u32[]{:S(2)}, u32[]{:S(2)}) %collective-permute-start.5) | collective-permute-done | bytes 36896 | tf_op jit(solution)/shard_map/ppermute | solution.py:152
  44.7 0.0 copy-start.4
  44.7 0.8 %copy-done.4 = bf16[16,8,2304]{2,1,0:T(8,128)(2,1)} copy-done((bf16[16,8,2304]{2,1,0:T(8,128)(2,1)}, bf16[16,8,2304]{2,1,0:T(8,128)(2,1)S(1)}, u32[]{:S(2)}) %copy-start.4) | copy-done | bytes 589848
  45.5 4.2 %all-to-all-start.1 = ((bf16[16,8,2304]{2,1,0:T(8,128)(2,1)}), bf16[16,8,2304]{2,1,0:T(8,128)(2,1)}, u32[]{:S(2)}, u32[]{:S(2)}) async-start(bf16[16,8,2304]{2,1,0:T(8,128)(2,1)} %copy-done.4), calls=%async_computation.1 | async-start | bytes 1179648 | tf_op jit(solution)/shard_map/all_to_all | solution.py:227
  49.8 0.7 shard_map.86.turned
  50.4 0.0 copy-start
  50.4 1.4 %copy-done = bf16[2,2304,256]{2,1,0:T(8,128)(2,1)} copy-done((bf16[2,2304,256]{2,1,0:T(8,128)(2,1)}, bf16[2,2304,256]{2,1,0:T(8,128)(2,1)S(1)}, u32[]{:S(2)}) %copy-start) | copy-done | bytes 2359320
  51.9 7.2 %all-to-all-done.1 = bf16[16,8,2304]{2,1,0:T(8,128)(2,1)} async-done(((bf16[16,8,2304]{2,1,0:T(8,128)(2,1)}), bf16[16,8,2304]{2,1,0:T(8,128)(2,1)}, u32[]{:S(2)}, u32[]{:S(2)}) %all-to-all-start.1) | async-done | bytes 589856 | tf_op jit(solution)/shard_map/all_to_all | solution.py:227
  59.1 0.8 %copy-done.6 = f32[4,8,256]{2,1,0:T(8,128)S(1)} copy-done((f32[4,8,256]{2,1,0:T(8,128)S(1)}, f32[4,8,256]{2,1,0:T(8,128)}, u32[]{:S(2)}) %copy-start.6) | copy-done | bytes 32792
  59.9 1.7 %shard_map.85 = bf16[128,256]{1,0:T(8,128)(2,1)S(1)} custom-call(f32[4,8,256]{2,1,0:T(8,128)S(1)} %copy-done.6, bf16[128,2304]{1,0:T(8,128)(2,1)} %bitcast.5.err, bf16[3,256,2304]{2,1,0:T(8,128)(2,1)S(1)} %get-tuple-element.11.dec), custom_call_target="tpu_custom_call" | custom-call | flops 150994944 | tf_op jit(solution)/shard_map/pallas_call | solution.py:233
  61.6 0.1 copy-done.1
  61.7 1.4 %shard_map.87 = bf16[128,256]{1,0:T(8,128)(2,1)S(1)} custom-call(f32[4,8,256]{2,1,0:T(8,128)S(1)} %copy-done.6, bf16[128,2304]{1,0:T(8,128)(2,1)} %bitcast.5.err, bf16[2,2304,256]{2,1,0:T(8,128)(2,1)S(1)} %copy-done.1), custom_call_target="tpu_custom_call" | custom-call | flops 150994944 | tf_op jit(solution)/shard_map/pallas_call | solution.py:233
  63.1 0.0 copy-done.7
  63.1 0.0 copy-start.3
  63.1 1.5 %shard_map.88 = bf16[128,256]{1,0:T(8,128)(2,1)S(1)} custom-call(f32[4,8,256]{2,1,0:T(8,128)S(1)} %copy-done.7, bf16[128,2304]{1,0:T(8,128)(2,1)} %bitcast.5.err, bf16[2,2304,256]{2,1,0:T(8,128)(2,1)S(1)} %copy-done.1), custom_call_target="tpu_custom_call" | custom-call | flops 150994944 | tf_op jit(solution)/shard_map/pallas_call | solution.py:233
  64.6 4.2 %collective-permute-start.6 = (bf16[128,256]{1,0:T(8,128)(2,1)S(1)}, bf16[128,256]{1,0:T(8,128)(2,1)S(1)}, u32[]{:S(2)}, u32[]{:S(2)}) collective-permute-start(bf16[128,256]{1,0:T(8,128)(2,1)S(1)} %shard_map.85), channel_id=1, source_target_pairs={{0,1},{1,0},{2,3},{3,2},{4,5},{5,4},{6,7},{7,6},{8,9},{9,8},{10,11... | collective-permute-start | bytes 196616 | tf_op jit(solution)/shard_map/ppermute | solution.py:152
  68.8 0.4 collective-permute-start.7
  69.2 1.3 %collective-permute-start.8 = (bf16[128,256]{1,0:T(8,128)(2,1)S(1)}, bf16[128,256]{1,0:T(8,128)(2,1)S(1)}, u32[]{:S(2)}, u32[]{:S(2)}) collective-permute-start(bf16[128,256]{1,0:T(8,128)(2,1)S(1)} %shard_map.88), channel_id=1, source_target_pairs={{0,3},{1,2},{2,1},{3,0},{4,7},{5,6},{6,5},{7,4},{8,11},{9,10},{10,... | collective-permute-start | bytes 196616 | tf_op jit(solution)/shard_map/ppermute | solution.py:152
  70.6 1.7 %shard_map.83 = bf16[2,2304]{1,0:T(2,128)(2,1)} custom-call(bf16[128,2304]{1,0:T(8,128)(2,1)} %bitcast.5.err), custom_call_target="tpu_custom_call" | custom-call | tf_op jit(solution)/shard_map/pallas_call | solution.py:242
  72.3 0.0 copy-done.3
  72.3 1.6 %shard_map.84 = f32[128,256]{1,0:T(8,128)S(1)} custom-call(f32[4,8,256]{2,1,0:T(8,128)S(1)} %copy-done.7, bf16[128,2304]{1,0:T(8,128)(2,1)} %bitcast.5.err, bf16[256,2304]{1,0:T(8,128)(2,1)S(1)} %copy-done.3), custom_call_target="tpu_custom_call" | custom-call | flops 150994944 | tf_op jit(solution)/shard_map/pallas_call | solution.py:233
  73.9 0.0 collective-permute-done.6
  73.9 0.0 collective-permute-done.7
  73.9 0.1 collective-permute-done.8
  74.0 0.7 fusion
  (4 shorter events, 0.0 us)
Async XLA Ops:
  2.5 9.6 %copy-start.2 = (bf16[256,2304]{1,0:T(8,128)(2,1)}, bf16[256,2304]{1,0:T(8,128)(2,1)S(1)}, u32[]{:S(2)}) copy-start(bf16[256,2304]{1,0:T(8,128)(2,1)S(1)} %get-tuple-element.8.mine.dec) | copy-start | bytes 3538948
  2.5 3.9 %collective-permute-start.1 = (bf16[128,256]{1,0:T(8,128)(2,1)S(1)}, bf16[128,256]{1,0:T(8,128)(2,1)S(1)}, u32[]{:S(2)}, u32[]{:S(2)}) collective-permute-start(bf16[128,256]{1,0:T(8,128)(2,1)S(1)} %get-tuple-element.7.latent), channel_id=1, source_target_pairs={{0,2},{1,3},{2,0},{3,1},{4,6},{5,7},{6,4},{7,5},{8,10},{9,11},{10,... | collective-permute-start | bytes 196616 | tf_op jit(solution)/shard_map/ppermute | solution.py:152
  4.7 7.4 %collective-permute-start = (bf16[128,256]{1,0:T(8,128)(2,1)S(1)}, bf16[128,256]{1,0:T(8,128)(2,1)S(1)}, u32[]{:S(2)}, u32[]{:S(2)}) collective-permute-start(bf16[128,256]{1,0:T(8,128)(2,1)S(1)} %get-tuple-element.7.latent), channel_id=1, source_target_pairs={{0,1},{1,0},{2,3},{3,2},{4,5},{5,4},{6,7},{7,6},{8,9},{9,8},{10,11... | collective-permute-start | bytes 196616 | tf_op jit(solution)/shard_map/ppermute | solution.py:152
  6.4 6.3 %collective-permute-start.2 = (bf16[128,256]{1,0:T(8,128)(2,1)S(1)}, bf16[128,256]{1,0:T(8,128)(2,1)S(1)}, u32[]{:S(2)}, u32[]{:S(2)}) collective-permute-start(bf16[128,256]{1,0:T(8,128)(2,1)S(1)} %collective-permute-done.1.l2), channel_id=1, source_target_pairs={{0,1},{1,0},{2,3},{3,2},{4,5},{5,4},{6,7},{7,6},{8,9},{9,8},{10,11... | collective-permute-start | bytes 196616 | tf_op jit(solution)/shard_map/ppermute | solution.py:152
  12.1 0.6 copy-start.5
  12.1 0.7 copy-start.8
  32.1 7.3 %collective-permute-start.3 = (bf16[8,2304]{1,0:T(8,128)(2,1)S(1)}, bf16[8,2304]{1,0:T(8,128)(2,1)S(1)}, u32[]{:S(2)}, u32[]{:S(2)}) collective-permute-start(bf16[8,2304]{1,0:T(8,128)(2,1)S(1)} %shard_map.81.s0), channel_id=1, source_target_pairs={{0,8},{8,0},{16,24},{24,16},{1,9},{9,1},{17,25},{25,17},{2,10},{10... | collective-permute-start | bytes 110600 | tf_op jit(solution)/shard_map/ppermute | solution.py:152
  35.1 6.8 %collective-permute-start.4 = (bf16[8,2304]{1,0:T(8,128)(2,1)S(1)}, bf16[8,2304]{1,0:T(8,128)(2,1)S(1)}, u32[]{:S(2)}, u32[]{:S(2)}) collective-permute-start(bf16[8,2304]{1,0:T(8,128)(2,1)S(1)} %shard_map.81.s0), channel_id=1, source_target_pairs={{0,16},{8,24},{16,0},{24,8},{1,17},{9,25},{17,1},{25,9},{2,18},{10... | collective-permute-start | bytes 110600 | tf_op jit(solution)/shard_map/ppermute | solution.py:152
  39.3 5.3 %collective-permute-start.5 = (bf16[8,2304]{1,0:T(8,128)(2,1)S(1)}, bf16[8,2304]{1,0:T(8,128)(2,1)S(1)}, u32[]{:S(2)}, u32[]{:S(2)}) collective-permute-start(bf16[8,2304]{1,0:T(8,128)(2,1)S(1)} %shard_map.81.s0), channel_id=1, source_target_pairs={{0,24},{8,16},{16,8},{24,0},{1,25},{9,17},{17,9},{25,1},{2,26},{10... | collective-permute-start | bytes 110600 | tf_op jit(solution)/shard_map/ppermute | solution.py:152
  44.7 0.8 %copy-start.4 = (bf16[16,8,2304]{2,1,0:T(8,128)(2,1)}, bf16[16,8,2304]{2,1,0:T(8,128)(2,1)S(1)}, u32[]{:S(2)}) copy-start(bf16[16,8,2304]{2,1,0:T(8,128)(2,1)S(1)} %shard_map.82) | copy-start | bytes 1769476
  45.5 13.6 %all-to-all-start.1 = ((bf16[16,8,2304]{2,1,0:T(8,128)(2,1)}), bf16[16,8,2304]{2,1,0:T(8,128)(2,1)}, u32[]{:S(2)}, u32[]{:S(2)}) async-start(bf16[16,8,2304]{2,1,0:T(8,128)(2,1)} %copy-done.4), calls=%async_computation.1 | async-start | bytes 1179648 | tf_op jit(solution)/shard_map/all_to_all | solution.py:227
  50.4 1.4 %copy-start = (bf16[2,2304,256]{2,1,0:T(8,128)(2,1)}, bf16[2,2304,256]{2,1,0:T(8,128)(2,1)S(1)}, u32[]{:S(2)}) copy-start(bf16[2,2304,256]{2,1,0:T(8,128)(2,1)S(1)} %shard_map.86.turned) | copy-start | bytes 7077892
  59.1 0.8 %copy-start.6 = (f32[4,8,256]{2,1,0:T(8,128)S(1)}, f32[4,8,256]{2,1,0:T(8,128)}, u32[]{:S(2)}) copy-start(f32[4,8,256]{2,1,0:T(8,128)} %copy-done.5) | copy-start | bytes 98308
  59.9 1.8 %copy-start.1 = (bf16[2,2304,256]{2,1,0:T(8,128)(2,1)S(1)}, bf16[2,2304,256]{2,1,0:T(8,128)(2,1)}, u32[]{:S(2)}) copy-start(bf16[2,2304,256]{2,1,0:T(8,128)(2,1)} %copy-done) | copy-start | bytes 7077892
  61.7 1.4 %copy-start.7 = (f32[4,8,256]{2,1,0:T(8,128)S(1)}, f32[4,8,256]{2,1,0:T(8,128)}, u32[]{:S(2)}) copy-start(f32[4,8,256]{2,1,0:T(8,128)} %copy-done.5) | copy-start | bytes 98308
  63.1 9.2 %copy-start.3 = (bf16[256,2304]{1,0:T(8,128)(2,1)S(1)}, bf16[256,2304]{1,0:T(8,128)(2,1)}, u32[]{:S(2)}) copy-start(bf16[256,2304]{1,0:T(8,128)(2,1)} %copy-done.2) | copy-start | bytes 3538948
  64.6 9.3 %collective-permute-start.6 = (bf16[128,256]{1,0:T(8,128)(2,1)S(1)}, bf16[128,256]{1,0:T(8,128)(2,1)S(1)}, u32[]{:S(2)}, u32[]{:S(2)}) collective-permute-start(bf16[128,256]{1,0:T(8,128)(2,1)S(1)} %shard_map.85), channel_id=1, source_target_pairs={{0,1},{1,0},{2,3},{3,2},{4,5},{5,4},{6,7},{7,6},{8,9},{9,8},{10,11... | collective-permute-start | bytes 196616 | tf_op jit(solution)/shard_map/ppermute | solution.py:152
  68.8 5.1 %collective-permute-start.7 = (bf16[128,256]{1,0:T(8,128)(2,1)S(1)}, bf16[128,256]{1,0:T(8,128)(2,1)S(1)}, u32[]{:S(2)}, u32[]{:S(2)}) collective-permute-start(bf16[128,256]{1,0:T(8,128)(2,1)S(1)} %shard_map.87), channel_id=1, source_target_pairs={{0,2},{1,3},{2,0},{3,1},{4,6},{5,7},{6,4},{7,5},{8,10},{9,11},{10,... | collective-permute-start | bytes 196616 | tf_op jit(solution)/shard_map/ppermute | solution.py:152
  69.2 4.8 %collective-permute-start.8 = (bf16[128,256]{1,0:T(8,128)(2,1)S(1)}, bf16[128,256]{1,0:T(8,128)(2,1)S(1)}, u32[]{:S(2)}, u32[]{:S(2)}) collective-permute-start(bf16[128,256]{1,0:T(8,128)(2,1)S(1)} %shard_map.88), channel_id=1, source_target_pairs={{0,3},{1,2},{2,1},{3,0},{4,7},{5,6},{6,5},{7,4},{8,11},{9,10},{10,... | collective-permute-start | bytes 196616 | tf_op jit(solution)/shard_map/ppermute | solution.py:152

commit v8 on v7

--- a/solution.py
+++ b/solution.py
@@ -9,9 +9,9 @@
 
 
 X, YH, ZH, ZL, TG = 4, 2, 4, 2, 4
-NEAR = ("x", "yh", "zl")
+NEAR = ("x", "zl")
 FEAT = ("x", "yh", "zh", "zl")
-GROUP = X * YH * ZL
+GROUP = X * ZL
 DOT = dict(preferred_element_type=jnp.float32)
 BF, F32 = jnp.bfloat16, jnp.float32
 VMEM = pl.BlockSpec(memory_space=pltpu.VMEM)
@@ -110,6 +110,10 @@
     for i in range(1, shares.shape[0]):
         total = total + shares[i].astype(F32)
     out[...] = total.astype(out.dtype)
+
+
+def pair_kernel(a, b, out):
+    out[...] = (a[...].astype(F32) + b[...].astype(F32)).astype(out.dtype)
 
 
 def spread_kernel(s0, s1, s2, s3, out):
@@ -219,6 +223,8 @@
     shares = shares.reshape(GROUP, rows, width)
     shares = lax.all_to_all(shares, NEAR, 0, 0, tiled=True)
     near = call(gather_sum_kernel, shape((rows, width), BF), [VMEM])(shares)
+    other = swap(near, "yh", 1)
+    near = call(pair_kernel, shape((rows, width), BF), [VMEM] * 2)(near, other)
     parts = [near] * ZH
     for flip in (2, 3, 1):
         parts[flip] = swap(near, "zh", flip)

time: 75.3 us -> 75.3 us (level)
  blocking collectives: 18.7 us -> 13.8 us
  starting transfers between devices: 24.6 us -> 28.2 us
  waiting for transfers between devices: 13.1 us -> 14.4 us
    all_to_all x1, blocking collectives: 18.7 us -> 13.8 us  [per_device(): shares = lax.all_to_all(shares, NEAR, 0, 0, tiled=True)]
    ppermute x9 -> x10, starting transfers between devices: 20.3 us -> 23.6 us  [swap(): return lax.ppermute(value, name, [(i, i ^ flip) for i in range(size)])]
    ppermute x9 -> x10, waiting for transfers between devices: 5.89 us -> 8.52 us  [swap(): return lax.ppermute(value, name, [(i, i ^ flip) for i in range(size)])]
    all_to_all x1, waiting for transfers between devices: 7.24 us -> 5.93 us  [per_device(): lax.all_to_all(copies, NEAR, 0, 0, tiled=True).reshape(tok, width)]
    unnamed x18 -> x16, local copies, waits for them, and re-layouts: 3.3 us -> 3.29 us
  transfers between devices with their start and end apart: 10 -> 11, of which waited for: 5 -> 6; matrix products, arithmetic and copies ran while one was open for 0% -> 0% of each run, Pallas kernels for 9% -> 9%
where the time goes in v8:
time: 75.3 us; the launch traced here: 74.8 us
  starting transfers between devices  28.2 us (37%)
  waiting for transfers between devices  14.4 us (19%)
  blocking collectives  13.8 us (18%)
  Pallas kernels  13.5 us (18%)
  local copies, waits for them, and re-layouts  3.29 us (4%)
  between operations  0.8 us (1%)
    ppermute x10, starting transfers between devices, swap(): return lax.ppermute(value, name, [(i, i ^ flip) for i in range(size)])  23.6 us
    all_to_all x1, blocking collectives, per_device(): shares = lax.all_to_all(shares, NEAR, 0, 0, tiled=True)  13.8 us
    ppermute x10, waiting for transfers between devices, swap(): return lax.ppermute(value, name, [(i, i ^ flip) for i in range(size)])  8.52 us
    pallas_call x4, Pallas kernels, term(): call(kernel, shape((tok, feats), kind), [VMEM] * 3, flops)  6.22 us
    all_to_all x1, waiting for transfers between devices, per_device(): lax.all_to_all(copies, NEAR, 0, 0, tiled=True).reshape(tok, width)  5.93 us
    all_to_all x1, starting transfers between devices, per_device(): lax.all_to_all(copies, NEAR, 0, 0, tiled=True).reshape(tok, width)  4.66 us
    unnamed x16, local copies, waits for them, and re-layouts  3.29 us
    pallas_call x1, Pallas kernels, per_device(): dec, own, keep = load(in_hbm(pair_mask), latent, mine, slabs)  2.01 us
  transfers between devices with their start and end apart: 11, of which 6 were waited for; matrix products, arithmetic and copies ran while one was open for 0% of the time, Pallas kernels for 9%

profile of v8, /device:TPU:1, one launch (start us, length us, event | category | flops | bytes accessed | tf_op | source)
XLA Modules:
  0.0 74.8 jit_solution(2533224353759719504)
XLA Ops:
  0.6 1.9 %shard_map.77 = (bf16[128,256]{1,0:T(8,128)(2,1)S(1)}, bf16[256,2304]{1,0:T(8,128)(2,1)S(1)}) custom-call(bf16[128,2304]{1,0:T(8,128)(2,1)} %bitcast.14, bf16[2304,256]{1,0:T(8,128)(2,1)} %bitcast.13, f32[1,256]{1,0:T(1,128)} %bias.1, bf16[4,256,2304]{2,1,0:T(8,128)(2,1)} %bitcast.11), custom_call_target="tpu_custom_call" | custom-call | flops 150994944 | bytes 1179648 | tf_op jit(solution)/shard_map/pallas_call | solution.py:184
  2.5 0.0 copy-start.2
  2.5 2.2 %collective-permute-start.1 = (bf16[128,256]{1,0:T(8,128)(2,1)S(1)}, bf16[128,256]{1,0:T(8,128)(2,1)S(1)}, u32[]{:S(2)}, u32[]{:S(2)}) collective-permute-start(bf16[128,256]{1,0:T(8,128)(2,1)S(1)} %get-tuple-element.7.latent), channel_id=1, source_target_pairs={{0,2},{1,3},{2,0},{3,1},{4,6},{5,7},{6,4},{7,5},{8,10},{9,11},{10,... | collective-permute-start | bytes 196616 | tf_op jit(solution)/shard_map/ppermute | solution.py:156
  4.7 1.2 %collective-permute-start = (bf16[128,256]{1,0:T(8,128)(2,1)S(1)}, bf16[128,256]{1,0:T(8,128)(2,1)S(1)}, u32[]{:S(2)}, u32[]{:S(2)}) collective-permute-start(bf16[128,256]{1,0:T(8,128)(2,1)S(1)} %get-tuple-element.7.latent), channel_id=1, source_target_pairs={{0,1},{1,0},{2,3},{3,2},{4,5},{5,4},{6,7},{7,6},{8,9},{9,8},{10,11... | collective-permute-start | bytes 196616 | tf_op jit(solution)/shard_map/ppermute | solution.py:156
  5.9 0.5 collective-permute-done.1.l2
  6.4 3.7 %collective-permute-start.2 = (bf16[128,256]{1,0:T(8,128)(2,1)S(1)}, bf16[128,256]{1,0:T(8,128)(2,1)S(1)}, u32[]{:S(2)}, u32[]{:S(2)}) collective-permute-start(bf16[128,256]{1,0:T(8,128)(2,1)S(1)} %collective-permute-done.1.l2), channel_id=1, source_target_pairs={{0,1},{1,0},{2,3},{3,2},{4,5},{5,4},{6,7},{7,6},{8,9},{9,8},{10,11... | collective-permute-start | bytes 196616 | tf_op jit(solution)/shard_map/ppermute | solution.py:156
  10.1 2.0 %shard_map.78 = (bf16[3,256,2304]{2,1,0:T(8,128)(2,1)S(1)}, f32[128,2304]{1,0:T(8,128)S(1)}, f32[4,8,256]{2,1,0:T(8,128)S(1)}) custom-call(s32[4,4]{1,0:T(4,128)} %mask.1, bf16[128,256]{1,0:T(8,128)(2,1)S(1)} %get-tuple-element.7.latent, bf16[256,2304]{1,0:T(8,128)(2,1)S(1)} %get-tuple-element.8.mine.dec, bf16[4,256,2304]{2,1,0:T(8,128)(2,1)} %bitcast.12), custom_call_target="tpu_custom_call" | custom-call | flops 150994944 | bytes 4718592 | tf_op jit(solution)/shard_map/pallas_call | solution.py:214
  12.1 0.0 copy-done.2
  12.1 0.0 copy-start.5
  12.1 0.0 collective-permute-done.l1
  12.1 0.0 copy-start.7
  12.2 0.5 shard_map.79.most
  12.6 0.0 collective-permute-done.2.l3
  12.7 0.1 copy-done.5
  12.7 0.1 copy-done.7
  12.8 0.4 shard_map.80
  13.3 13.8 %all_to_all.10.shares = bf16[8,16,2304]{2,1,0:T(8,128)(2,1)S(1)} all-to-all(bf16[8,16,2304]{2,1,0:T(8,128)(2,1)S(1)} %bitcast.9), channel_id=1, replica_groups=mesh['x'=4,'yh'=2,'zh'=4,'zl'=2,'tgt'=4] {'x','zl'}, dimensions={0} | all-to-all | bytes 1179648 | tf_op jit(solution)/shard_map/all_to_all | solution.py:224
  27.0 0.1 shard_map.81.a
  27.1 3.0 %collective-permute-start.3 = (bf16[16,2304]{1,0:T(8,128)(2,1)S(1)}, bf16[16,2304]{1,0:T(8,128)(2,1)S(1)}, u32[]{:S(2)}, u32[]{:S(2)}) collective-permute-start(bf16[16,2304]{1,0:T(8,128)(2,1)S(1)} %shard_map.81.a), channel_id=1, source_target_pairs={{0,32},{32,0},{1,33},{33,1},{2,34},{34,2},{3,35},{35,3},{4,36},{36... | collective-permute-start | bytes 221192 | tf_op jit(solution)/shard_map/ppermute | solution.py:156
  30.1 1.8 %collective-permute-done.3.b = bf16[16,2304]{1,0:T(8,128)(2,1)S(1)} collective-permute-done((bf16[16,2304]{1,0:T(8,128)(2,1)S(1)}, bf16[16,2304]{1,0:T(8,128)(2,1)S(1)}, u32[]{:S(2)}, u32[]{:S(2)}) %collective-permute-start.3) | collective-permute-done | bytes 73760 | tf_op jit(solution)/shard_map/ppermute | solution.py:156
  31.9 3.1 %collective-permute-start.4 = (bf16[16,2304]{1,0:T(8,128)(2,1)S(1)}, bf16[16,2304]{1,0:T(8,128)(2,1)S(1)}, u32[]{:S(2)}, u32[]{:S(2)}) collective-permute-start(bf16[16,2304]{1,0:T(8,128)(2,1)S(1)} %shard_map.82.s0), channel_id=1, source_target_pairs={{0,8},{8,0},{16,24},{24,16},{1,9},{9,1},{17,25},{25,17},{2,10},{10... | collective-permute-start | bytes 221192 | tf_op jit(solution)/shard_map/ppermute | solution.py:156
  35.0 4.2 %collective-permute-start.5 = (bf16[16,2304]{1,0:T(8,128)(2,1)S(1)}, bf16[16,2304]{1,0:T(8,128)(2,1)S(1)}, u32[]{:S(2)}, u32[]{:S(2)}) collective-permute-start(bf16[16,2304]{1,0:T(8,128)(2,1)S(1)} %shard_map.82.s0), channel_id=1, source_target_pairs={{0,16},{8,24},{16,0},{24,8},{1,17},{9,25},{17,1},{25,9},{2,18},{10... | collective-permute-start | bytes 221192 | tf_op jit(solution)/shard_map/ppermute | solution.py:156
  39.2 0.0 collective-permute-start.6
  39.2 0.0 collective-permute-done.4.s1
  39.2 2.9 %collective-permute-done.5.s2 = bf16[16,2304]{1,0:T(8,128)(2,1)S(1)} collective-permute-done((bf16[16,2304]{1,0:T(8,128)(2,1)S(1)}, bf16[16,2304]{1,0:T(8,128)(2,1)S(1)}, u32[]{:S(2)}, u32[]{:S(2)}) %collective-permute-start.5) | collective-permute-done | bytes 73760 | tf_op jit(solution)/shard_map/ppermute | solution.py:156
  42.1 3.1 %collective-permute-done.6.s3 = bf16[16,2304]{1,0:T(8,128)(2,1)S(1)} collective-permute-done((bf16[16,2304]{1,0:T(8,128)(2,1)S(1)}, bf16[16,2304]{1,0:T(8,128)(2,1)S(1)}, u32[]{:S(2)}, u32[]{:S(2)}) %collective-permute-start.6) | collective-permute-done | bytes 73760 | tf_op jit(solution)/shard_map/ppermute | solution.py:156
  45.2 0.0 copy-start.4
  45.2 0.8 %copy-done.4 = bf16[8,16,2304]{2,1,0:T(8,128)(2,1)} copy-done((bf16[8,16,2304]{2,1,0:T(8,128)(2,1)}, bf16[8,16,2304]{2,1,0:T(8,128)(2,1)S(1)}, u32[]{:S(2)}) %copy-start.4) | copy-done | bytes 589848
  46.0 4.7 %all-to-all-start.1 = ((bf16[8,16,2304]{2,1,0:T(8,128)(2,1)}), bf16[8,16,2304]{2,1,0:T(8,128)(2,1)}, u32[]{:S(2)}, u32[]{:S(2)}) async-start(bf16[8,16,2304]{2,1,0:T(8,128)(2,1)} %copy-done.4), calls=%async_computation.1 | async-start | bytes 1179648 | tf_op jit(solution)/shard_map/all_to_all | solution.py:233
  50.7 0.7 shard_map.87.turned
  51.4 0.0 copy-start
  51.4 1.4 %copy-done = bf16[2,2304,256]{2,1,0:T(8,128)(2,1)} copy-done((bf16[2,2304,256]{2,1,0:T(8,128)(2,1)}, bf16[2,2304,256]{2,1,0:T(8,128)(2,1)S(1)}, u32[]{:S(2)}) %copy-start) | copy-done | bytes 2359320
  52.8 5.9 %all-to-all-done.1 = bf16[8,16,2304]{2,1,0:T(8,128)(2,1)} async-done(((bf16[8,16,2304]{2,1,0:T(8,128)(2,1)}), bf16[8,16,2304]{2,1,0:T(8,128)(2,1)}, u32[]{:S(2)}, u32[]{:S(2)}) %all-to-all-start.1) | async-done | bytes 589856 | tf_op jit(solution)/shard_map/all_to_all | solution.py:233
  58.7 0.8 %copy-done.6 = f32[4,8,256]{2,1,0:T(8,128)S(1)} copy-done((f32[4,8,256]{2,1,0:T(8,128)S(1)}, f32[4,8,256]{2,1,0:T(8,128)}, u32[]{:S(2)}) %copy-start.6) | copy-done | bytes 32792
  59.5 1.8 %shard_map.86 = bf16[128,256]{1,0:T(8,128)(2,1)S(1)} custom-call(f32[4,8,256]{2,1,0:T(8,128)S(1)} %copy-done.6, bf16[128,2304]{1,0:T(8,128)(2,1)} %bitcast.5.err, bf16[3,256,2304]{2,1,0:T(8,128)(2,1)S(1)} %get-tuple-element.11.dec), custom_call_target="tpu_custom_call" | custom-call | flops 150994944 | tf_op jit(solution)/shard_map/pallas_call | solution.py:239
  61.2 0.1 copy-done.1
  61.3 1.4 %shard_map.88 = bf16[128,256]{1,0:T(8,128)(2,1)S(1)} custom-call(f32[4,8,256]{2,1,0:T(8,128)S(1)} %copy-done.6, bf16[128,2304]{1,0:T(8,128)(2,1)} %bitcast.5.err, bf16[2,2304,256]{2,1,0:T(8,128)(2,1)S(1)} %copy-done.1), custom_call_target="tpu_custom_call" | custom-call | flops 150994944 | tf_op jit(solution)/shard_map/pallas_call | solution.py:239
  62.7 1.5 %shard_map.89 = bf16[128,256]{1,0:T(8,128)(2,1)S(1)} custom-call(f32[4,8,256]{2,1,0:T(8,128)S(1)} %copy-done.6, bf16[128,2304]{1,0:T(8,128)(2,1)} %bitcast.5.err, bf16[2,2304,256]{2,1,0:T(8,128)(2,1)S(1)} %copy-done.1), custom_call_target="tpu_custom_call" | custom-call | flops 150994944 | tf_op jit(solution)/shard_map/pallas_call | solution.py:239
  64.2 4.5 %collective-permute-start.7 = (bf16[128,256]{1,0:T(8,128)(2,1)S(1)}, bf16[128,256]{1,0:T(8,128)(2,1)S(1)}, u32[]{:S(2)}, u32[]{:S(2)}) collective-permute-start(bf16[128,256]{1,0:T(8,128)(2,1)S(1)} %shard_map.86), channel_id=1, source_target_pairs={{0,1},{1,0},{2,3},{3,2},{4,5},{5,4},{6,7},{7,6},{8,9},{9,8},{10,11... | collective-permute-start | bytes 196616 | tf_op jit(solution)/shard_map/ppermute | solution.py:156
  68.7 1.3 %collective-permute-start.8 = (bf16[128,256]{1,0:T(8,128)(2,1)S(1)}, bf16[128,256]{1,0:T(8,128)(2,1)S(1)}, u32[]{:S(2)}, u32[]{:S(2)}) collective-permute-start(bf16[128,256]{1,0:T(8,128)(2,1)S(1)} %shard_map.88), channel_id=1, source_target_pairs={{0,2},{1,3},{2,0},{3,1},{4,6},{5,7},{6,4},{7,5},{8,10},{9,11},{10,... | collective-permute-start | bytes 196616 | tf_op jit(solution)/shard_map/ppermute | solution.py:156
  70.0 0.4 collective-permute-start.9
  70.5 1.7 %shard_map.84 = bf16[2,2304]{1,0:T(2,128)(2,1)} custom-call(bf16[128,2304]{1,0:T(8,128)(2,1)} %bitcast.5.err), custom_call_target="tpu_custom_call" | custom-call | tf_op jit(solution)/shard_map/pallas_call | solution.py:248
  72.2 0.0 copy-done.3
  72.2 1.6 %shard_map.85 = f32[128,256]{1,0:T(8,128)S(1)} custom-call(f32[4,8,256]{2,1,0:T(8,128)S(1)} %copy-done.6, bf16[128,2304]{1,0:T(8,128)(2,1)} %bitcast.5.err, bf16[256,2304]{1,0:T(8,128)(2,1)S(1)} %copy-done.3), custom_call_target="tpu_custom_call" | custom-call | flops 150994944 | tf_op jit(solution)/shard_map/pallas_call | solution.py:239
  73.8 0.0 collective-permute-done.7
  73.8 0.0 collective-permute-done.8
  73.8 0.3 collective-permute-done.9
  74.1 0.7 fusion
  (5 shorter events, 0.1 us)
Async XLA Ops:
  2.5 9.6 %copy-start.2 = (bf16[256,2304]{1,0:T(8,128)(2,1)}, bf16[256,2304]{1,0:T(8,128)(2,1)S(1)}, u32[]{:S(2)}) copy-start(bf16[256,2304]{1,0:T(8,128)(2,1)S(1)} %get-tuple-element.8.mine.dec) | copy-start | bytes 3538948
  2.5 3.9 %collective-permute-start.1 = (bf16[128,256]{1,0:T(8,128)(2,1)S(1)}, bf16[128,256]{1,0:T(8,128)(2,1)S(1)}, u32[]{:S(2)}, u32[]{:S(2)}) collective-permute-start(bf16[128,256]{1,0:T(8,128)(2,1)S(1)} %get-tuple-element.7.latent), channel_id=1, source_target_pairs={{0,2},{1,3},{2,0},{3,1},{4,6},{5,7},{6,4},{7,5},{8,10},{9,11},{10,... | collective-permute-start | bytes 196616 | tf_op jit(solution)/shard_map/ppermute | solution.py:156
  4.7 7.4 %collective-permute-start = (bf16[128,256]{1,0:T(8,128)(2,1)S(1)}, bf16[128,256]{1,0:T(8,128)(2,1)S(1)}, u32[]{:S(2)}, u32[]{:S(2)}) collective-permute-start(bf16[128,256]{1,0:T(8,128)(2,1)S(1)} %get-tuple-element.7.latent), channel_id=1, source_target_pairs={{0,1},{1,0},{2,3},{3,2},{4,5},{5,4},{6,7},{7,6},{8,9},{9,8},{10,11... | collective-permute-start | bytes 196616 | tf_op jit(solution)/shard_map/ppermute | solution.py:156
  6.4 6.3 %collective-permute-start.2 = (bf16[128,256]{1,0:T(8,128)(2,1)S(1)}, bf16[128,256]{1,0:T(8,128)(2,1)S(1)}, u32[]{:S(2)}, u32[]{:S(2)}) collective-permute-start(bf16[128,256]{1,0:T(8,128)(2,1)S(1)} %collective-permute-done.1.l2), channel_id=1, source_target_pairs={{0,1},{1,0},{2,3},{3,2},{4,5},{5,4},{6,7},{7,6},{8,9},{9,8},{10,11... | collective-permute-start | bytes 196616 | tf_op jit(solution)/shard_map/ppermute | solution.py:156
  12.1 0.6 copy-start.5
  12.1 0.7 copy-start.7
  27.1 4.8 %collective-permute-start.3 = (bf16[16,2304]{1,0:T(8,128)(2,1)S(1)}, bf16[16,2304]{1,0:T(8,128)(2,1)S(1)}, u32[]{:S(2)}, u32[]{:S(2)}) collective-permute-start(bf16[16,2304]{1,0:T(8,128)(2,1)S(1)} %shard_map.81.a), channel_id=1, source_target_pairs={{0,32},{32,0},{1,33},{33,1},{2,34},{34,2},{3,35},{35,3},{4,36},{36... | collective-permute-start | bytes 221192 | tf_op jit(solution)/shard_map/ppermute | solution.py:156
  31.9 7.3 %collective-permute-start.4 = (bf16[16,2304]{1,0:T(8,128)(2,1)S(1)}, bf16[16,2304]{1,0:T(8,128)(2,1)S(1)}, u32[]{:S(2)}, u32[]{:S(2)}) collective-permute-start(bf16[16,2304]{1,0:T(8,128)(2,1)S(1)} %shard_map.82.s0), channel_id=1, source_target_pairs={{0,8},{8,0},{16,24},{24,16},{1,9},{9,1},{17,25},{25,17},{2,10},{10... | collective-permute-start | bytes 221192 | tf_op jit(solution)/shard_map/ppermute | solution.py:156
  35.0 7.1 %collective-permute-start.5 = (bf16[16,2304]{1,0:T(8,128)(2,1)S(1)}, bf16[16,2304]{1,0:T(8,128)(2,1)S(1)}, u32[]{:S(2)}, u32[]{:S(2)}) collective-permute-start(bf16[16,2304]{1,0:T(8,128)(2,1)S(1)} %shard_map.82.s0), channel_id=1, source_target_pairs={{0,16},{8,24},{16,0},{24,8},{1,17},{9,25},{17,1},{25,9},{2,18},{10... | collective-permute-start | bytes 221192 | tf_op jit(solution)/shard_map/ppermute | solution.py:156
  39.2 6.0 %collective-permute-start.6 = (bf16[16,2304]{1,0:T(8,128)(2,1)S(1)}, bf16[16,2304]{1,0:T(8,128)(2,1)S(1)}, u32[]{:S(2)}, u32[]{:S(2)}) collective-permute-start(bf16[16,2304]{1,0:T(8,128)(2,1)S(1)} %shard_map.82.s0), channel_id=1, source_target_pairs={{0,24},{8,16},{16,8},{24,0},{1,25},{9,17},{17,9},{25,1},{2,26},{10... | collective-permute-start | bytes 221192 | tf_op jit(solution)/shard_map/ppermute | solution.py:156
  45.2 0.8 %copy-start.4 = (bf16[8,16,2304]{2,1,0:T(8,128)(2,1)}, bf16[8,16,2304]{2,1,0:T(8,128)(2,1)S(1)}, u32[]{:S(2)}) copy-start(bf16[8,16,2304]{2,1,0:T(8,128)(2,1)S(1)} %shard_map.83) | copy-start | bytes 1769476
  46.0 12.7 %all-to-all-start.1 = ((bf16[8,16,2304]{2,1,0:T(8,128)(2,1)}), bf16[8,16,2304]{2,1,0:T(8,128)(2,1)}, u32[]{:S(2)}, u32[]{:S(2)}) async-start(bf16[8,16,2304]{2,1,0:T(8,128)(2,1)} %copy-done.4), calls=%async_computation.1 | async-start | bytes 1179648 | tf_op jit(solution)/shard_map/all_to_all | solution.py:233
  51.4 1.4 %copy-start = (bf16[2,2304,256]{2,1,0:T(8,128)(2,1)}, bf16[2,2304,256]{2,1,0:T(8,128)(2,1)S(1)}, u32[]{:S(2)}) copy-start(bf16[2,2304,256]{2,1,0:T(8,128)(2,1)S(1)} %shard_map.87.turned) | copy-start | bytes 7077892
  58.7 0.8 %copy-start.6 = (f32[4,8,256]{2,1,0:T(8,128)S(1)}, f32[4,8,256]{2,1,0:T(8,128)}, u32[]{:S(2)}) copy-start(f32[4,8,256]{2,1,0:T(8,128)} %copy-done.5) | copy-start | bytes 98308
  59.5 1.8 %copy-start.1 = (bf16[2,2304,256]{2,1,0:T(8,128)(2,1)S(1)}, bf16[2,2304,256]{2,1,0:T(8,128)(2,1)}, u32[]{:S(2)}) copy-start(bf16[2,2304,256]{2,1,0:T(8,128)(2,1)} %copy-done) | copy-start | bytes 7077892
  62.7 9.5 %copy-start.3 = (bf16[256,2304]{1,0:T(8,128)(2,1)S(1)}, bf16[256,2304]{1,0:T(8,128)(2,1)}, u32[]{:S(2)}) copy-start(bf16[256,2304]{1,0:T(8,128)(2,1)} %copy-done.2) | copy-start | bytes 3538948
  64.2 9.6 %collective-permute-start.7 = (bf16[128,256]{1,0:T(8,128)(2,1)S(1)}, bf16[128,256]{1,0:T(8,128)(2,1)S(1)}, u32[]{:S(2)}, u32[]{:S(2)}) collective-permute-start(bf16[128,256]{1,0:T(8,128)(2,1)S(1)} %shard_map.86), channel_id=1, source_target_pairs={{0,1},{1,0},{2,3},{3,2},{4,5},{5,4},{6,7},{7,6},{8,9},{9,8},{10,11... | collective-permute-start | bytes 196616 | tf_op jit(solution)/shard_map/ppermute | solution.py:156
  68.7 5.1 %collective-permute-start.8 = (bf16[128,256]{1,0:T(8,128)(2,1)S(1)}, bf16[128,256]{1,0:T(8,128)(2,1)S(1)}, u32[]{:S(2)}, u32[]{:S(2)}) collective-permute-start(bf16[128,256]{1,0:T(8,128)(2,1)S(1)} %shard_map.88), channel_id=1, source_target_pairs={{0,2},{1,3},{2,0},{3,1},{4,6},{5,7},{6,4},{7,5},{8,10},{9,11},{10,... | collective-permute-start | bytes 196616 | tf_op jit(solution)/shard_map/ppermute | solution.py:156
  70.0 4.1 %collective-permute-start.9 = (bf16[128,256]{1,0:T(8,128)(2,1)S(1)}, bf16[128,256]{1,0:T(8,128)(2,1)S(1)}, u32[]{:S(2)}, u32[]{:S(2)}) collective-permute-start(bf16[128,256]{1,0:T(8,128)(2,1)S(1)} %shard_map.89), channel_id=1, source_target_pairs={{0,3},{1,2},{2,1},{3,0},{4,7},{5,6},{6,5},{7,4},{8,11},{9,10},{10,... | collective-permute-start | bytes 196616 | tf_op jit(solution)/shard_map/ppermute | solution.py:156

commit v9 on v7

--- a/solution.py
+++ b/solution.py
@@ -125,6 +125,10 @@
     slab = dec[flip - 1] if flip else dec[...]
     term = lax.dot_general(err[...], slab, (((1,), (1,)), ((), ())), **DOT)
     out[...] = (keep[flip, 0:1, :] * term).astype(out.dtype)
+
+
+def join_kernel(a, b, out):
+    out[...] = (a[...] + b[...].astype(F32)).astype(out.dtype)
 
 
 def turn_kernel(dec, out):
@@ -234,14 +238,16 @@
             keep, err_full, slab
         )
 
-    back = {}
-    for flip in (3, 2, 1):
-        part = term(flip, BF)
-        back[flip] = swap(part, "tgt", flip)
+    diag = term(3, BF)
+    diag = swap(diag, "tgt", 1)
+    far = term(2, F32)
+    far = call(join_kernel, shape((tok, feats), BF), [VMEM] * 2)(far, diag)
+    far = swap(far, "tgt", 2)
+    near = term(1, BF)
+    near = swap(near, "tgt", 1)
     grad = term(0, F32)
     err_local = call(pick_kernel, shape((rows_local, width), BF), [VMEM])(err_full)
-    for flip in FLIPS:
-        grad = grad + back[flip].astype(F32)
+    grad = grad + near.astype(F32) + far.astype(F32)
     return (err_local[None], grad.astype(BF)[None])
 
 

time: 75.3 us -> 75.5 us (level)
  local copies, waits for them, and re-layouts: 3.3 us -> 4.86 us
  starting transfers between devices: 24.6 us -> 23.4 us
    unnamed x18 -> x16, local copies, waits for them, and re-layouts: 3.3 us -> 4.86 us
    ppermute x9, starting transfers between devices: 20.3 us -> 19.2 us  [swap(): return lax.ppermute(value, name, [(i, i ^ flip) for i in range(size)])]
  transfers between devices with their start and end apart: 10 -> 10, of which waited for: 5 -> 4; matrix products, arithmetic and copies ran while one was open for 0% -> 0% of each run, Pallas kernels for 9% -> 13%
where the time goes in v9:
time: 75.5 us; the launch traced here: 74.9 us
  starting transfers between devices  23.4 us (31%)
  blocking collectives  18.7 us (25%)
  Pallas kernels  13.4 us (18%)
  waiting for transfers between devices  13 us (17%)
  local copies, waits for them, and re-layouts  4.86 us (6%)
  between operations  0.81 us (1%)
    ppermute x9, starting transfers between devices, swap(): return lax.ppermute(value, name, [(i, i ^ flip) for i in range(size)])  19.2 us
    all_to_all x1, blocking collectives, per_device(): shares = lax.all_to_all(shares, NEAR, 0, 0, tiled=True)  18.7 us
    all_to_all x1, waiting for transfers between devices, per_device(): lax.all_to_all(copies, NEAR, 0, 0, tiled=True).reshape(tok, width)  7.25 us
    pallas_call x4, Pallas kernels, term(): call(kernel, shape((tok, feats), kind), [VMEM] * 3, flops)  6.06 us
    ppermute x9, waiting for transfers between devices, swap(): return lax.ppermute(value, name, [(i, i ^ flip) for i in range(size)])  5.77 us
    unnamed x16, local copies, waits for them, and re-layouts  4.86 us
    all_to_all x1, starting transfers between devices, per_device(): lax.all_to_all(copies, NEAR, 0, 0, tiled=True).reshape(tok, width)  4.25 us
    pallas_call x1, Pallas kernels, per_device(): dec, own, keep = load(in_hbm(pair_mask), latent, mine, slabs)  2.01 us
  transfers between devices with their start and end apart: 10, of which 4 were waited for; matrix products, arithmetic and copies ran while one was open for 0% of the time, Pallas kernels for 13%

profile of v9, /device:TPU:1, one launch (start us, length us, event | category | flops | bytes accessed | tf_op | source)
XLA Modules:
  0.0 74.9 jit_solution(8217317079378477403)
XLA Ops:
  0.6 1.9 %shard_map.77 = (bf16[128,256]{1,0:T(8,128)(2,1)S(1)}, bf16[256,2304]{1,0:T(8,128)(2,1)S(1)}) custom-call(bf16[128,2304]{1,0:T(8,128)(2,1)} %bitcast.14, bf16[2304,256]{1,0:T(8,128)(2,1)} %bitcast.13, f32[1,256]{1,0:T(1,128)} %bias.1, bf16[4,256,2304]{2,1,0:T(8,128)(2,1)} %bitcast.11), custom_call_target="tpu_custom_call" | custom-call | flops 150994944 | bytes 1179648 | tf_op jit(solution)/shard_map/pallas_call | solution.py:184
  2.5 0.0 copy-start.2
  2.5 2.2 %collective-permute-start.1 = (bf16[128,256]{1,0:T(8,128)(2,1)S(1)}, bf16[128,256]{1,0:T(8,128)(2,1)S(1)}, u32[]{:S(2)}, u32[]{:S(2)}) collective-permute-start(bf16[128,256]{1,0:T(8,128)(2,1)S(1)} %get-tuple-element.7.latent), channel_id=1, source_target_pairs={{0,2},{1,3},{2,0},{3,1},{4,6},{5,7},{6,4},{7,5},{8,10},{9,11},{10,... | collective-permute-start | bytes 196616 | tf_op jit(solution)/shard_map/ppermute | solution.py:156
  4.7 1.2 %collective-permute-start = (bf16[128,256]{1,0:T(8,128)(2,1)S(1)}, bf16[128,256]{1,0:T(8,128)(2,1)S(1)}, u32[]{:S(2)}, u32[]{:S(2)}) collective-permute-start(bf16[128,256]{1,0:T(8,128)(2,1)S(1)} %get-tuple-element.7.latent), channel_id=1, source_target_pairs={{0,1},{1,0},{2,3},{3,2},{4,5},{5,4},{6,7},{7,6},{8,9},{9,8},{10,11... | collective-permute-start | bytes 196616 | tf_op jit(solution)/shard_map/ppermute | solution.py:156
  5.9 0.5 collective-permute-done.1.l2
  6.4 3.7 %collective-permute-start.2 = (bf16[128,256]{1,0:T(8,128)(2,1)S(1)}, bf16[128,256]{1,0:T(8,128)(2,1)S(1)}, u32[]{:S(2)}, u32[]{:S(2)}) collective-permute-start(bf16[128,256]{1,0:T(8,128)(2,1)S(1)} %collective-permute-done.1.l2), channel_id=1, source_target_pairs={{0,1},{1,0},{2,3},{3,2},{4,5},{5,4},{6,7},{7,6},{8,9},{9,8},{10,11... | collective-permute-start | bytes 196616 | tf_op jit(solution)/shard_map/ppermute | solution.py:156
  10.1 2.0 %shard_map.78 = (bf16[3,256,2304]{2,1,0:T(8,128)(2,1)S(1)}, f32[128,2304]{1,0:T(8,128)S(1)}, f32[4,8,256]{2,1,0:T(8,128)S(1)}) custom-call(s32[4,4]{1,0:T(4,128)} %mask.1, bf16[128,256]{1,0:T(8,128)(2,1)S(1)} %get-tuple-element.7.latent, bf16[256,2304]{1,0:T(8,128)(2,1)S(1)} %get-tuple-element.8.mine.dec, bf16[4,256,2304]{2,1,0:T(8,128)(2,1)} %bitcast.12), custom_call_target="tpu_custom_call" | custom-call | flops 150994944 | bytes 4718592 | tf_op jit(solution)/shard_map/pallas_call | solution.py:214
  12.1 0.0 copy-done.2
  12.1 0.0 copy-start.5
  12.1 0.0 collective-permute-done.l1
  12.1 0.0 copy-start.7
  12.2 0.5 shard_map.79.most
  12.6 0.0 collective-permute-done.2.l3
  12.7 0.1 copy-done.5
  12.7 0.1 copy-done.7
  12.8 0.4 shard_map.80
  13.3 18.7 %all_to_all.10.shares = bf16[16,8,2304]{2,1,0:T(8,128)(2,1)S(1)} all-to-all(bf16[16,8,2304]{2,1,0:T(8,128)(2,1)S(1)} %bitcast.9), channel_id=1, replica_groups=mesh['x'=4,'yh'=2,'zh'=4,'zl'=2,'tgt'=4] {'x','yh','zl'}, dimensions={0} | all-to-all | bytes 1179648 | tf_op jit(solution)/shard_map/all_to_all | solution.py:224
  32.0 0.1 shard_map.81.s0
  32.1 3.1 %collective-permute-start.3 = (bf16[8,2304]{1,0:T(8,128)(2,1)S(1)}, bf16[8,2304]{1,0:T(8,128)(2,1)S(1)}, u32[]{:S(2)}, u32[]{:S(2)}) collective-permute-start(bf16[8,2304]{1,0:T(8,128)(2,1)S(1)} %shard_map.81.s0), channel_id=1, source_target_pairs={{0,8},{8,0},{16,24},{24,16},{1,9},{9,1},{17,25},{25,17},{2,10},{10... | collective-permute-start | bytes 110600 | tf_op jit(solution)/shard_map/ppermute | solution.py:156
  35.1 4.2 %collective-permute-start.4 = (bf16[8,2304]{1,0:T(8,128)(2,1)S(1)}, bf16[8,2304]{1,0:T(8,128)(2,1)S(1)}, u32[]{:S(2)}, u32[]{:S(2)}) collective-permute-start(bf16[8,2304]{1,0:T(8,128)(2,1)S(1)} %shard_map.81.s0), channel_id=1, source_target_pairs={{0,16},{8,24},{16,0},{24,8},{1,17},{9,25},{17,1},{25,9},{2,18},{10... | collective-permute-start | bytes 110600 | tf_op jit(solution)/shard_map/ppermute | solution.py:156
  39.3 0.0 collective-permute-start.5
  39.3 0.0 collective-permute-done.3.s1
  39.4 2.5 %collective-permute-done.4.s2 = bf16[8,2304]{1,0:T(8,128)(2,1)S(1)} collective-permute-done((bf16[8,2304]{1,0:T(8,128)(2,1)S(1)}, bf16[8,2304]{1,0:T(8,128)(2,1)S(1)}, u32[]{:S(2)}, u32[]{:S(2)}) %collective-permute-start.4) | collective-permute-done | bytes 36896 | tf_op jit(solution)/shard_map/ppermute | solution.py:156
  41.9 2.7 %collective-permute-done.5.s3 = bf16[8,2304]{1,0:T(8,128)(2,1)S(1)} collective-permute-done((bf16[8,2304]{1,0:T(8,128)(2,1)S(1)}, bf16[8,2304]{1,0:T(8,128)(2,1)S(1)}, u32[]{:S(2)}, u32[]{:S(2)}) %collective-permute-start.5) | collective-permute-done | bytes 36896 | tf_op jit(solution)/shard_map/ppermute | solution.py:156
  44.7 0.0 copy-start.4
  44.7 0.8 %copy-done.4 = bf16[16,8,2304]{2,1,0:T(8,128)(2,1)} copy-done((bf16[16,8,2304]{2,1,0:T(8,128)(2,1)}, bf16[16,8,2304]{2,1,0:T(8,128)(2,1)S(1)}, u32[]{:S(2)}) %copy-start.4) | copy-done | bytes 589848
  45.5 4.2 %all-to-all-start.1 = ((bf16[16,8,2304]{2,1,0:T(8,128)(2,1)}), bf16[16,8,2304]{2,1,0:T(8,128)(2,1)}, u32[]{:S(2)}, u32[]{:S(2)}) async-start(bf16[16,8,2304]{2,1,0:T(8,128)(2,1)} %copy-done.4), calls=%async_computation.1 | async-start | bytes 1179648 | tf_op jit(solution)/shard_map/all_to_all | solution.py:231
  49.8 0.7 shard_map.86.turned
  50.4 0.0 copy-start
  50.4 1.4 %copy-done = bf16[2,2304,256]{2,1,0:T(8,128)(2,1)} copy-done((bf16[2,2304,256]{2,1,0:T(8,128)(2,1)}, bf16[2,2304,256]{2,1,0:T(8,128)(2,1)S(1)}, u32[]{:S(2)}) %copy-start) | copy-done | bytes 2359320
  51.8 7.3 %all-to-all-done.1 = bf16[16,8,2304]{2,1,0:T(8,128)(2,1)} async-done(((bf16[16,8,2304]{2,1,0:T(8,128)(2,1)}), bf16[16,8,2304]{2,1,0:T(8,128)(2,1)}, u32[]{:S(2)}, u32[]{:S(2)}) %all-to-all-start.1) | async-done | bytes 589856 | tf_op jit(solution)/shard_map/all_to_all | solution.py:231
  59.1 0.0 copy-start.1
  59.1 1.7 %copy-done.1 = bf16[2,2304,256]{2,1,0:T(8,128)(2,1)S(1)} copy-done((bf16[2,2304,256]{2,1,0:T(8,128)(2,1)S(1)}, bf16[2,2304,256]{2,1,0:T(8,128)(2,1)}, u32[]{:S(2)}) %copy-start.1) | copy-done | bytes 2359320
  60.8 0.0 copy-start.6
  60.8 0.8 %copy-done.6 = f32[4,8,256]{2,1,0:T(8,128)S(1)} copy-done((f32[4,8,256]{2,1,0:T(8,128)S(1)}, f32[4,8,256]{2,1,0:T(8,128)}, u32[]{:S(2)}) %copy-start.6) | copy-done | bytes 32792
  61.5 1.4 %shard_map.88 = bf16[128,256]{1,0:T(8,128)(2,1)S(1)} custom-call(f32[4,8,256]{2,1,0:T(8,128)S(1)} %copy-done.6, bf16[128,2304]{1,0:T(8,128)(2,1)} %bitcast.5.err, bf16[2,2304,256]{2,1,0:T(8,128)(2,1)S(1)} %copy-done.1), custom_call_target="tpu_custom_call" | custom-call | flops 150994944 | tf_op jit(solution)/shard_map/pallas_call | solution.py:237
  62.9 4.2 %collective-permute-start.7 = (bf16[128,256]{1,0:T(8,128)(2,1)S(1)}, bf16[128,256]{1,0:T(8,128)(2,1)S(1)}, u32[]{:S(2)}, u32[]{:S(2)}) collective-permute-start(bf16[128,256]{1,0:T(8,128)(2,1)S(1)} %shard_map.88), channel_id=1, source_target_pairs={{0,1},{1,0},{2,3},{3,2},{4,5},{5,4},{6,7},{7,6},{8,9},{9,8},{10,11... | collective-permute-start | bytes 196616 | tf_op jit(solution)/shard_map/ppermute | solution.py:156
  67.1 1.6 %shard_map.85 = bf16[128,256]{1,0:T(8,128)(2,1)S(1)} custom-call(f32[4,8,256]{2,1,0:T(8,128)S(1)} %copy-done.6, bf16[128,2304]{1,0:T(8,128)(2,1)} %bitcast.5.err, bf16[3,256,2304]{2,1,0:T(8,128)(2,1)S(1)} %get-tuple-element.11.dec), custom_call_target="tpu_custom_call" | custom-call | flops 150994944 | tf_op jit(solution)/shard_map/pallas_call | solution.py:237
  68.7 0.1 collective-permute-start.6
  68.8 1.5 %shard_map.87.a = f32[128,256]{1,0:T(8,128)S(1)} custom-call(f32[4,8,256]{2,1,0:T(8,128)S(1)} %copy-done.6, bf16[128,2304]{1,0:T(8,128)(2,1)} %bitcast.5.err, bf16[2,2304,256]{2,1,0:T(8,128)(2,1)S(1)} %copy-done.1), custom_call_target="tpu_custom_call" | custom-call | flops 150994944 | tf_op jit(solution)/shard_map/pallas_call | solution.py:237
  70.3 0.0 collective-permute-done.7.b
  70.4 0.5 collective-permute-start.8
  70.8 1.7 %shard_map.83 = bf16[2,2304]{1,0:T(2,128)(2,1)} custom-call(bf16[128,2304]{1,0:T(8,128)(2,1)} %bitcast.5.err), custom_call_target="tpu_custom_call" | custom-call | tf_op jit(solution)/shard_map/pallas_call | solution.py:249
  72.6 0.0 copy-done.3
  72.6 1.6 %shard_map.84 = f32[128,256]{1,0:T(8,128)S(1)} custom-call(f32[4,8,256]{2,1,0:T(8,128)S(1)} %copy-done.6, bf16[128,2304]{1,0:T(8,128)(2,1)} %bitcast.5.err, bf16[256,2304]{1,0:T(8,128)(2,1)S(1)} %copy-done.3), custom_call_target="tpu_custom_call" | custom-call | flops 150994944 | tf_op jit(solution)/shard_map/pallas_call | solution.py:237
  74.2 0.0 collective-permute-done.6
  74.2 0.0 collective-permute-done.8
  74.2 0.7 fusion
  (3 shorter events, 0.1 us)
Async XLA Ops:
  2.5 9.6 %copy-start.2 = (bf16[256,2304]{1,0:T(8,128)(2,1)}, bf16[256,2304]{1,0:T(8,128)(2,1)S(1)}, u32[]{:S(2)}) copy-start(bf16[256,2304]{1,0:T(8,128)(2,1)S(1)} %get-tuple-element.8.mine.dec) | copy-start | bytes 3538948
  2.5 3.9 %collective-permute-start.1 = (bf16[128,256]{1,0:T(8,128)(2,1)S(1)}, bf16[128,256]{1,0:T(8,128)(2,1)S(1)}, u32[]{:S(2)}, u32[]{:S(2)}) collective-permute-start(bf16[128,256]{1,0:T(8,128)(2,1)S(1)} %get-tuple-element.7.latent), channel_id=1, source_target_pairs={{0,2},{1,3},{2,0},{3,1},{4,6},{5,7},{6,4},{7,5},{8,10},{9,11},{10,... | collective-permute-start | bytes 196616 | tf_op jit(solution)/shard_map/ppermute | solution.py:156
  4.7 7.4 %collective-permute-start = (bf16[128,256]{1,0:T(8,128)(2,1)S(1)}, bf16[128,256]{1,0:T(8,128)(2,1)S(1)}, u32[]{:S(2)}, u32[]{:S(2)}) collective-permute-start(bf16[128,256]{1,0:T(8,128)(2,1)S(1)} %get-tuple-element.7.latent), channel_id=1, source_target_pairs={{0,1},{1,0},{2,3},{3,2},{4,5},{5,4},{6,7},{7,6},{8,9},{9,8},{10,11... | collective-permute-start | bytes 196616 | tf_op jit(solution)/shard_map/ppermute | solution.py:156
  6.4 6.3 %collective-permute-start.2 = (bf16[128,256]{1,0:T(8,128)(2,1)S(1)}, bf16[128,256]{1,0:T(8,128)(2,1)S(1)}, u32[]{:S(2)}, u32[]{:S(2)}) collective-permute-start(bf16[128,256]{1,0:T(8,128)(2,1)S(1)} %collective-permute-done.1.l2), channel_id=1, source_target_pairs={{0,1},{1,0},{2,3},{3,2},{4,5},{5,4},{6,7},{7,6},{8,9},{9,8},{10,11... | collective-permute-start | bytes 196616 | tf_op jit(solution)/shard_map/ppermute | solution.py:156
  12.1 0.6 copy-start.5
  12.1 0.7 copy-start.7
  32.1 7.3 %collective-permute-start.3 = (bf16[8,2304]{1,0:T(8,128)(2,1)S(1)}, bf16[8,2304]{1,0:T(8,128)(2,1)S(1)}, u32[]{:S(2)}, u32[]{:S(2)}) collective-permute-start(bf16[8,2304]{1,0:T(8,128)(2,1)S(1)} %shard_map.81.s0), channel_id=1, source_target_pairs={{0,8},{8,0},{16,24},{24,16},{1,9},{9,1},{17,25},{25,17},{2,10},{10... | collective-permute-start | bytes 110600 | tf_op jit(solution)/shard_map/ppermute | solution.py:156
  35.1 6.8 %collective-permute-start.4 = (bf16[8,2304]{1,0:T(8,128)(2,1)S(1)}, bf16[8,2304]{1,0:T(8,128)(2,1)S(1)}, u32[]{:S(2)}, u32[]{:S(2)}) collective-permute-start(bf16[8,2304]{1,0:T(8,128)(2,1)S(1)} %shard_map.81.s0), channel_id=1, source_target_pairs={{0,16},{8,24},{16,0},{24,8},{1,17},{9,25},{17,1},{25,9},{2,18},{10... | collective-permute-start | bytes 110600 | tf_op jit(solution)/shard_map/ppermute | solution.py:156
  39.3 5.3 %collective-permute-start.5 = (bf16[8,2304]{1,0:T(8,128)(2,1)S(1)}, bf16[8,2304]{1,0:T(8,128)(2,1)S(1)}, u32[]{:S(2)}, u32[]{:S(2)}) collective-permute-start(bf16[8,2304]{1,0:T(8,128)(2,1)S(1)} %shard_map.81.s0), channel_id=1, source_target_pairs={{0,24},{8,16},{16,8},{24,0},{1,25},{9,17},{17,9},{25,1},{2,26},{10... | collective-permute-start | bytes 110600 | tf_op jit(solution)/shard_map/ppermute | solution.py:156
  44.7 0.8 %copy-start.4 = (bf16[16,8,2304]{2,1,0:T(8,128)(2,1)}, bf16[16,8,2304]{2,1,0:T(8,128)(2,1)S(1)}, u32[]{:S(2)}) copy-start(bf16[16,8,2304]{2,1,0:T(8,128)(2,1)S(1)} %shard_map.82) | copy-start | bytes 1769476
  45.5 13.6 %all-to-all-start.1 = ((bf16[16,8,2304]{2,1,0:T(8,128)(2,1)}), bf16[16,8,2304]{2,1,0:T(8,128)(2,1)}, u32[]{:S(2)}, u32[]{:S(2)}) async-start(bf16[16,8,2304]{2,1,0:T(8,128)(2,1)} %copy-done.4), calls=%async_computation.1 | async-start | bytes 1179648 | tf_op jit(solution)/shard_map/all_to_all | solution.py:231
  50.4 1.4 %copy-start = (bf16[2,2304,256]{2,1,0:T(8,128)(2,1)}, bf16[2,2304,256]{2,1,0:T(8,128)(2,1)S(1)}, u32[]{:S(2)}) copy-start(bf16[2,2304,256]{2,1,0:T(8,128)(2,1)S(1)} %shard_map.86.turned) | copy-start | bytes 7077892
  59.1 1.7 %copy-start.1 = (bf16[2,2304,256]{2,1,0:T(8,128)(2,1)S(1)}, bf16[2,2304,256]{2,1,0:T(8,128)(2,1)}, u32[]{:S(2)}) copy-start(bf16[2,2304,256]{2,1,0:T(8,128)(2,1)} %copy-done) | copy-start | bytes 7077892
  60.8 0.8 %copy-start.6 = (f32[4,8,256]{2,1,0:T(8,128)S(1)}, f32[4,8,256]{2,1,0:T(8,128)}, u32[]{:S(2)}) copy-start(f32[4,8,256]{2,1,0:T(8,128)} %copy-done.5) | copy-start | bytes 98308
  62.9 7.4 %collective-permute-start.7 = (bf16[128,256]{1,0:T(8,128)(2,1)S(1)}, bf16[128,256]{1,0:T(8,128)(2,1)S(1)}, u32[]{:S(2)}, u32[]{:S(2)}) collective-permute-start(bf16[128,256]{1,0:T(8,128)(2,1)S(1)} %shard_map.88), channel_id=1, source_target_pairs={{0,1},{1,0},{2,3},{3,2},{4,5},{5,4},{6,7},{7,6},{8,9},{9,8},{10,11... | collective-permute-start | bytes 196616 | tf_op jit(solution)/shard_map/ppermute | solution.py:156
  68.7 5.5 %collective-permute-start.6 = (bf16[128,256]{1,0:T(8,128)(2,1)S(1)}, bf16[128,256]{1,0:T(8,128)(2,1)S(1)}, u32[]{:S(2)}, u32[]{:S(2)}) collective-permute-start(bf16[128,256]{1,0:T(8,128)(2,1)S(1)} %shard_map.85), channel_id=1, source_target_pairs={{0,1},{1,0},{2,3},{3,2},{4,5},{5,4},{6,7},{7,6},{8,9},{9,8},{10,11... | collective-permute-start | bytes 196616 | tf_op jit(solution)/shard_map/ppermute | solution.py:156
  68.8 3.8 %copy-start.3 = (bf16[256,2304]{1,0:T(8,128)(2,1)S(1)}, bf16[256,2304]{1,0:T(8,128)(2,1)}, u32[]{:S(2)}) copy-start(bf16[256,2304]{1,0:T(8,128)(2,1)} %copy-done.2) | copy-start | bytes 3538948
  70.4 3.8 %collective-permute-start.8 = (bf16[128,256]{1,0:T(8,128)(2,1)S(1)}, bf16[128,256]{1,0:T(8,128)(2,1)S(1)}, u32[]{:S(2)}, u32[]{:S(2)}) collective-permute-start(bf16[128,256]{1,0:T(8,128)(2,1)S(1)} %shard_map.89), channel_id=1, source_target_pairs={{0,2},{1,3},{2,0},{3,1},{4,6},{5,7},{6,4},{7,5},{8,10},{9,11},{10,... | collective-permute-start | bytes 196616 | tf_op jit(solution)/shard_map/ppermute | solution.py:156

commit v10 on v9

--- a/solution.py
+++ b/solution.py
@@ -121,23 +121,18 @@
         out[i] = err
 
 
-def grad_kernel(flip, keep, err, dec, out):
-    slab = dec[flip - 1] if flip else dec[...]
-    term = lax.dot_general(err[...], slab, (((1,), (1,)), ((), ())), **DOT)
-    out[...] = (keep[flip, 0:1, :] * term).astype(out.dtype)
-
-
 def join_kernel(a, b, out):
     out[...] = (a[...] + b[...].astype(F32)).astype(out.dtype)
 
 
-def turn_kernel(dec, out):
-    for flip in (2, 3):
-        out[flip - 2] = dec[flip - 1].T
-
-
-def turned_kernel(flip, keep, err, turned, out):
-    term = jnp.dot(err[...], turned[flip - 2], **DOT)
+def turn_kernel(mine, dec, out):
+    out[0] = mine[...].T
+    for flip in FLIPS:
+        out[flip] = dec[flip - 1].T
+
+
+def term_kernel(flip, keep, err, turned, out):
+    term = jnp.dot(err[...], turned[flip], **DOT)
     out[...] = (keep[flip, 0:1, :] * term).astype(out.dtype)
 
 
@@ -226,16 +221,14 @@
     parts = [near] * ZH
     for flip in (2, 3, 1):
         parts[flip] = swap(near, "zh", flip)
-    turned = call(turn_kernel, shape((2, width, feats), BF), [VMEM])(dec)
+    turned = call(turn_kernel, shape((TG, width, feats), BF), [VMEM] * 2)(mine, dec)
     copies = call(spread_kernel, shape((GROUP, rows, width), BF), [VMEM] * 4)(*parts)
     err_full = lax.all_to_all(copies, NEAR, 0, 0, tiled=True).reshape(tok, width)
 
     def term(flip, kind):
-        far = flip > 1
-        kernel = functools.partial(turned_kernel if far else grad_kernel, flip)
-        slab = turned if far else dec if flip else mine
+        kernel = functools.partial(term_kernel, flip)
         return call(kernel, shape((tok, feats), kind), [VMEM] * 3, flops)(
-            keep, err_full, slab
+            keep, err_full, turned
         )
 
     diag = term(3, BF)

time: 75.5 us -> 75.5 us (level)
  local copies, waits for them, and re-layouts: 4.86 us -> 7.52 us
  waiting for transfers between devices: 13 us -> 10.4 us
    unnamed x16 -> x18, local copies, waits for them, and re-layouts: 4.86 us -> 7.52 us
    all_to_all x1, waiting for transfers between devices: 7.25 us -> 4.72 us  [per_device(): lax.all_to_all(copies, NEAR, 0, 0, tiled=True).reshape(tok, width)]
  transfers between devices with their start and end apart: 10 -> 10, of which waited for: 4 -> 3; matrix products, arithmetic and copies ran while one was open for 0% -> 0% of each run, Pallas kernels for 13% -> 13%
where the time goes in v10:
time: 75.5 us; the launch traced here: 74.8 us
  starting transfers between devices  23.2 us (31%)
  blocking collectives  18.7 us (25%)
  Pallas kernels  13.5 us (18%)
  waiting for transfers between devices  10.4 us (14%)
  local copies, waits for them, and re-layouts  7.52 us (10%)
  between operations  0.84 us (1%)
    ppermute x9, starting transfers between devices, swap(): return lax.ppermute(value, name, [(i, i ^ flip) for i in range(size)])  18.9 us
    all_to_all x1, blocking collectives, per_device(): shares = lax.all_to_all(shares, NEAR, 0, 0, tiled=True)  18.7 us
    unnamed x18, local copies, waits for them, and re-layouts  7.52 us
    ppermute x9, waiting for transfers between devices, swap(): return lax.ppermute(value, name, [(i, i ^ flip) for i in range(size)])  5.72 us
    pallas_call x4, Pallas kernels, term(): call(kernel, shape((tok, feats), kind), [VMEM] * 3, flops)  5.56 us
    all_to_all x1, waiting for transfers between devices, per_device(): lax.all_to_all(copies, NEAR, 0, 0, tiled=True).reshape(tok, width)  4.72 us
    all_to_all x1, starting transfers between devices, per_device(): lax.all_to_all(copies, NEAR, 0, 0, tiled=True).reshape(tok, width)  4.24 us
    pallas_call x1, Pallas kernels, per_device(): dec, own, keep = load(in_hbm(pair_mask), latent, mine, slabs)  2.01 us
  transfers between devices with their start and end apart: 10, of which 3 were waited for; matrix products, arithmetic and copies ran while one was open for 0% of the time, Pallas kernels for 13%

profile of v10, /device:TPU:1, one launch (start us, length us, event | category | flops | bytes accessed | tf_op | source)
XLA Modules:
  0.0 74.8 jit_solution(1628261326240525965)
XLA Ops:
  0.6 1.9 %shard_map.77 = (bf16[128,256]{1,0:T(8,128)(2,1)S(1)}, bf16[256,2304]{1,0:T(8,128)(2,1)S(1)}) custom-call(bf16[128,2304]{1,0:T(8,128)(2,1)} %bitcast.14, bf16[2304,256]{1,0:T(8,128)(2,1)} %bitcast.13, f32[1,256]{1,0:T(1,128)} %bias.1, bf16[4,256,2304]{2,1,0:T(8,128)(2,1)} %bitcast.11), custom_call_target="tpu_custom_call" | custom-call | flops 150994944 | bytes 1179648 | tf_op jit(solution)/shard_map/pallas_call | solution.py:179
  2.5 0.0 copy-start.2
  2.5 2.2 %collective-permute-start.1 = (bf16[128,256]{1,0:T(8,128)(2,1)S(1)}, bf16[128,256]{1,0:T(8,128)(2,1)S(1)}, u32[]{:S(2)}, u32[]{:S(2)}) collective-permute-start(bf16[128,256]{1,0:T(8,128)(2,1)S(1)} %get-tuple-element.7.latent), channel_id=1, source_target_pairs={{0,2},{1,3},{2,0},{3,1},{4,6},{5,7},{6,4},{7,5},{8,10},{9,11},{10,... | collective-permute-start | bytes 196616 | tf_op jit(solution)/shard_map/ppermute | solution.py:151
  4.7 1.2 %collective-permute-start = (bf16[128,256]{1,0:T(8,128)(2,1)S(1)}, bf16[128,256]{1,0:T(8,128)(2,1)S(1)}, u32[]{:S(2)}, u32[]{:S(2)}) collective-permute-start(bf16[128,256]{1,0:T(8,128)(2,1)S(1)} %get-tuple-element.7.latent), channel_id=1, source_target_pairs={{0,1},{1,0},{2,3},{3,2},{4,5},{5,4},{6,7},{7,6},{8,9},{9,8},{10,11... | collective-permute-start | bytes 196616 | tf_op jit(solution)/shard_map/ppermute | solution.py:151
  5.9 0.5 collective-permute-done.1.l2
  6.4 3.7 %collective-permute-start.2 = (bf16[128,256]{1,0:T(8,128)(2,1)S(1)}, bf16[128,256]{1,0:T(8,128)(2,1)S(1)}, u32[]{:S(2)}, u32[]{:S(2)}) collective-permute-start(bf16[128,256]{1,0:T(8,128)(2,1)S(1)} %collective-permute-done.1.l2), channel_id=1, source_target_pairs={{0,1},{1,0},{2,3},{3,2},{4,5},{5,4},{6,7},{7,6},{8,9},{9,8},{10,11... | collective-permute-start | bytes 196616 | tf_op jit(solution)/shard_map/ppermute | solution.py:151
  10.1 2.0 %shard_map.78 = (bf16[3,256,2304]{2,1,0:T(8,128)(2,1)S(1)}, f32[128,2304]{1,0:T(8,128)S(1)}, f32[4,8,256]{2,1,0:T(8,128)S(1)}) custom-call(s32[4,4]{1,0:T(4,128)} %mask.1, bf16[128,256]{1,0:T(8,128)(2,1)S(1)} %get-tuple-element.7.latent, bf16[256,2304]{1,0:T(8,128)(2,1)S(1)} %get-tuple-element.8.mine, bf16[4,256,2304]{2,1,0:T(8,128)(2,1)} %bitcast.12), custom_call_target="tpu_custom_call" | custom-call | flops 150994944 | bytes 4718592 | tf_op jit(solution)/shard_map/pallas_call | solution.py:209
  12.1 0.0 copy-done.2
  12.1 0.0 copy-start.5
  12.1 0.0 collective-permute-done.l1
  12.1 0.0 copy-start.8
  12.2 0.5 shard_map.79.most
  12.6 0.0 collective-permute-done.2.l3
  12.7 0.1 copy-done.5
  12.7 0.1 copy-done.8
  12.8 0.4 shard_map.80
  13.3 18.7 %all_to_all.10.shares = bf16[16,8,2304]{2,1,0:T(8,128)(2,1)S(1)} all-to-all(bf16[16,8,2304]{2,1,0:T(8,128)(2,1)S(1)} %bitcast.9), channel_id=1, replica_groups=mesh['x'=4,'yh'=2,'zh'=4,'zl'=2,'tgt'=4] {'x','yh','zl'}, dimensions={0} | all-to-all | bytes 1179648 | tf_op jit(solution)/shard_map/all_to_all | solution.py:219
  32.0 0.1 shard_map.81.s0
  32.1 5.2 %collective-permute-start.5 = (bf16[8,2304]{1,0:T(8,128)(2,1)S(1)}, bf16[8,2304]{1,0:T(8,128)(2,1)S(1)}, u32[]{:S(2)}, u32[]{:S(2)}) collective-permute-start(bf16[8,2304]{1,0:T(8,128)(2,1)S(1)} %shard_map.81.s0), channel_id=1, source_target_pairs={{0,24},{8,16},{16,8},{24,0},{1,25},{9,17},{17,9},{25,1},{2,26},{10... | collective-permute-start | bytes 110600 | tf_op jit(solution)/shard_map/ppermute | solution.py:151
  37.3 1.2 %collective-permute-start.4 = (bf16[8,2304]{1,0:T(8,128)(2,1)S(1)}, bf16[8,2304]{1,0:T(8,128)(2,1)S(1)}, u32[]{:S(2)}, u32[]{:S(2)}) collective-permute-start(bf16[8,2304]{1,0:T(8,128)(2,1)S(1)} %shard_map.81.s0), channel_id=1, source_target_pairs={{0,16},{8,24},{16,0},{24,8},{1,17},{9,25},{17,1},{25,9},{2,18},{10... | collective-permute-start | bytes 110600 | tf_op jit(solution)/shard_map/ppermute | solution.py:151
  38.4 1.0 %collective-permute-start.3 = (bf16[8,2304]{1,0:T(8,128)(2,1)S(1)}, bf16[8,2304]{1,0:T(8,128)(2,1)S(1)}, u32[]{:S(2)}, u32[]{:S(2)}) collective-permute-start(bf16[8,2304]{1,0:T(8,128)(2,1)S(1)} %shard_map.81.s0), channel_id=1, source_target_pairs={{0,8},{8,0},{16,24},{24,16},{1,9},{9,1},{17,25},{25,17},{2,10},{10... | collective-permute-start | bytes 110600 | tf_op jit(solution)/shard_map/ppermute | solution.py:151
  39.4 0.0 collective-permute-done.5.s3
  39.4 5.2 %collective-permute-done.4.s2 = bf16[8,2304]{1,0:T(8,128)(2,1)S(1)} collective-permute-done((bf16[8,2304]{1,0:T(8,128)(2,1)S(1)}, bf16[8,2304]{1,0:T(8,128)(2,1)S(1)}, u32[]{:S(2)}, u32[]{:S(2)}) %collective-permute-start.4) | collective-permute-done | bytes 36896 | tf_op jit(solution)/shard_map/ppermute | solution.py:151
  44.7 0.0 collective-permute-done.3.s1
  44.7 0.0 copy-start.4
  44.7 0.8 %copy-done.4 = bf16[16,8,2304]{2,1,0:T(8,128)(2,1)} copy-done((bf16[16,8,2304]{2,1,0:T(8,128)(2,1)}, bf16[16,8,2304]{2,1,0:T(8,128)(2,1)S(1)}, u32[]{:S(2)}) %copy-start.4) | copy-done | bytes 589848
  45.6 4.2 %all-to-all-start.1 = ((bf16[16,8,2304]{2,1,0:T(8,128)(2,1)}), bf16[16,8,2304]{2,1,0:T(8,128)(2,1)}, u32[]{:S(2)}, u32[]{:S(2)}) async-start(bf16[16,8,2304]{2,1,0:T(8,128)(2,1)} %copy-done.4), calls=%async_computation.1 | async-start | bytes 1179648 | tf_op jit(solution)/shard_map/all_to_all | solution.py:226
  49.8 0.0 copy-start.3
  49.8 1.3 %copy-done.3 = bf16[256,2304]{1,0:T(8,128)(2,1)S(1)} copy-done((bf16[256,2304]{1,0:T(8,128)(2,1)S(1)}, bf16[256,2304]{1,0:T(8,128)(2,1)}, u32[]{:S(2)}) %copy-start.3) | copy-done | bytes 1179672
  51.1 1.3 %shard_map.84.turned = bf16[4,2304,256]{2,1,0:T(8,128)(2,1)S(1)} custom-call(bf16[256,2304]{1,0:T(8,128)(2,1)S(1)} %copy-done.3, bf16[3,256,2304]{2,1,0:T(8,128)(2,1)S(1)} %get-tuple-element.11.dec), custom_call_target="tpu_custom_call" | custom-call | tf_op jit(solution)/shard_map/pallas_call | solution.py:224
  52.4 2.1 %copy-done = bf16[4,2304,256]{2,1,0:T(8,128)(2,1)} copy-done((bf16[4,2304,256]{2,1,0:T(8,128)(2,1)}, bf16[4,2304,256]{2,1,0:T(8,128)(2,1)S(1)}, u32[]{:S(2)}) %copy-start) | copy-done | bytes 4718616
  54.5 4.7 %all-to-all-done.1 = bf16[16,8,2304]{2,1,0:T(8,128)(2,1)} async-done(((bf16[16,8,2304]{2,1,0:T(8,128)(2,1)}), bf16[16,8,2304]{2,1,0:T(8,128)(2,1)}, u32[]{:S(2)}, u32[]{:S(2)}) %all-to-all-start.1) | async-done | bytes 589856 | tf_op jit(solution)/shard_map/all_to_all | solution.py:226
  59.2 2.3 %copy-done.1 = bf16[4,2304,256]{2,1,0:T(8,128)(2,1)S(1)} copy-done((bf16[4,2304,256]{2,1,0:T(8,128)(2,1)S(1)}, bf16[4,2304,256]{2,1,0:T(8,128)(2,1)}, u32[]{:S(2)}) %copy-start.1) | copy-done | bytes 4718616
  61.6 0.8 %copy-done.6 = f32[4,8,256]{2,1,0:T(8,128)S(1)} copy-done((f32[4,8,256]{2,1,0:T(8,128)S(1)}, f32[4,8,256]{2,1,0:T(8,128)}, u32[]{:S(2)}) %copy-start.6) | copy-done | bytes 32792
  62.3 1.4 %shard_map.88 = bf16[128,256]{1,0:T(8,128)(2,1)S(1)} custom-call(f32[4,8,256]{2,1,0:T(8,128)S(1)} %copy-done.6, bf16[128,2304]{1,0:T(8,128)(2,1)} %bitcast.5.err, bf16[4,2304,256]{2,1,0:T(8,128)(2,1)S(1)} %copy-done.1), custom_call_target="tpu_custom_call" | custom-call | flops 150994944 | tf_op jit(solution)/shard_map/pallas_call | solution.py:230
  63.7 0.0 copy-start.7
  63.7 3.9 %collective-permute-start.7 = (bf16[128,256]{1,0:T(8,128)(2,1)S(1)}, bf16[128,256]{1,0:T(8,128)(2,1)S(1)}, u32[]{:S(2)}, u32[]{:S(2)}) collective-permute-start(bf16[128,256]{1,0:T(8,128)(2,1)S(1)} %shard_map.88), channel_id=1, source_target_pairs={{0,1},{1,0},{2,3},{3,2},{4,5},{5,4},{6,7},{7,6},{8,9},{9,8},{10,11... | collective-permute-start | bytes 196616 | tf_op jit(solution)/shard_map/ppermute | solution.py:151
  67.6 1.4 %shard_map.86 = bf16[128,256]{1,0:T(8,128)(2,1)S(1)} custom-call(f32[4,8,256]{2,1,0:T(8,128)S(1)} %copy-done.6, bf16[128,2304]{1,0:T(8,128)(2,1)} %bitcast.5.err, bf16[4,2304,256]{2,1,0:T(8,128)(2,1)S(1)} %copy-done.1), custom_call_target="tpu_custom_call" | custom-call | flops 150994944 | tf_op jit(solution)/shard_map/pallas_call | solution.py:230
  69.0 0.1 collective-permute-start.6
  69.1 0.0 copy-done.7
  69.1 1.4 %shard_map.87.a = f32[128,256]{1,0:T(8,128)S(1)} custom-call(f32[4,8,256]{2,1,0:T(8,128)S(1)} %copy-done.7, bf16[128,2304]{1,0:T(8,128)(2,1)} %bitcast.5.err, bf16[4,2304,256]{2,1,0:T(8,128)(2,1)S(1)} %copy-done.1), custom_call_target="tpu_custom_call" | custom-call | flops 150994944 | tf_op jit(solution)/shard_map/pallas_call | solution.py:230
  70.5 0.0 collective-permute-done.7.b
  70.5 0.5 collective-permute-start.8
  71.0 1.7 %shard_map.83 = bf16[2,2304]{1,0:T(2,128)(2,1)} custom-call(bf16[128,2304]{1,0:T(8,128)(2,1)} %bitcast.5.err), custom_call_target="tpu_custom_call" | custom-call | tf_op jit(solution)/shard_map/pallas_call | solution.py:242
  72.7 1.4 %shard_map.85 = f32[128,256]{1,0:T(8,128)S(1)} custom-call(f32[4,8,256]{2,1,0:T(8,128)S(1)} %copy-done.7, bf16[128,2304]{1,0:T(8,128)(2,1)} %bitcast.5.err, bf16[4,2304,256]{2,1,0:T(8,128)(2,1)S(1)} %copy-done.1), custom_call_target="tpu_custom_call" | custom-call | flops 150994944 | tf_op jit(solution)/shard_map/pallas_call | solution.py:230
  74.1 0.0 collective-permute-done.6
  74.1 0.0 collective-permute-done.8
  74.2 0.7 fusion
  (5 shorter events, 0.1 us)
Async XLA Ops:
  2.5 9.6 %copy-start.2 = (bf16[256,2304]{1,0:T(8,128)(2,1)}, bf16[256,2304]{1,0:T(8,128)(2,1)S(1)}, u32[]{:S(2)}) copy-start(bf16[256,2304]{1,0:T(8,128)(2,1)S(1)} %get-tuple-element.8.mine) | copy-start | bytes 3538948
  2.5 3.9 %collective-permute-start.1 = (bf16[128,256]{1,0:T(8,128)(2,1)S(1)}, bf16[128,256]{1,0:T(8,128)(2,1)S(1)}, u32[]{:S(2)}, u32[]{:S(2)}) collective-permute-start(bf16[128,256]{1,0:T(8,128)(2,1)S(1)} %get-tuple-element.7.latent), channel_id=1, source_target_pairs={{0,2},{1,3},{2,0},{3,1},{4,6},{5,7},{6,4},{7,5},{8,10},{9,11},{10,... | collective-permute-start | bytes 196616 | tf_op jit(solution)/shard_map/ppermute | solution.py:151
  4.7 7.4 %collective-permute-start = (bf16[128,256]{1,0:T(8,128)(2,1)S(1)}, bf16[128,256]{1,0:T(8,128)(2,1)S(1)}, u32[]{:S(2)}, u32[]{:S(2)}) collective-permute-start(bf16[128,256]{1,0:T(8,128)(2,1)S(1)} %get-tuple-element.7.latent), channel_id=1, source_target_pairs={{0,1},{1,0},{2,3},{3,2},{4,5},{5,4},{6,7},{7,6},{8,9},{9,8},{10,11... | collective-permute-start | bytes 196616 | tf_op jit(solution)/shard_map/ppermute | solution.py:151
  6.4 6.3 %collective-permute-start.2 = (bf16[128,256]{1,0:T(8,128)(2,1)S(1)}, bf16[128,256]{1,0:T(8,128)(2,1)S(1)}, u32[]{:S(2)}, u32[]{:S(2)}) collective-permute-start(bf16[128,256]{1,0:T(8,128)(2,1)S(1)} %collective-permute-done.1.l2), channel_id=1, source_target_pairs={{0,1},{1,0},{2,3},{3,2},{4,5},{5,4},{6,7},{7,6},{8,9},{9,8},{10,11... | collective-permute-start | bytes 196616 | tf_op jit(solution)/shard_map/ppermute | solution.py:151
  12.1 0.6 copy-start.5
  12.1 0.7 copy-start.8
  32.1 7.4 %collective-permute-start.5 = (bf16[8,2304]{1,0:T(8,128)(2,1)S(1)}, bf16[8,2304]{1,0:T(8,128)(2,1)S(1)}, u32[]{:S(2)}, u32[]{:S(2)}) collective-permute-start(bf16[8,2304]{1,0:T(8,128)(2,1)S(1)} %shard_map.81.s0), channel_id=1, source_target_pairs={{0,24},{8,16},{16,8},{24,0},{1,25},{9,17},{17,9},{25,1},{2,26},{10... | collective-permute-start | bytes 110600 | tf_op jit(solution)/shard_map/ppermute | solution.py:151
  37.3 7.4 %collective-permute-start.4 = (bf16[8,2304]{1,0:T(8,128)(2,1)S(1)}, bf16[8,2304]{1,0:T(8,128)(2,1)S(1)}, u32[]{:S(2)}, u32[]{:S(2)}) collective-permute-start(bf16[8,2304]{1,0:T(8,128)(2,1)S(1)} %shard_map.81.s0), channel_id=1, source_target_pairs={{0,16},{8,24},{16,0},{24,8},{1,17},{9,25},{17,1},{25,9},{2,18},{10... | collective-permute-start | bytes 110600 | tf_op jit(solution)/shard_map/ppermute | solution.py:151
  38.4 6.3 %collective-permute-start.3 = (bf16[8,2304]{1,0:T(8,128)(2,1)S(1)}, bf16[8,2304]{1,0:T(8,128)(2,1)S(1)}, u32[]{:S(2)}, u32[]{:S(2)}) collective-permute-start(bf16[8,2304]{1,0:T(8,128)(2,1)S(1)} %shard_map.81.s0), channel_id=1, source_target_pairs={{0,8},{8,0},{16,24},{24,16},{1,9},{9,1},{17,25},{25,17},{2,10},{10... | collective-permute-start | bytes 110600 | tf_op jit(solution)/shard_map/ppermute | solution.py:151
  44.7 0.8 %copy-start.4 = (bf16[16,8,2304]{2,1,0:T(8,128)(2,1)}, bf16[16,8,2304]{2,1,0:T(8,128)(2,1)S(1)}, u32[]{:S(2)}) copy-start(bf16[16,8,2304]{2,1,0:T(8,128)(2,1)S(1)} %shard_map.82) | copy-start | bytes 1769476
  45.6 13.6 %all-to-all-start.1 = ((bf16[16,8,2304]{2,1,0:T(8,128)(2,1)}), bf16[16,8,2304]{2,1,0:T(8,128)(2,1)}, u32[]{:S(2)}, u32[]{:S(2)}) async-start(bf16[16,8,2304]{2,1,0:T(8,128)(2,1)} %copy-done.4), calls=%async_computation.1 | async-start | bytes 1179648 | tf_op jit(solution)/shard_map/all_to_all | solution.py:226
  49.8 1.3 %copy-start.3 = (bf16[256,2304]{1,0:T(8,128)(2,1)S(1)}, bf16[256,2304]{1,0:T(8,128)(2,1)}, u32[]{:S(2)}) copy-start(bf16[256,2304]{1,0:T(8,128)(2,1)} %copy-done.2) | copy-start | bytes 3538948
  52.4 2.1 %copy-start = (bf16[4,2304,256]{2,1,0:T(8,128)(2,1)}, bf16[4,2304,256]{2,1,0:T(8,128)(2,1)S(1)}, u32[]{:S(2)}) copy-start(bf16[4,2304,256]{2,1,0:T(8,128)(2,1)S(1)} %shard_map.84.turned) | copy-start | bytes 14155780
  59.2 2.3 %copy-start.1 = (bf16[4,2304,256]{2,1,0:T(8,128)(2,1)S(1)}, bf16[4,2304,256]{2,1,0:T(8,128)(2,1)}, u32[]{:S(2)}) copy-start(bf16[4,2304,256]{2,1,0:T(8,128)(2,1)} %copy-done) | copy-start | bytes 14155780
  61.6 0.8 %copy-start.6 = (f32[4,8,256]{2,1,0:T(8,128)S(1)}, f32[4,8,256]{2,1,0:T(8,128)}, u32[]{:S(2)}) copy-start(f32[4,8,256]{2,1,0:T(8,128)} %copy-done.5) | copy-start | bytes 98308
  63.7 5.4 %copy-start.7 = (f32[4,8,256]{2,1,0:T(8,128)S(1)}, f32[4,8,256]{2,1,0:T(8,128)}, u32[]{:S(2)}) copy-start(f32[4,8,256]{2,1,0:T(8,128)} %copy-done.5) | copy-start | bytes 98308
  63.7 6.8 %collective-permute-start.7 = (bf16[128,256]{1,0:T(8,128)(2,1)S(1)}, bf16[128,256]{1,0:T(8,128)(2,1)S(1)}, u32[]{:S(2)}, u32[]{:S(2)}) collective-permute-start(bf16[128,256]{1,0:T(8,128)(2,1)S(1)} %shard_map.88), channel_id=1, source_target_pairs={{0,1},{1,0},{2,3},{3,2},{4,5},{5,4},{6,7},{7,6},{8,9},{9,8},{10,11... | collective-permute-start | bytes 196616 | tf_op jit(solution)/shard_map/ppermute | solution.py:151
  69.0 5.2 %collective-permute-start.6 = (bf16[128,256]{1,0:T(8,128)(2,1)S(1)}, bf16[128,256]{1,0:T(8,128)(2,1)S(1)}, u32[]{:S(2)}, u32[]{:S(2)}) collective-permute-start(bf16[128,256]{1,0:T(8,128)(2,1)S(1)} %shard_map.86), channel_id=1, source_target_pairs={{0,1},{1,0},{2,3},{3,2},{4,5},{5,4},{6,7},{7,6},{8,9},{9,8},{10,11... | collective-permute-start | bytes 196616 | tf_op jit(solution)/shard_map/ppermute | solution.py:151
  70.5 3.6 %collective-permute-start.8 = (bf16[128,256]{1,0:T(8,128)(2,1)S(1)}, bf16[128,256]{1,0:T(8,128)(2,1)S(1)}, u32[]{:S(2)}, u32[]{:S(2)}) collective-permute-start(bf16[128,256]{1,0:T(8,128)(2,1)S(1)} %shard_map.89), channel_id=1, source_target_pairs={{0,2},{1,3},{2,0},{3,1},{4,6},{5,7},{6,4},{7,5},{8,10},{9,11},{10,... | collective-permute-start | bytes 196616 | tf_op jit(solution)/shard_map/ppermute | solution.py:151

commit v11 on v10

--- a/solution.py
+++ b/solution.py
@@ -90,7 +90,7 @@
         out[:, cols] = total
 
 
-def decode_last_kernel(keep, most, l3, targets, dec, out):
+def decode_last_kernel(keep, most, l3, targets, mine, dec, out, turned):
     base = spot_of() * targets.shape[0]
     tok, width = out.shape
     step = 256
@@ -104,6 +104,10 @@
             total = total - jnp.where(row_ids == base + r, line, 0.0)
         out[:, cols] = total.astype(BF)
 
+    @pl.when(lax.axis_index("tgt") % 2 == 1)
+    def _():
+        turn(mine, dec, turned)
+
 
 def gather_sum_kernel(shares, out):
     total = shares[0].astype(F32)
@@ -125,10 +129,16 @@
     out[...] = (a[...] + b[...].astype(F32)).astype(out.dtype)
 
 
-def turn_kernel(mine, dec, out):
+def turn(mine, dec, out):
     out[0] = mine[...].T
     for flip in FLIPS:
         out[flip] = dec[flip - 1].T
+
+
+def turn_kernel(mine, dec, early, out):
+    @pl.when(lax.axis_index("tgt") % 2 == 0)
+    def _():
+        turn(mine, dec, out)
 
 
 def term_kernel(flip, keep, err, turned, out):
@@ -155,13 +165,14 @@
     return pltpu.with_memory_space_constraint(value, pltpu.HBM)
 
 
-def call(kernel, outs, specs, flops=0, moved=0, scratch=(), out_spec=VMEM):
+def call(kernel, outs, specs, flops=0, moved=0, scratch=(), out_spec=VMEM, alias=None):
     return pl.pallas_call(
         kernel,
         out_shape=outs,
         in_specs=specs,
         out_specs=out_spec,
         scratch_shapes=scratch,
+        input_output_aliases=alias or {},
         cost_estimate=cost(flops, moved),
         compiler_params=pltpu.CompilerParams(vmem_limit_bytes=LIMIT),
     )
@@ -211,9 +222,14 @@
     most = call(decode_pair_kernel, shape((tok, width), F32), [VMEM] * 5, 2 * flops)(
         keep, own, l1, l2, dec
     )
-    shares = call(decode_last_kernel, shape((tok, width), BF), [VMEM] * 5, flops)(
-        keep, most, l3, targets[0], dec
-    )
+    turns = shape((TG, width, feats), BF)
+    shares, early = call(
+        decode_last_kernel,
+        [shape((tok, width), BF), turns],
+        [VMEM] * 6,
+        flops,
+        out_spec=[VMEM] * 2,
+    )(keep, most, l3, targets[0], mine, dec)
 
     shares = shares.reshape(GROUP, rows, width)
     shares = lax.all_to_all(shares, NEAR, 0, 0, tiled=True)
@@ -221,7 +237,7 @@
     parts = [near] * ZH
     for flip in (2, 3, 1):
         parts[flip] = swap(near, "zh", flip)
-    turned = call(turn_kernel, shape((TG, width, feats), BF), [VMEM] * 2)(mine, dec)
+    turned = call(turn_kernel, turns, [VMEM, VMEM, ANY], alias={2: 0})(mine, dec, early)
     copies = call(spread_kernel, shape((GROUP, rows, width), BF), [VMEM] * 4)(*parts)
     err_full = lax.all_to_all(copies, NEAR, 0, 0, tiled=True).reshape(tok, width)
 

time: 75.5 us -> 80 us (1.060)
  local copies, waits for them, and re-layouts: 7.52 us -> 12 us
  starting transfers between devices: 23.2 us -> 22.1 us
    unnamed x18 -> x26, local copies, waits for them, and re-layouts: 7.52 us -> 12 us
    ppermute x9, starting transfers between devices: 18.9 us -> 17.9 us  [swap(): return lax.ppermute(value, name, [(i, i ^ flip) for i in range(size)])]
  transfers between devices with their start and end apart: 10 -> 10, of which waited for: 3 -> 3; matrix products, arithmetic and copies ran while one was open for 0% -> 0% of each run, Pallas kernels for 13% -> 11%
where the time goes in v11:
time: 80 us; the launch traced here: 79.3 us
  starting transfers between devices  22.1 us (28%)
  blocking collectives  19.1 us (24%)
  Pallas kernels  13.6 us (17%)
  local copies, waits for them, and re-layouts  12 us (15%)
  waiting for transfers between devices  10.9 us (14%)
  between operations  0.84 us (1%)
    all_to_all x1, blocking collectives, per_device(): shares = lax.all_to_all(shares, NEAR, 0, 0, tiled=True)  19.1 us
    ppermute x9, starting transfers between devices, swap(): return lax.ppermute(value, name, [(i, i ^ flip) for i in range(size)])  17.9 us
    unnamed x26, local copies, waits for them, and re-layouts  12 us
    ppermute x9, waiting for transfers between devices, swap(): return lax.ppermute(value, name, [(i, i ^ flip) for i in range(size)])  6.23 us
    pallas_call x4, Pallas kernels, term(): call(kernel, shape((tok, feats), kind), [VMEM] * 3, flops)  5.7 us
    all_to_all x1, waiting for transfers between devices, per_device(): lax.all_to_all(copies, NEAR, 0, 0, tiled=True).reshape(tok, width)  4.71 us
    all_to_all x1, starting transfers between devices, per_device(): lax.all_to_all(copies, NEAR, 0, 0, tiled=True).reshape(tok, width)  4.25 us
    pallas_call x1, Pallas kernels, per_device(): dec, own, keep = load(in_hbm(pair_mask), latent, mine, slabs)  2.01 us
  transfers between devices with their start and end apart: 10, of which 3 were waited for; matrix products, arithmetic and copies ran while one was open for 0% of the time, Pallas kernels for 11%

profile of v11, /device:TPU:1, one launch (start us, length us, event | category | flops | bytes accessed | tf_op | source)
XLA Modules:
  0.0 79.3 jit_solution(6777138552993141626)
XLA Ops:
  0.6 1.9 %shard_map.77 = (bf16[128,256]{1,0:T(8,128)(2,1)S(1)}, bf16[256,2304]{1,0:T(8,128)(2,1)S(1)}) custom-call(bf16[128,2304]{1,0:T(8,128)(2,1)} %bitcast.16, bf16[2304,256]{1,0:T(8,128)(2,1)} %bitcast.15, f32[1,256]{1,0:T(1,128)} %bias.1, bf16[4,256,2304]{2,1,0:T(8,128)(2,1)} %bitcast.13), custom_call_target="tpu_custom_call" | custom-call | flops 150994944 | bytes 1179648 | tf_op jit(solution)/shard_map/pallas_call | solution.py:190
  2.5 0.0 copy-start.4
  2.5 2.2 %collective-permute-start.1 = (bf16[128,256]{1,0:T(8,128)(2,1)S(1)}, bf16[128,256]{1,0:T(8,128)(2,1)S(1)}, u32[]{:S(2)}, u32[]{:S(2)}) collective-permute-start(bf16[128,256]{1,0:T(8,128)(2,1)S(1)} %get-tuple-element.9.latent), channel_id=1, source_target_pairs={{0,2},{1,3},{2,0},{3,1},{4,6},{5,7},{6,4},{7,5},{8,10},{9,11},{10,... | collective-permute-start | bytes 196616 | tf_op jit(solution)/shard_map/ppermute | solution.py:161
  4.7 1.2 %collective-permute-start = (bf16[128,256]{1,0:T(8,128)(2,1)S(1)}, bf16[128,256]{1,0:T(8,128)(2,1)S(1)}, u32[]{:S(2)}, u32[]{:S(2)}) collective-permute-start(bf16[128,256]{1,0:T(8,128)(2,1)S(1)} %get-tuple-element.9.latent), channel_id=1, source_target_pairs={{0,1},{1,0},{2,3},{3,2},{4,5},{5,4},{6,7},{7,6},{8,9},{9,8},{10,11... | collective-permute-start | bytes 196616 | tf_op jit(solution)/shard_map/ppermute | solution.py:161
  5.9 0.5 collective-permute-done.1.l2
  6.4 3.7 %collective-permute-start.2 = (bf16[128,256]{1,0:T(8,128)(2,1)S(1)}, bf16[128,256]{1,0:T(8,128)(2,1)S(1)}, u32[]{:S(2)}, u32[]{:S(2)}) collective-permute-start(bf16[128,256]{1,0:T(8,128)(2,1)S(1)} %collective-permute-done.1.l2), channel_id=1, source_target_pairs={{0,1},{1,0},{2,3},{3,2},{4,5},{5,4},{6,7},{7,6},{8,9},{9,8},{10,11... | collective-permute-start | bytes 196616 | tf_op jit(solution)/shard_map/ppermute | solution.py:161
  10.1 2.0 %shard_map.78 = (bf16[3,256,2304]{2,1,0:T(8,128)(2,1)S(1)}, f32[128,2304]{1,0:T(8,128)S(1)}, f32[4,8,256]{2,1,0:T(8,128)S(1)}) custom-call(s32[4,4]{1,0:T(4,128)} %mask.1, bf16[128,256]{1,0:T(8,128)(2,1)S(1)} %get-tuple-element.9.latent, bf16[256,2304]{1,0:T(8,128)(2,1)S(1)} %get-tuple-element.10.mine, bf16[4,256,2304]{2,1,0:T(8,128)(2,1)} %bitcast.14), custom_call_target="tpu_custom_call" | custom-call | flops 150994944 | bytes 4718592 | tf_op jit(solution)/shard_map/pallas_call | solution.py:220
  12.1 0.0 copy-start.7
  12.1 0.0 copy-start.10
  12.1 0.0 collective-permute-done.l1
  12.1 0.5 shard_map.79.most
  12.6 0.0 collective-permute-done.2.l3
  12.6 0.0 copy-done.4
  12.7 0.2 copy-done.10
  12.8 1.7 %shard_map.80 = (bf16[128,2304]{1,0:T(8,128)(2,1)S(1)}, bf16[4,2304,256]{2,1,0:T(8,128)(2,1)S(1)}) custom-call(f32[4,8,256]{2,1,0:T(8,128)S(1)} %get-tuple-element.11.keep, f32[128,2304]{1,0:T(8,128)S(1)} %shard_map.79.most, bf16[128,256]{1,0:T(8,128)(2,1)S(1)} %collective-permute-done.2.l3, bf16[2,2304]{1,0:T(2,128)(2,1)S(1)} %bitcast.12, ...), custom_call_target="tpu_custom_call" | custom-call | flops 150994944 | tf_op jit(solution)/shard_map/pallas_call | solution.py:226
  14.5 0.0 copy-done.7
  14.5 0.0 copy-start
  14.5 2.1 %copy-done = bf16[4,2304,256]{2,1,0:T(8,128)(2,1)} copy-done((bf16[4,2304,256]{2,1,0:T(8,128)(2,1)}, bf16[4,2304,256]{2,1,0:T(8,128)(2,1)S(1)}, u32[]{:S(2)}) %copy-start) | copy-done | bytes 4718616
  16.7 19.1 %all_to_all.10.shares = bf16[16,8,2304]{2,1,0:T(8,128)(2,1)S(1)} all-to-all(bf16[16,8,2304]{2,1,0:T(8,128)(2,1)S(1)} %bitcast.11), channel_id=1, replica_groups=mesh['x'=4,'yh'=2,'zh'=4,'zl'=2,'tgt'=4] {'x','yh','zl'}, dimensions={0} | all-to-all | bytes 1179648 | tf_op jit(solution)/shard_map/all_to_all | solution.py:235
  35.8 0.1 shard_map.81.s0
  35.9 5.2 %collective-permute-start.5 = (bf16[8,2304]{1,0:T(8,128)(2,1)S(1)}, bf16[8,2304]{1,0:T(8,128)(2,1)S(1)}, u32[]{:S(2)}, u32[]{:S(2)}) collective-permute-start(bf16[8,2304]{1,0:T(8,128)(2,1)S(1)} %shard_map.81.s0), channel_id=1, source_target_pairs={{0,24},{8,16},{16,8},{24,0},{1,25},{9,17},{17,9},{25,1},{2,26},{10... | collective-permute-start | bytes 110600 | tf_op jit(solution)/shard_map/ppermute | solution.py:161
  41.1 1.2 %collective-permute-start.4 = (bf16[8,2304]{1,0:T(8,128)(2,1)S(1)}, bf16[8,2304]{1,0:T(8,128)(2,1)S(1)}, u32[]{:S(2)}, u32[]{:S(2)}) collective-permute-start(bf16[8,2304]{1,0:T(8,128)(2,1)S(1)} %shard_map.81.s0), channel_id=1, source_target_pairs={{0,16},{8,24},{16,0},{24,8},{1,17},{9,25},{17,1},{25,9},{2,18},{10... | collective-permute-start | bytes 110600 | tf_op jit(solution)/shard_map/ppermute | solution.py:161
  42.3 1.0 %collective-permute-start.3 = (bf16[8,2304]{1,0:T(8,128)(2,1)S(1)}, bf16[8,2304]{1,0:T(8,128)(2,1)S(1)}, u32[]{:S(2)}, u32[]{:S(2)}) collective-permute-start(bf16[8,2304]{1,0:T(8,128)(2,1)S(1)} %shard_map.81.s0), channel_id=1, source_target_pairs={{0,8},{8,0},{16,24},{24,16},{1,9},{9,1},{17,25},{25,17},{2,10},{10... | collective-permute-start | bytes 110600 | tf_op jit(solution)/shard_map/ppermute | solution.py:161
  43.3 0.0 collective-permute-done.5.s3
  43.3 5.7 %collective-permute-done.4.s2 = bf16[8,2304]{1,0:T(8,128)(2,1)S(1)} collective-permute-done((bf16[8,2304]{1,0:T(8,128)(2,1)S(1)}, bf16[8,2304]{1,0:T(8,128)(2,1)S(1)}, u32[]{:S(2)}, u32[]{:S(2)}) %collective-permute-start.4) | collective-permute-done | bytes 36896 | tf_op jit(solution)/shard_map/ppermute | solution.py:161
  49.0 0.0 collective-permute-done.3.s1
  49.1 0.0 copy-start.6
  49.1 0.8 %copy-done.6 = bf16[16,8,2304]{2,1,0:T(8,128)(2,1)} copy-done((bf16[16,8,2304]{2,1,0:T(8,128)(2,1)}, bf16[16,8,2304]{2,1,0:T(8,128)(2,1)S(1)}, u32[]{:S(2)}) %copy-start.6) | copy-done | bytes 589848
  49.9 4.3 %all-to-all-start.1 = ((bf16[16,8,2304]{2,1,0:T(8,128)(2,1)}), bf16[16,8,2304]{2,1,0:T(8,128)(2,1)}, u32[]{:S(2)}, u32[]{:S(2)}) async-start(bf16[16,8,2304]{2,1,0:T(8,128)(2,1)} %copy-done.6), calls=%async_computation.1 | async-start | bytes 1179648 | tf_op jit(solution)/shard_map/all_to_all | solution.py:242
  54.2 2.3 %copy-done.1 = bf16[4,2304,256]{2,1,0:T(8,128)(2,1)S(1)} copy-done((bf16[4,2304,256]{2,1,0:T(8,128)(2,1)S(1)}, bf16[4,2304,256]{2,1,0:T(8,128)(2,1)}, u32[]{:S(2)}) %copy-start.1) | copy-done | bytes 4718616
  56.5 1.3 %copy-done.5 = bf16[256,2304]{1,0:T(8,128)(2,1)S(1)} copy-done((bf16[256,2304]{1,0:T(8,128)(2,1)S(1)}, bf16[256,2304]{1,0:T(8,128)(2,1)}, u32[]{:S(2)}) %copy-start.5) | copy-done | bytes 1179672
  57.8 2.1 %copy-done.2 = bf16[4,2304,256]{2,1,0:T(8,128)(2,1)} copy-done((bf16[4,2304,256]{2,1,0:T(8,128)(2,1)}, bf16[4,2304,256]{2,1,0:T(8,128)(2,1)S(1)}, u32[]{:S(2)}) %copy-start.2) | copy-done | bytes 4718616
  59.9 4.7 %all-to-all-done.1 = bf16[16,8,2304]{2,1,0:T(8,128)(2,1)} async-done(((bf16[16,8,2304]{2,1,0:T(8,128)(2,1)}), bf16[16,8,2304]{2,1,0:T(8,128)(2,1)}, u32[]{:S(2)}, u32[]{:S(2)}) %all-to-all-start.1) | async-done | bytes 589856 | tf_op jit(solution)/shard_map/all_to_all | solution.py:242
  64.7 2.3 %copy-done.3 = bf16[4,2304,256]{2,1,0:T(8,128)(2,1)S(1)} copy-done((bf16[4,2304,256]{2,1,0:T(8,128)(2,1)S(1)}, bf16[4,2304,256]{2,1,0:T(8,128)(2,1)}, u32[]{:S(2)}) %copy-start.3) | copy-done | bytes 4718616
  67.0 0.8 copy-done.8
  67.7 1.5 %shard_map.88 = bf16[128,256]{1,0:T(8,128)(2,1)S(1)} custom-call(f32[4,8,256]{2,1,0:T(8,128)S(1)} %copy-done.8, bf16[128,2304]{1,0:T(8,128)(2,1)} %bitcast.5.err, bf16[4,2304,256]{2,1,0:T(8,128)(2,1)S(1)} %copy-done.3), custom_call_target="tpu_custom_call" | custom-call | flops 150994944 | tf_op jit(solution)/shard_map/pallas_call | solution.py:246
  69.3 0.0 slice-start.1
  69.3 2.8 %collective-permute-start.7 = (bf16[128,256]{1,0:T(8,128)(2,1)S(1)}, bf16[128,256]{1,0:T(8,128)(2,1)S(1)}, u32[]{:S(2)}, u32[]{:S(2)}) collective-permute-start(bf16[128,256]{1,0:T(8,128)(2,1)S(1)} %shard_map.88), channel_id=1, source_target_pairs={{0,1},{1,0},{2,3},{3,2},{4,5},{5,4},{6,7},{7,6},{8,9},{9,8},{10,11... | collective-permute-start | bytes 196616 | tf_op jit(solution)/shard_map/ppermute | solution.py:161
  72.1 1.4 %shard_map.86 = bf16[128,256]{1,0:T(8,128)(2,1)S(1)} custom-call(f32[4,8,256]{2,1,0:T(8,128)S(1)} %copy-done.9, bf16[128,2304]{1,0:T(8,128)(2,1)} %bitcast.5.err, bf16[4,2304,256]{2,1,0:T(8,128)(2,1)S(1)} %copy-done.3), custom_call_target="tpu_custom_call" | custom-call | flops 150994944 | tf_op jit(solution)/shard_map/pallas_call | solution.py:246
  73.5 0.1 collective-permute-start.6
  73.6 1.4 %shard_map.87.a = f32[128,256]{1,0:T(8,128)S(1)} custom-call(f32[4,8,256]{2,1,0:T(8,128)S(1)} %copy-done.9, bf16[128,2304]{1,0:T(8,128)(2,1)} %bitcast.5.err, bf16[4,2304,256]{2,1,0:T(8,128)(2,1)S(1)} %copy-done.3), custom_call_target="tpu_custom_call" | custom-call | flops 150994944 | tf_op jit(solution)/shard_map/pallas_call | solution.py:246
  75.0 0.0 collective-permute-done.7.b
  75.1 0.5 collective-permute-start.8
  75.5 1.7 %shard_map.83 = bf16[2,2304]{1,0:T(2,128)(2,1)} custom-call(bf16[128,2304]{1,0:T(8,128)(2,1)} %bitcast.5.err), custom_call_target="tpu_custom_call" | custom-call | tf_op jit(solution)/shard_map/pallas_call | solution.py:258
  77.3 1.4 %shard_map.85 = f32[128,256]{1,0:T(8,128)S(1)} custom-call(f32[4,8,256]{2,1,0:T(8,128)S(1)} %copy-done.9, bf16[128,2304]{1,0:T(8,128)(2,1)} %bitcast.5.err, bf16[4,2304,256]{2,1,0:T(8,128)(2,1)S(1)} %bitcast.10), custom_call_target="tpu_custom_call" | custom-call | flops 150994944 | tf_op jit(solution)/shard_map/pallas_call | solution.py:246
  78.7 0.0 collective-permute-done.6
  78.7 0.0 collective-permute-done.8
  78.7 0.7 fusion
  (14 shorter events, 0.1 us)
Async XLA Ops:
  2.5 10.1 %copy-start.4 = (bf16[256,2304]{1,0:T(8,128)(2,1)}, bf16[256,2304]{1,0:T(8,128)(2,1)S(1)}, u32[]{:S(2)}) copy-start(bf16[256,2304]{1,0:T(8,128)(2,1)S(1)} %get-tuple-element.10.mine) | copy-start | bytes 3538948
  2.5 3.9 %collective-permute-start.1 = (bf16[128,256]{1,0:T(8,128)(2,1)S(1)}, bf16[128,256]{1,0:T(8,128)(2,1)S(1)}, u32[]{:S(2)}, u32[]{:S(2)}) collective-permute-start(bf16[128,256]{1,0:T(8,128)(2,1)S(1)} %get-tuple-element.9.latent), channel_id=1, source_target_pairs={{0,2},{1,3},{2,0},{3,1},{4,6},{5,7},{6,4},{7,5},{8,10},{9,11},{10,... | collective-permute-start | bytes 196616 | tf_op jit(solution)/shard_map/ppermute | solution.py:161
  4.7 7.4 %collective-permute-start = (bf16[128,256]{1,0:T(8,128)(2,1)S(1)}, bf16[128,256]{1,0:T(8,128)(2,1)S(1)}, u32[]{:S(2)}, u32[]{:S(2)}) collective-permute-start(bf16[128,256]{1,0:T(8,128)(2,1)S(1)} %get-tuple-element.9.latent), channel_id=1, source_target_pairs={{0,1},{1,0},{2,3},{3,2},{4,5},{5,4},{6,7},{7,6},{8,9},{9,8},{10,11... | collective-permute-start | bytes 196616 | tf_op jit(solution)/shard_map/ppermute | solution.py:161
  6.4 6.2 %collective-permute-start.2 = (bf16[128,256]{1,0:T(8,128)(2,1)S(1)}, bf16[128,256]{1,0:T(8,128)(2,1)S(1)}, u32[]{:S(2)}, u32[]{:S(2)}) collective-permute-start(bf16[128,256]{1,0:T(8,128)(2,1)S(1)} %collective-permute-done.1.l2), channel_id=1, source_target_pairs={{0,1},{1,0},{2,3},{3,2},{4,5},{5,4},{6,7},{7,6},{8,9},{9,8},{10,11... | collective-permute-start | bytes 196616 | tf_op jit(solution)/shard_map/ppermute | solution.py:161
  12.1 2.4 %copy-start.7 = (f32[4,8,256]{2,1,0:T(8,128)}, f32[4,8,256]{2,1,0:T(8,128)S(1)}, u32[]{:S(2)}) copy-start(f32[4,8,256]{2,1,0:T(8,128)S(1)} %get-tuple-element.11.keep) | copy-start | bytes 98308
  12.1 0.7 copy-start.10
  14.5 2.2 %copy-start = (bf16[4,2304,256]{2,1,0:T(8,128)(2,1)}, bf16[4,2304,256]{2,1,0:T(8,128)(2,1)S(1)}, u32[]{:S(2)}) copy-start(bf16[4,2304,256]{2,1,0:T(8,128)(2,1)S(1)} %get-tuple-element.15.early) | copy-start | bytes 14155780
  35.9 7.4 %collective-permute-start.5 = (bf16[8,2304]{1,0:T(8,128)(2,1)S(1)}, bf16[8,2304]{1,0:T(8,128)(2,1)S(1)}, u32[]{:S(2)}, u32[]{:S(2)}) collective-permute-start(bf16[8,2304]{1,0:T(8,128)(2,1)S(1)} %shard_map.81.s0), channel_id=1, source_target_pairs={{0,24},{8,16},{16,8},{24,0},{1,25},{9,17},{17,9},{25,1},{2,26},{10... | collective-permute-start | bytes 110600 | tf_op jit(solution)/shard_map/ppermute | solution.py:161
  41.1 7.9 %collective-permute-start.4 = (bf16[8,2304]{1,0:T(8,128)(2,1)S(1)}, bf16[8,2304]{1,0:T(8,128)(2,1)S(1)}, u32[]{:S(2)}, u32[]{:S(2)}) collective-permute-start(bf16[8,2304]{1,0:T(8,128)(2,1)S(1)} %shard_map.81.s0), channel_id=1, source_target_pairs={{0,16},{8,24},{16,0},{24,8},{1,17},{9,25},{17,1},{25,9},{2,18},{10... | collective-permute-start | bytes 110600 | tf_op jit(solution)/shard_map/ppermute | solution.py:161
  42.3 6.8 %collective-permute-start.3 = (bf16[8,2304]{1,0:T(8,128)(2,1)S(1)}, bf16[8,2304]{1,0:T(8,128)(2,1)S(1)}, u32[]{:S(2)}, u32[]{:S(2)}) collective-permute-start(bf16[8,2304]{1,0:T(8,128)(2,1)S(1)} %shard_map.81.s0), channel_id=1, source_target_pairs={{0,8},{8,0},{16,24},{24,16},{1,9},{9,1},{17,25},{25,17},{2,10},{10... | collective-permute-start | bytes 110600 | tf_op jit(solution)/shard_map/ppermute | solution.py:161
  49.1 0.8 %copy-start.6 = (bf16[16,8,2304]{2,1,0:T(8,128)(2,1)}, bf16[16,8,2304]{2,1,0:T(8,128)(2,1)S(1)}, u32[]{:S(2)}) copy-start(bf16[16,8,2304]{2,1,0:T(8,128)(2,1)S(1)} %shard_map.82) | copy-start | bytes 1769476
  49.9 14.7 %all-to-all-start.1 = ((bf16[16,8,2304]{2,1,0:T(8,128)(2,1)}), bf16[16,8,2304]{2,1,0:T(8,128)(2,1)}, u32[]{:S(2)}, u32[]{:S(2)}) async-start(bf16[16,8,2304]{2,1,0:T(8,128)(2,1)} %copy-done.6), calls=%async_computation.1 | async-start | bytes 1179648 | tf_op jit(solution)/shard_map/all_to_all | solution.py:242
  54.2 2.3 %copy-start.1 = (bf16[4,2304,256]{2,1,0:T(8,128)(2,1)S(1)}, bf16[4,2304,256]{2,1,0:T(8,128)(2,1)}, u32[]{:S(2)}) copy-start(bf16[4,2304,256]{2,1,0:T(8,128)(2,1)} %copy-done) | copy-start | bytes 14155780
  56.5 1.3 %copy-start.5 = (bf16[256,2304]{1,0:T(8,128)(2,1)S(1)}, bf16[256,2304]{1,0:T(8,128)(2,1)}, u32[]{:S(2)}) copy-start(bf16[256,2304]{1,0:T(8,128)(2,1)} %copy-done.4) | copy-start | bytes 3538948
  57.8 2.2 %copy-start.2 = (bf16[4,2304,256]{2,1,0:T(8,128)(2,1)}, bf16[4,2304,256]{2,1,0:T(8,128)(2,1)S(1)}, u32[]{:S(2)}) copy-start(bf16[4,2304,256]{2,1,0:T(8,128)(2,1)S(1)} %shard_map.84.turned) | copy-start | bytes 14155780
  64.6 2.3 %copy-start.3 = (bf16[4,2304,256]{2,1,0:T(8,128)(2,1)S(1)}, bf16[4,2304,256]{2,1,0:T(8,128)(2,1)}, u32[]{:S(2)}) copy-start(bf16[4,2304,256]{2,1,0:T(8,128)(2,1)} %copy-done.2) | copy-start | bytes 14155780
  67.0 0.8 copy-start.8
  67.7 4.3 %copy-start.9 = (f32[4,8,256]{2,1,0:T(8,128)S(1)}, f32[4,8,256]{2,1,0:T(8,128)}, u32[]{:S(2)}) copy-start(f32[4,8,256]{2,1,0:T(8,128)} %copy-done.7) | copy-start | bytes 98308
  67.7 9.5 %slice-start = ((s8[4718592]{0:T(1024)(128)(4,1)}), s8[4194304]{0:T(1024)(128)(4,1)S(1)}, s32[]{:S(2)}) async-start(s8[4718592]{0:T(1024)(128)(4,1)} %bitcast.9), calls=%async_computation.2 | async-start | bytes 8388608
  69.3 8.0 %slice-start.1 = ((s8[4718592]{0:T(1024)(128)(4,1)}), s8[524288]{0:T(1024)(128)(4,1)S(1)}, s32[]{:S(2)}) async-start(s8[4718592]{0:T(1024)(128)(4,1)} %bitcast.9), calls=%async_computation.3 | async-start | bytes 1048576
  69.3 5.7 %collective-permute-start.7 = (bf16[128,256]{1,0:T(8,128)(2,1)S(1)}, bf16[128,256]{1,0:T(8,128)(2,1)S(1)}, u32[]{:S(2)}, u32[]{:S(2)}) collective-permute-start(bf16[128,256]{1,0:T(8,128)(2,1)S(1)} %shard_map.88), channel_id=1, source_target_pairs={{0,1},{1,0},{2,3},{3,2},{4,5},{5,4},{6,7},{7,6},{8,9},{9,8},{10,11... | collective-permute-start | bytes 196616 | tf_op jit(solution)/shard_map/ppermute | solution.py:161
  73.5 5.2 %collective-permute-start.6 = (bf16[128,256]{1,0:T(8,128)(2,1)S(1)}, bf16[128,256]{1,0:T(8,128)(2,1)S(1)}, u32[]{:S(2)}, u32[]{:S(2)}) collective-permute-start(bf16[128,256]{1,0:T(8,128)(2,1)S(1)} %shard_map.86), channel_id=1, source_target_pairs={{0,1},{1,0},{2,3},{3,2},{4,5},{5,4},{6,7},{7,6},{8,9},{9,8},{10,11... | collective-permute-start | bytes 196616 | tf_op jit(solution)/shard_map/ppermute | solution.py:161
  75.1 3.6 %collective-permute-start.8 = (bf16[128,256]{1,0:T(8,128)(2,1)S(1)}, bf16[128,256]{1,0:T(8,128)(2,1)S(1)}, u32[]{:S(2)}, u32[]{:S(2)}) collective-permute-start(bf16[128,256]{1,0:T(8,128)(2,1)S(1)} %shard_map.89), channel_id=1, source_target_pairs={{0,2},{1,3},{2,0},{3,1},{4,6},{5,7},{6,4},{7,5},{8,10},{9,11},{10,... | collective-permute-start | bytes 196616 | tf_op jit(solution)/shard_map/ppermute | solution.py:161

commit v12 on v10

--- a/solution.py
+++ b/solution.py
@@ -77,31 +77,31 @@
         copy.wait()
 
 
-def decode_pair_kernel(keep, own, l1, l2, dec, out):
+def decode_pair_kernel(keep, own, l1, l2, targets, dec, out):
+    base = spot_of() * targets.shape[0]
+    tok, width = out.shape
     step = 256
     rows = []
     for flip, ref in ((1, l1), (2, l2)):
         rows.append((flip - 1, ref[...] * keep[flip, 0:1, :].astype(BF)))
-    for start in range(0, out.shape[1], step):
+    row_ids = lax.broadcasted_iota(jnp.int32, (tok, 1), 0)
+    for start in range(0, width, step):
         cols = pl.ds(start, step)
         total = own[:, cols]
         for slab, latent in rows:
             total = total + jnp.dot(latent, dec[slab, :, cols], **DOT)
-        out[:, cols] = total
-
-
-def decode_last_kernel(keep, most, l3, targets, dec, out):
-    base = spot_of() * targets.shape[0]
-    tok, width = out.shape
-    step = 256
-    latent = l3[...] * keep[3, 0:1, :].astype(BF)
-    row_ids = lax.broadcasted_iota(jnp.int32, (tok, 1), 0)
-    for start in range(0, width, step):
-        cols = pl.ds(start, step)
-        total = most[:, cols] + jnp.dot(latent, dec[2, :, cols], **DOT)
         for r in range(targets.shape[0]):
             line = targets[r : r + 1, cols].astype(F32)
             total = total - jnp.where(row_ids == base + r, line, 0.0)
+        out[:, cols] = total
+
+
+def decode_last_kernel(keep, most, l3, dec, out):
+    step = 256
+    latent = l3[...] * keep[3, 0:1, :].astype(BF)
+    for start in range(0, out.shape[1], step):
+        cols = pl.ds(start, step)
+        total = most[:, cols] + jnp.dot(latent, dec[2, :, cols], **DOT)
         out[:, cols] = total.astype(BF)
 
 
@@ -208,11 +208,11 @@
     )
     dec, own, keep = load(in_hbm(pair_mask), latent, mine, slabs)
     l3 = swap(l2, "tgt", 1)
-    most = call(decode_pair_kernel, shape((tok, width), F32), [VMEM] * 5, 2 * flops)(
-        keep, own, l1, l2, dec
-    )
-    shares = call(decode_last_kernel, shape((tok, width), BF), [VMEM] * 5, flops)(
-        keep, most, l3, targets[0], dec
+    most = call(decode_pair_kernel, shape((tok, width), F32), [VMEM] * 6, 2 * flops)(
+        keep, own, l1, l2, targets[0], dec
+    )
+    shares = call(decode_last_kernel, shape((tok, width), BF), [VMEM] * 4, flops)(
+        keep, most, l3, dec
     )
 
     shares = shares.reshape(GROUP, rows, width)

time: 75.5 us -> 75.3 us (level)
  no operation moved by 1% of the time
where the time goes in v12:
time: 75.3 us; the launch traced here: 74.6 us
  starting transfers between devices  23.2 us (31%)
  blocking collectives  18.7 us (25%)
  Pallas kernels  13.4 us (18%)
  waiting for transfers between devices  10.4 us (14%)
  local copies, waits for them, and re-layouts  7.37 us (10%)
  between operations  0.84 us (1%)
    ppermute x9, starting transfers between devices, swap(): return lax.ppermute(value, name, [(i, i ^ flip) for i in range(size)])  18.9 us
    all_to_all x1, blocking collectives, per_device(): shares = lax.all_to_all(shares, NEAR, 0, 0, tiled=True)  18.7 us
    unnamed x18, local copies, waits for them, and re-layouts  7.37 us
    ppermute x9, waiting for transfers between devices, swap(): return lax.ppermute(value, name, [(i, i ^ flip) for i in range(size)])  5.72 us
    pallas_call x4, Pallas kernels, term(): call(kernel, shape((tok, feats), kind), [VMEM] * 3, flops)  5.55 us
    all_to_all x1, waiting for transfers between devices, per_device(): lax.all_to_all(copies, NEAR, 0, 0, tiled=True).reshape(tok, width)  4.72 us
    all_to_all x1, starting transfers between devices, per_device(): lax.all_to_all(copies, NEAR, 0, 0, tiled=True).reshape(tok, width)  4.24 us
    pallas_call x1, Pallas kernels, per_device(): dec, own, keep = load(in_hbm(pair_mask), latent, mine, slabs)  2.03 us
  transfers between devices with their start and end apart: 10, of which 3 were waited for; matrix products, arithmetic and copies ran while one was open for 0% of the time, Pallas kernels for 13%

profile of v12, /device:TPU:1, one launch (start us, length us, event | category | flops | bytes accessed | tf_op | source)
XLA Modules:
  0.0 74.6 jit_solution(12231724786273361538)
XLA Ops:
  0.6 1.9 %shard_map.77 = (bf16[128,256]{1,0:T(8,128)(2,1)S(1)}, bf16[256,2304]{1,0:T(8,128)(2,1)S(1)}) custom-call(bf16[128,2304]{1,0:T(8,128)(2,1)} %bitcast.14, bf16[2304,256]{1,0:T(8,128)(2,1)} %bitcast.13, f32[1,256]{1,0:T(1,128)} %bias.1, bf16[4,256,2304]{2,1,0:T(8,128)(2,1)} %bitcast.11), custom_call_target="tpu_custom_call" | custom-call | flops 150994944 | bytes 1179648 | tf_op jit(solution)/shard_map/pallas_call | solution.py:179
  2.5 0.0 copy-start.2
  2.5 2.2 %collective-permute-start.1 = (bf16[128,256]{1,0:T(8,128)(2,1)S(1)}, bf16[128,256]{1,0:T(8,128)(2,1)S(1)}, u32[]{:S(2)}, u32[]{:S(2)}) collective-permute-start(bf16[128,256]{1,0:T(8,128)(2,1)S(1)} %get-tuple-element.7.latent), channel_id=1, source_target_pairs={{0,2},{1,3},{2,0},{3,1},{4,6},{5,7},{6,4},{7,5},{8,10},{9,11},{10,... | collective-permute-start | bytes 196616 | tf_op jit(solution)/shard_map/ppermute | solution.py:151
  4.7 1.2 %collective-permute-start = (bf16[128,256]{1,0:T(8,128)(2,1)S(1)}, bf16[128,256]{1,0:T(8,128)(2,1)S(1)}, u32[]{:S(2)}, u32[]{:S(2)}) collective-permute-start(bf16[128,256]{1,0:T(8,128)(2,1)S(1)} %get-tuple-element.7.latent), channel_id=1, source_target_pairs={{0,1},{1,0},{2,3},{3,2},{4,5},{5,4},{6,7},{7,6},{8,9},{9,8},{10,11... | collective-permute-start | bytes 196616 | tf_op jit(solution)/shard_map/ppermute | solution.py:151
  5.9 0.5 collective-permute-done.1.l2
  6.4 3.7 %collective-permute-start.2 = (bf16[128,256]{1,0:T(8,128)(2,1)S(1)}, bf16[128,256]{1,0:T(8,128)(2,1)S(1)}, u32[]{:S(2)}, u32[]{:S(2)}) collective-permute-start(bf16[128,256]{1,0:T(8,128)(2,1)S(1)} %collective-permute-done.1.l2), channel_id=1, source_target_pairs={{0,1},{1,0},{2,3},{3,2},{4,5},{5,4},{6,7},{7,6},{8,9},{9,8},{10,11... | collective-permute-start | bytes 196616 | tf_op jit(solution)/shard_map/ppermute | solution.py:151
  10.1 2.0 %shard_map.78 = (bf16[3,256,2304]{2,1,0:T(8,128)(2,1)S(1)}, f32[128,2304]{1,0:T(8,128)S(1)}, f32[4,8,256]{2,1,0:T(8,128)S(1)}) custom-call(s32[4,4]{1,0:T(4,128)} %mask.1, bf16[128,256]{1,0:T(8,128)(2,1)S(1)} %get-tuple-element.7.latent, bf16[256,2304]{1,0:T(8,128)(2,1)S(1)} %get-tuple-element.8.mine, bf16[4,256,2304]{2,1,0:T(8,128)(2,1)} %bitcast.12), custom_call_target="tpu_custom_call" | custom-call | flops 150994944 | bytes 4718592 | tf_op jit(solution)/shard_map/pallas_call | solution.py:209
  12.1 0.0 copy-done.2
  12.1 0.0 copy-start.5
  12.1 0.0 collective-permute-done.l1
  12.2 0.0 copy-done.8
  12.2 0.5 shard_map.79.most
  12.7 0.0 collective-permute-done.2.l3
  12.7 0.0 copy-done.5
  12.8 0.3 shard_map.80
  13.1 18.7 %all_to_all.10.shares = bf16[16,8,2304]{2,1,0:T(8,128)(2,1)S(1)} all-to-all(bf16[16,8,2304]{2,1,0:T(8,128)(2,1)S(1)} %bitcast.9), channel_id=1, replica_groups=mesh['x'=4,'yh'=2,'zh'=4,'zl'=2,'tgt'=4] {'x','yh','zl'}, dimensions={0} | all-to-all | bytes 1179648 | tf_op jit(solution)/shard_map/all_to_all | solution.py:219
  31.8 0.1 shard_map.81.s0
  31.9 5.2 %collective-permute-start.5 = (bf16[8,2304]{1,0:T(8,128)(2,1)S(1)}, bf16[8,2304]{1,0:T(8,128)(2,1)S(1)}, u32[]{:S(2)}, u32[]{:S(2)}) collective-permute-start(bf16[8,2304]{1,0:T(8,128)(2,1)S(1)} %shard_map.81.s0), channel_id=1, source_target_pairs={{0,24},{8,16},{16,8},{24,0},{1,25},{9,17},{17,9},{25,1},{2,26},{10... | collective-permute-start | bytes 110600 | tf_op jit(solution)/shard_map/ppermute | solution.py:151
  37.1 1.2 %collective-permute-start.4 = (bf16[8,2304]{1,0:T(8,128)(2,1)S(1)}, bf16[8,2304]{1,0:T(8,128)(2,1)S(1)}, u32[]{:S(2)}, u32[]{:S(2)}) collective-permute-start(bf16[8,2304]{1,0:T(8,128)(2,1)S(1)} %shard_map.81.s0), channel_id=1, source_target_pairs={{0,16},{8,24},{16,0},{24,8},{1,17},{9,25},{17,1},{25,9},{2,18},{10... | collective-permute-start | bytes 110600 | tf_op jit(solution)/shard_map/ppermute | solution.py:151
  38.3 1.0 %collective-permute-start.3 = (bf16[8,2304]{1,0:T(8,128)(2,1)S(1)}, bf16[8,2304]{1,0:T(8,128)(2,1)S(1)}, u32[]{:S(2)}, u32[]{:S(2)}) collective-permute-start(bf16[8,2304]{1,0:T(8,128)(2,1)S(1)} %shard_map.81.s0), channel_id=1, source_target_pairs={{0,8},{8,0},{16,24},{24,16},{1,9},{9,1},{17,25},{25,17},{2,10},{10... | collective-permute-start | bytes 110600 | tf_op jit(solution)/shard_map/ppermute | solution.py:151
  39.3 0.0 collective-permute-done.5.s3
  39.3 5.2 %collective-permute-done.4.s2 = bf16[8,2304]{1,0:T(8,128)(2,1)S(1)} collective-permute-done((bf16[8,2304]{1,0:T(8,128)(2,1)S(1)}, bf16[8,2304]{1,0:T(8,128)(2,1)S(1)}, u32[]{:S(2)}, u32[]{:S(2)}) %collective-permute-start.4) | collective-permute-done | bytes 36896 | tf_op jit(solution)/shard_map/ppermute | solution.py:151
  44.5 0.0 collective-permute-done.3.s1
  44.6 0.0 copy-start.4
  44.6 0.8 %copy-done.4 = bf16[16,8,2304]{2,1,0:T(8,128)(2,1)} copy-done((bf16[16,8,2304]{2,1,0:T(8,128)(2,1)}, bf16[16,8,2304]{2,1,0:T(8,128)(2,1)S(1)}, u32[]{:S(2)}) %copy-start.4) | copy-done | bytes 589848
  45.4 4.2 %all-to-all-start.1 = ((bf16[16,8,2304]{2,1,0:T(8,128)(2,1)}), bf16[16,8,2304]{2,1,0:T(8,128)(2,1)}, u32[]{:S(2)}, u32[]{:S(2)}) async-start(bf16[16,8,2304]{2,1,0:T(8,128)(2,1)} %copy-done.4), calls=%async_computation.1 | async-start | bytes 1179648 | tf_op jit(solution)/shard_map/all_to_all | solution.py:226
  49.7 0.0 copy-start.3
  49.7 1.3 %copy-done.3 = bf16[256,2304]{1,0:T(8,128)(2,1)S(1)} copy-done((bf16[256,2304]{1,0:T(8,128)(2,1)S(1)}, bf16[256,2304]{1,0:T(8,128)(2,1)}, u32[]{:S(2)}) %copy-start.3) | copy-done | bytes 1179672
  50.9 1.3 %shard_map.84.turned = bf16[4,2304,256]{2,1,0:T(8,128)(2,1)S(1)} custom-call(bf16[256,2304]{1,0:T(8,128)(2,1)S(1)} %copy-done.3, bf16[3,256,2304]{2,1,0:T(8,128)(2,1)S(1)} %get-tuple-element.11.dec), custom_call_target="tpu_custom_call" | custom-call | tf_op jit(solution)/shard_map/pallas_call | solution.py:224
  52.2 0.0 copy-start
  52.2 2.1 %copy-done = bf16[4,2304,256]{2,1,0:T(8,128)(2,1)} copy-done((bf16[4,2304,256]{2,1,0:T(8,128)(2,1)}, bf16[4,2304,256]{2,1,0:T(8,128)(2,1)S(1)}, u32[]{:S(2)}) %copy-start) | copy-done | bytes 4718616
  54.3 4.7 %all-to-all-done.1 = bf16[16,8,2304]{2,1,0:T(8,128)(2,1)} async-done(((bf16[16,8,2304]{2,1,0:T(8,128)(2,1)}), bf16[16,8,2304]{2,1,0:T(8,128)(2,1)}, u32[]{:S(2)}, u32[]{:S(2)}) %all-to-all-start.1) | async-done | bytes 589856 | tf_op jit(solution)/shard_map/all_to_all | solution.py:226
  59.0 2.3 %copy-done.1 = bf16[4,2304,256]{2,1,0:T(8,128)(2,1)S(1)} copy-done((bf16[4,2304,256]{2,1,0:T(8,128)(2,1)S(1)}, bf16[4,2304,256]{2,1,0:T(8,128)(2,1)}, u32[]{:S(2)}) %copy-start.1) | copy-done | bytes 4718616
  61.4 0.8 %copy-done.6 = f32[4,8,256]{2,1,0:T(8,128)S(1)} copy-done((f32[4,8,256]{2,1,0:T(8,128)S(1)}, f32[4,8,256]{2,1,0:T(8,128)}, u32[]{:S(2)}) %copy-start.6) | copy-done | bytes 32792
  62.1 1.4 %shard_map.88 = bf16[128,256]{1,0:T(8,128)(2,1)S(1)} custom-call(f32[4,8,256]{2,1,0:T(8,128)S(1)} %copy-done.6, bf16[128,2304]{1,0:T(8,128)(2,1)} %bitcast.5.err, bf16[4,2304,256]{2,1,0:T(8,128)(2,1)S(1)} %copy-done.1), custom_call_target="tpu_custom_call" | custom-call | flops 150994944 | tf_op jit(solution)/shard_map/pallas_call | solution.py:230
  63.5 0.0 copy-start.7
  63.5 3.9 %collective-permute-start.7 = (bf16[128,256]{1,0:T(8,128)(2,1)S(1)}, bf16[128,256]{1,0:T(8,128)(2,1)S(1)}, u32[]{:S(2)}, u32[]{:S(2)}) collective-permute-start(bf16[128,256]{1,0:T(8,128)(2,1)S(1)} %shard_map.88), channel_id=1, source_target_pairs={{0,1},{1,0},{2,3},{3,2},{4,5},{5,4},{6,7},{7,6},{8,9},{9,8},{10,11... | collective-permute-start | bytes 196616 | tf_op jit(solution)/shard_map/ppermute | solution.py:151
  67.4 1.4 %shard_map.86 = bf16[128,256]{1,0:T(8,128)(2,1)S(1)} custom-call(f32[4,8,256]{2,1,0:T(8,128)S(1)} %copy-done.6, bf16[128,2304]{1,0:T(8,128)(2,1)} %bitcast.5.err, bf16[4,2304,256]{2,1,0:T(8,128)(2,1)S(1)} %copy-done.1), custom_call_target="tpu_custom_call" | custom-call | flops 150994944 | tf_op jit(solution)/shard_map/pallas_call | solution.py:230
  68.8 0.1 collective-permute-start.6
  68.9 0.0 copy-done.7
  68.9 1.4 %shard_map.87.a = f32[128,256]{1,0:T(8,128)S(1)} custom-call(f32[4,8,256]{2,1,0:T(8,128)S(1)} %copy-done.7, bf16[128,2304]{1,0:T(8,128)(2,1)} %bitcast.5.err, bf16[4,2304,256]{2,1,0:T(8,128)(2,1)S(1)} %copy-done.1), custom_call_target="tpu_custom_call" | custom-call | flops 150994944 | tf_op jit(solution)/shard_map/pallas_call | solution.py:230
  70.3 0.0 collective-permute-done.7.b
  70.3 0.5 collective-permute-start.8
  70.8 1.7 %shard_map.83 = bf16[2,2304]{1,0:T(2,128)(2,1)} custom-call(bf16[128,2304]{1,0:T(8,128)(2,1)} %bitcast.5.err), custom_call_target="tpu_custom_call" | custom-call | tf_op jit(solution)/shard_map/pallas_call | solution.py:242
  72.6 1.4 %shard_map.85 = f32[128,256]{1,0:T(8,128)S(1)} custom-call(f32[4,8,256]{2,1,0:T(8,128)S(1)} %copy-done.7, bf16[128,2304]{1,0:T(8,128)(2,1)} %bitcast.5.err, bf16[4,2304,256]{2,1,0:T(8,128)(2,1)S(1)} %copy-done.1), custom_call_target="tpu_custom_call" | custom-call | flops 150994944 | tf_op jit(solution)/shard_map/pallas_call | solution.py:230
  74.0 0.0 collective-permute-done.6
  74.0 0.0 collective-permute-done.8
  74.0 0.7 fusion
  (5 shorter events, 0.1 us)
Async XLA Ops:
  2.5 9.6 %copy-start.2 = (bf16[256,2304]{1,0:T(8,128)(2,1)}, bf16[256,2304]{1,0:T(8,128)(2,1)S(1)}, u32[]{:S(2)}) copy-start(bf16[256,2304]{1,0:T(8,128)(2,1)S(1)} %get-tuple-element.8.mine) | copy-start | bytes 3538948
  2.5 3.9 %collective-permute-start.1 = (bf16[128,256]{1,0:T(8,128)(2,1)S(1)}, bf16[128,256]{1,0:T(8,128)(2,1)S(1)}, u32[]{:S(2)}, u32[]{:S(2)}) collective-permute-start(bf16[128,256]{1,0:T(8,128)(2,1)S(1)} %get-tuple-element.7.latent), channel_id=1, source_target_pairs={{0,2},{1,3},{2,0},{3,1},{4,6},{5,7},{6,4},{7,5},{8,10},{9,11},{10,... | collective-permute-start | bytes 196616 | tf_op jit(solution)/shard_map/ppermute | solution.py:151
  4.7 7.4 %collective-permute-start = (bf16[128,256]{1,0:T(8,128)(2,1)S(1)}, bf16[128,256]{1,0:T(8,128)(2,1)S(1)}, u32[]{:S(2)}, u32[]{:S(2)}) collective-permute-start(bf16[128,256]{1,0:T(8,128)(2,1)S(1)} %get-tuple-element.7.latent), channel_id=1, source_target_pairs={{0,1},{1,0},{2,3},{3,2},{4,5},{5,4},{6,7},{7,6},{8,9},{9,8},{10,11... | collective-permute-start | bytes 196616 | tf_op jit(solution)/shard_map/ppermute | solution.py:151
  6.4 6.3 %collective-permute-start.2 = (bf16[128,256]{1,0:T(8,128)(2,1)S(1)}, bf16[128,256]{1,0:T(8,128)(2,1)S(1)}, u32[]{:S(2)}, u32[]{:S(2)}) collective-permute-start(bf16[128,256]{1,0:T(8,128)(2,1)S(1)} %collective-permute-done.1.l2), channel_id=1, source_target_pairs={{0,1},{1,0},{2,3},{3,2},{4,5},{5,4},{6,7},{7,6},{8,9},{9,8},{10,11... | collective-permute-start | bytes 196616 | tf_op jit(solution)/shard_map/ppermute | solution.py:151
  10.1 2.1 %copy-start.8 = (bf16[1,2,2304]{2,1,0:T(2,128)(2,1)S(1)}, bf16[1,2,2304]{2,1,0:T(2,128)(2,1)}, u32[]{:S(2)}) copy-start(bf16[1,2,2304]{2,1,0:T(2,128)(2,1)} %param.7) | copy-start | bytes 27652
  12.1 0.6 copy-start.5
  31.9 7.4 %collective-permute-start.5 = (bf16[8,2304]{1,0:T(8,128)(2,1)S(1)}, bf16[8,2304]{1,0:T(8,128)(2,1)S(1)}, u32[]{:S(2)}, u32[]{:S(2)}) collective-permute-start(bf16[8,2304]{1,0:T(8,128)(2,1)S(1)} %shard_map.81.s0), channel_id=1, source_target_pairs={{0,24},{8,16},{16,8},{24,0},{1,25},{9,17},{17,9},{25,1},{2,26},{10... | collective-permute-start | bytes 110600 | tf_op jit(solution)/shard_map/ppermute | solution.py:151
  37.1 7.4 %collective-permute-start.4 = (bf16[8,2304]{1,0:T(8,128)(2,1)S(1)}, bf16[8,2304]{1,0:T(8,128)(2,1)S(1)}, u32[]{:S(2)}, u32[]{:S(2)}) collective-permute-start(bf16[8,2304]{1,0:T(8,128)(2,1)S(1)} %shard_map.81.s0), channel_id=1, source_target_pairs={{0,16},{8,24},{16,0},{24,8},{1,17},{9,25},{17,1},{25,9},{2,18},{10... | collective-permute-start | bytes 110600 | tf_op jit(solution)/shard_map/ppermute | solution.py:151
  38.3 6.3 %collective-permute-start.3 = (bf16[8,2304]{1,0:T(8,128)(2,1)S(1)}, bf16[8,2304]{1,0:T(8,128)(2,1)S(1)}, u32[]{:S(2)}, u32[]{:S(2)}) collective-permute-start(bf16[8,2304]{1,0:T(8,128)(2,1)S(1)} %shard_map.81.s0), channel_id=1, source_target_pairs={{0,8},{8,0},{16,24},{24,16},{1,9},{9,1},{17,25},{25,17},{2,10},{10... | collective-permute-start | bytes 110600 | tf_op jit(solution)/shard_map/ppermute | solution.py:151
  44.6 0.8 %copy-start.4 = (bf16[16,8,2304]{2,1,0:T(8,128)(2,1)}, bf16[16,8,2304]{2,1,0:T(8,128)(2,1)S(1)}, u32[]{:S(2)}) copy-start(bf16[16,8,2304]{2,1,0:T(8,128)(2,1)S(1)} %shard_map.82) | copy-start | bytes 1769476
  45.4 13.6 %all-to-all-start.1 = ((bf16[16,8,2304]{2,1,0:T(8,128)(2,1)}), bf16[16,8,2304]{2,1,0:T(8,128)(2,1)}, u32[]{:S(2)}, u32[]{:S(2)}) async-start(bf16[16,8,2304]{2,1,0:T(8,128)(2,1)} %copy-done.4), calls=%async_computation.1 | async-start | bytes 1179648 | tf_op jit(solution)/shard_map/all_to_all | solution.py:226
  49.7 1.3 %copy-start.3 = (bf16[256,2304]{1,0:T(8,128)(2,1)S(1)}, bf16[256,2304]{1,0:T(8,128)(2,1)}, u32[]{:S(2)}) copy-start(bf16[256,2304]{1,0:T(8,128)(2,1)} %copy-done.2) | copy-start | bytes 3538948
  52.2 2.1 %copy-start = (bf16[4,2304,256]{2,1,0:T(8,128)(2,1)}, bf16[4,2304,256]{2,1,0:T(8,128)(2,1)S(1)}, u32[]{:S(2)}) copy-start(bf16[4,2304,256]{2,1,0:T(8,128)(2,1)S(1)} %shard_map.84.turned) | copy-start | bytes 14155780
  59.0 2.3 %copy-start.1 = (bf16[4,2304,256]{2,1,0:T(8,128)(2,1)S(1)}, bf16[4,2304,256]{2,1,0:T(8,128)(2,1)}, u32[]{:S(2)}) copy-start(bf16[4,2304,256]{2,1,0:T(8,128)(2,1)} %copy-done) | copy-start | bytes 14155780
  61.4 0.8 %copy-start.6 = (f32[4,8,256]{2,1,0:T(8,128)S(1)}, f32[4,8,256]{2,1,0:T(8,128)}, u32[]{:S(2)}) copy-start(f32[4,8,256]{2,1,0:T(8,128)} %copy-done.5) | copy-start | bytes 98308
  63.5 5.4 %copy-start.7 = (f32[4,8,256]{2,1,0:T(8,128)S(1)}, f32[4,8,256]{2,1,0:T(8,128)}, u32[]{:S(2)}) copy-start(f32[4,8,256]{2,1,0:T(8,128)} %copy-done.5) | copy-start | bytes 98308
  63.5 6.8 %collective-permute-start.7 = (bf16[128,256]{1,0:T(8,128)(2,1)S(1)}, bf16[128,256]{1,0:T(8,128)(2,1)S(1)}, u32[]{:S(2)}, u32[]{:S(2)}) collective-permute-start(bf16[128,256]{1,0:T(8,128)(2,1)S(1)} %shard_map.88), channel_id=1, source_target_pairs={{0,1},{1,0},{2,3},{3,2},{4,5},{5,4},{6,7},{7,6},{8,9},{9,8},{10,11... | collective-permute-start | bytes 196616 | tf_op jit(solution)/shard_map/ppermute | solution.py:151
  68.8 5.2 %collective-permute-start.6 = (bf16[128,256]{1,0:T(8,128)(2,1)S(1)}, bf16[128,256]{1,0:T(8,128)(2,1)S(1)}, u32[]{:S(2)}, u32[]{:S(2)}) collective-permute-start(bf16[128,256]{1,0:T(8,128)(2,1)S(1)} %shard_map.86), channel_id=1, source_target_pairs={{0,1},{1,0},{2,3},{3,2},{4,5},{5,4},{6,7},{7,6},{8,9},{9,8},{10,11... | collective-permute-start | bytes 196616 | tf_op jit(solution)/shard_map/ppermute | solution.py:151
  70.3 3.6 %collective-permute-start.8 = (bf16[128,256]{1,0:T(8,128)(2,1)S(1)}, bf16[128,256]{1,0:T(8,128)(2,1)S(1)}, u32[]{:S(2)}, u32[]{:S(2)}) collective-permute-start(bf16[128,256]{1,0:T(8,128)(2,1)S(1)} %shard_map.89), channel_id=1, source_target_pairs={{0,2},{1,3},{2,0},{3,1},{4,6},{5,7},{6,4},{7,5},{8,10},{9,11},{10,... | collective-permute-start | bytes 196616 | tf_op jit(solution)/shard_map/ppermute | solution.py:151

commit v13 on v12

--- a/solution.py
+++ b/solution.py
@@ -109,12 +109,14 @@
     total = shares[0].astype(F32)
     for i in range(1, shares.shape[0]):
         total = total + shares[i].astype(F32)
-    out[...] = total.astype(out.dtype)
-
-
-def spread_kernel(s0, s1, s2, s3, out):
-    total = (s0[...].astype(F32) + s1[...].astype(F32)) + (
-        s2[...].astype(F32) + s3[...].astype(F32)
+    value = total.astype(out.dtype)
+    for i in range(out.shape[0]):
+        out[i] = value
+
+
+def spread_kernel(parts, out):
+    total = (parts[0].astype(F32) + parts[1].astype(F32)) + (
+        parts[2].astype(F32) + parts[3].astype(F32)
     )
     err = total.astype(BF)
     for i in range(out.shape[0]):
@@ -125,14 +127,9 @@
     out[...] = (a[...] + b[...].astype(F32)).astype(out.dtype)
 
 
-def turn_kernel(mine, dec, out):
-    out[0] = mine[...].T
-    for flip in FLIPS:
-        out[flip] = dec[flip - 1].T
-
-
-def term_kernel(flip, keep, err, turned, out):
-    term = jnp.dot(err[...], turned[flip], **DOT)
+def term_kernel(flip, keep, err, dec, out):
+    slab = dec[flip - 1] if flip else dec[...]
+    term = lax.dot_general(err[...], slab, (((1,), (1,)), ((), ())), **DOT)
     out[...] = (keep[flip, 0:1, :] * term).astype(out.dtype)
 
 
@@ -217,18 +214,15 @@
 
     shares = shares.reshape(GROUP, rows, width)
     shares = lax.all_to_all(shares, NEAR, 0, 0, tiled=True)
-    near = call(gather_sum_kernel, shape((rows, width), BF), [VMEM])(shares)
-    parts = [near] * ZH
-    for flip in (2, 3, 1):
-        parts[flip] = swap(near, "zh", flip)
-    turned = call(turn_kernel, shape((TG, width, feats), BF), [VMEM] * 2)(mine, dec)
-    copies = call(spread_kernel, shape((GROUP, rows, width), BF), [VMEM] * 4)(*parts)
+    near = call(gather_sum_kernel, shape((ZH, rows, width), BF), [VMEM])(shares)
+    parts = lax.all_to_all(near, "zh", 0, 0, tiled=True)
+    copies = call(spread_kernel, shape((GROUP, rows, width), BF), [VMEM])(parts)
     err_full = lax.all_to_all(copies, NEAR, 0, 0, tiled=True).reshape(tok, width)
 
     def term(flip, kind):
         kernel = functools.partial(term_kernel, flip)
         return call(kernel, shape((tok, feats), kind), [VMEM] * 3, flops)(
-            keep, err_full, turned
+            keep, err_full, dec if flip else mine
         )
 
     diag = term(3, BF)

time: 75.3 us -> 70 us (0.930)
  blocking collectives: 18.7 us -> 47 us
  starting transfers between devices: 23.2 us -> 11.7 us
  waiting for transfers between devices: 10.4 us -> 1.98 us
  local copies, waits for them, and re-layouts: 7.37 us -> 0.01 us
  Pallas kernels: 13.4 us -> 7.73 us
    all_to_all x0 -> x2, blocking collectives: none -> 28.3 us  [the longest x1 14.4 us: per_device(): parts = lax.all_to_all(near, 'zh', 0, 0, tiled=True)]
    unnamed x18 -> x2, local copies, waits for them, and re-layouts: 7.37 us -> 0.01 us
    ppermute x9 -> x6, starting transfers between devices: 18.9 us -> 11.7 us  [swap(): return lax.ppermute(value, name, [(i, i ^ flip) for i in range(size)])]
    all_to_all x1 -> x0, waiting for transfers between devices: 4.72 us -> none  [per_device(): lax.all_to_all(copies, NEAR, 0, 0, tiled=True).reshape(tok, width)]
    all_to_all x1 -> x0, starting transfers between devices: 4.24 us -> none  [per_device(): lax.all_to_all(copies, NEAR, 0, 0, tiled=True).reshape(tok, width)]
    ppermute x9 -> x6, waiting for transfers between devices: 5.72 us -> 1.98 us  [swap(): return lax.ppermute(value, name, [(i, i ^ flip) for i in range(size)])]
    pallas_call x4, Pallas kernels: 5.55 us -> 2.12 us  [term(): call(kernel, shape((tok, feats), kind), [VMEM] * 3, flops)]
    pallas_call x3 -> x2, Pallas kernels: 1.39 us -> 0.13 us  [the longest x1 0.08 us: per_device(): near = call(gather_sum_kernel, shape((ZH, rows, width), BF), [VMEM])(shares)]
  transfers between devices with their start and end apart: 10 -> 6, of which waited for: 3 -> 2; matrix products, arithmetic and copies ran while one was open for 0% -> 0% of each run, Pallas kernels for 13% -> 7%
where the time goes in v13:
time: 70 us; the launch traced here: 69.8 us
  blocking collectives  47 us (67%)
  starting transfers between devices  11.7 us (17%)
  Pallas kernels  7.73 us (11%)
  waiting for transfers between devices  1.98 us (3%)
  between operations  0.73 us (1%)
    all_to_all x1, blocking collectives, per_device(): shares = lax.all_to_all(shares, NEAR, 0, 0, tiled=True)  18.7 us
    all_to_all x1, blocking collectives, per_device(): parts = lax.all_to_all(near, 'zh', 0, 0, tiled=True)  14.4 us
    all_to_all x1, blocking collectives, per_device(): lax.all_to_all(copies, NEAR, 0, 0, tiled=True).reshape(tok, width)  13.9 us
    ppermute x6, starting transfers between devices, swap(): return lax.ppermute(value, name, [(i, i ^ flip) for i in range(size)])  11.7 us
    pallas_call x4, Pallas kernels, term(): call(kernel, shape((tok, feats), kind), [VMEM] * 3, flops)  2.12 us
    pallas_call x1, Pallas kernels, per_device(): dec, own, keep = load(in_hbm(pair_mask), latent, mine, slabs)  2.03 us
    ppermute x6, waiting for transfers between devices, swap(): return lax.ppermute(value, name, [(i, i ^ flip) for i in range(size)])  1.98 us
    pallas_call x1, Pallas kernels, per_device(): call(encode_kernel, [shape((tok, feats), BF), shape((feats, width), BF)],...  1.88 us
  transfers between devices with their start and end apart: 6, of which 2 were waited for; matrix products, arithmetic and copies ran while one was open for 0% of the time, Pallas kernels for 7%

profile of v13, /device:TPU:1, one launch (start us, length us, event | category | flops | bytes accessed | tf_op | source)
XLA Modules:
  0.0 69.8 jit_solution(8305723445277336191)
XLA Ops:
  0.6 1.9 %shard_map.77 = (bf16[128,256]{1,0:T(8,128)(2,1)S(1)}, bf16[256,2304]{1,0:T(8,128)(2,1)S(1)}) custom-call(bf16[128,2304]{1,0:T(8,128)(2,1)} %bitcast.19, bf16[2304,256]{1,0:T(8,128)(2,1)} %bitcast.18, f32[1,256]{1,0:T(1,128)} %bias.1, bf16[4,256,2304]{2,1,0:T(8,128)(2,1)} %bitcast.16), custom_call_target="tpu_custom_call" | custom-call | flops 150994944 | bytes 1179648 | tf_op jit(solution)/shard_map/pallas_call | solution.py:176
  2.5 2.2 %collective-permute-start.1 = (bf16[128,256]{1,0:T(8,128)(2,1)S(1)}, bf16[128,256]{1,0:T(8,128)(2,1)S(1)}, u32[]{:S(2)}, u32[]{:S(2)}) collective-permute-start(bf16[128,256]{1,0:T(8,128)(2,1)S(1)} %get-tuple-element.7.latent), channel_id=1, source_target_pairs={{0,2},{1,3},{2,0},{3,1},{4,6},{5,7},{6,4},{7,5},{8,10},{9,11},{10,... | collective-permute-start | bytes 196616 | tf_op jit(solution)/shard_map/ppermute | solution.py:148
  4.7 1.2 %collective-permute-start = (bf16[128,256]{1,0:T(8,128)(2,1)S(1)}, bf16[128,256]{1,0:T(8,128)(2,1)S(1)}, u32[]{:S(2)}, u32[]{:S(2)}) collective-permute-start(bf16[128,256]{1,0:T(8,128)(2,1)S(1)} %get-tuple-element.7.latent), channel_id=1, source_target_pairs={{0,1},{1,0},{2,3},{3,2},{4,5},{5,4},{6,7},{7,6},{8,9},{9,8},{10,11... | collective-permute-start | bytes 196616 | tf_op jit(solution)/shard_map/ppermute | solution.py:148
  5.9 0.5 collective-permute-done.1.l2
  6.4 3.7 %collective-permute-start.2 = (bf16[128,256]{1,0:T(8,128)(2,1)S(1)}, bf16[128,256]{1,0:T(8,128)(2,1)S(1)}, u32[]{:S(2)}, u32[]{:S(2)}) collective-permute-start(bf16[128,256]{1,0:T(8,128)(2,1)S(1)} %collective-permute-done.1.l2), channel_id=1, source_target_pairs={{0,1},{1,0},{2,3},{3,2},{4,5},{5,4},{6,7},{7,6},{8,9},{9,8},{10,11... | collective-permute-start | bytes 196616 | tf_op jit(solution)/shard_map/ppermute | solution.py:148
  10.1 0.0 copy-start
  10.1 2.0 %shard_map.78 = (bf16[3,256,2304]{2,1,0:T(8,128)(2,1)S(1)}, f32[128,2304]{1,0:T(8,128)S(1)}, f32[4,8,256]{2,1,0:T(8,128)S(1)}) custom-call(s32[4,4]{1,0:T(4,128)} %mask.1, bf16[128,256]{1,0:T(8,128)(2,1)S(1)} %get-tuple-element.7.latent, bf16[256,2304]{1,0:T(8,128)(2,1)S(1)} %get-tuple-element.8.mine.dec, bf16[4,256,2304]{2,1,0:T(8,128)(2,1)} %bitcast.17), custom_call_target="tpu_custom_call" | custom-call | flops 150994944 | bytes 4718592 | tf_op jit(solution)/shard_map/pallas_call | solution.py:206
  12.1 0.0 collective-permute-done.l1
  12.1 0.0 copy-done
  12.1 0.5 shard_map.79.most
  12.7 0.0 collective-permute-done.2.l3
  12.7 0.3 shard_map.80
  13.0 18.7 %all_to_all.15.shares = bf16[16,8,2304]{2,1,0:T(8,128)(2,1)S(1)} all-to-all(bf16[16,8,2304]{2,1,0:T(8,128)(2,1)S(1)} %bitcast.14), channel_id=1, replica_groups=mesh['x'=4,'yh'=2,'zh'=4,'zl'=2,'tgt'=4] {'x','yh','zl'}, dimensions={0} | all-to-all | bytes 1179648 | tf_op jit(solution)/shard_map/all_to_all | solution.py:216
  31.7 0.1 shard_map.81
  31.8 14.4 %all_to_all.16.parts = bf16[4,8,2304]{2,1,0:T(8,128)(2,1)S(1)} all-to-all(bf16[4,8,2304]{2,1,0:T(8,128)(2,1)S(1)} %shard_map.81), channel_id=1, replica_groups=mesh['x'=4,'yh'=2,'zh'=4,'zl'=2,'tgt'=4] {'zh'}, dimensions={0} | all-to-all | bytes 294912 | tf_op jit(solution)/shard_map/all_to_all | solution.py:218
  46.3 13.9 %all_to_all.17 = bf16[16,8,2304]{2,1,0:T(8,128)(2,1)S(1)} all-to-all(bf16[16,8,2304]{2,1,0:T(8,128)(2,1)S(1)} %shard_map.82), channel_id=1, replica_groups=mesh['x'=4,'yh'=2,'zh'=4,'zl'=2,'tgt'=4] {'x','yh','zl'}, dimensions={0} | all-to-all | bytes 1179648 | tf_op jit(solution)/shard_map/all_to_all | solution.py:220
  60.2 0.5 shard_map.87
  60.7 4.0 %collective-permute-start.4 = (bf16[128,256]{1,0:T(8,128)(2,1)S(1)}, bf16[128,256]{1,0:T(8,128)(2,1)S(1)}, u32[]{:S(2)}, u32[]{:S(2)}) collective-permute-start(bf16[128,256]{1,0:T(8,128)(2,1)S(1)} %shard_map.87), channel_id=1, source_target_pairs={{0,1},{1,0},{2,3},{3,2},{4,5},{5,4},{6,7},{7,6},{8,9},{9,8},{10,11... | collective-permute-start | bytes 196616 | tf_op jit(solution)/shard_map/ppermute | solution.py:148
  64.7 0.5 shard_map.85
  65.3 0.1 collective-permute-start.3
  65.4 0.5 shard_map.86.a
  65.9 0.0 collective-permute-done.4.b
  65.9 0.5 collective-permute-start.5
  66.4 0.7 shard_map.83
  67.1 0.5 shard_map.84
  67.6 0.0 collective-permute-done.3
  67.6 1.5 %collective-permute-done.5 = bf16[128,256]{1,0:T(8,128)(2,1)S(1)} collective-permute-done((bf16[128,256]{1,0:T(8,128)(2,1)S(1)}, bf16[128,256]{1,0:T(8,128)(2,1)S(1)}, u32[]{:S(2)}, u32[]{:S(2)}) %collective-permute-start.5) | collective-permute-done | bytes 65568 | tf_op jit(solution)/shard_map/ppermute | solution.py:148
  69.1 0.7 fusion
  (2 shorter events, 0.1 us)
Async XLA Ops:
  2.5 3.9 %collective-permute-start.1 = (bf16[128,256]{1,0:T(8,128)(2,1)S(1)}, bf16[128,256]{1,0:T(8,128)(2,1)S(1)}, u32[]{:S(2)}, u32[]{:S(2)}) collective-permute-start(bf16[128,256]{1,0:T(8,128)(2,1)S(1)} %get-tuple-element.7.latent), channel_id=1, source_target_pairs={{0,2},{1,3},{2,0},{3,1},{4,6},{5,7},{6,4},{7,5},{8,10},{9,11},{10,... | collective-permute-start | bytes 196616 | tf_op jit(solution)/shard_map/ppermute | solution.py:148
  4.7 7.4 %collective-permute-start = (bf16[128,256]{1,0:T(8,128)(2,1)S(1)}, bf16[128,256]{1,0:T(8,128)(2,1)S(1)}, u32[]{:S(2)}, u32[]{:S(2)}) collective-permute-start(bf16[128,256]{1,0:T(8,128)(2,1)S(1)} %get-tuple-element.7.latent), channel_id=1, source_target_pairs={{0,1},{1,0},{2,3},{3,2},{4,5},{5,4},{6,7},{7,6},{8,9},{9,8},{10,11... | collective-permute-start | bytes 196616 | tf_op jit(solution)/shard_map/ppermute | solution.py:148
  6.4 6.3 %collective-permute-start.2 = (bf16[128,256]{1,0:T(8,128)(2,1)S(1)}, bf16[128,256]{1,0:T(8,128)(2,1)S(1)}, u32[]{:S(2)}, u32[]{:S(2)}) collective-permute-start(bf16[128,256]{1,0:T(8,128)(2,1)S(1)} %collective-permute-done.1.l2), channel_id=1, source_target_pairs={{0,1},{1,0},{2,3},{3,2},{4,5},{5,4},{6,7},{7,6},{8,9},{9,8},{10,11... | collective-permute-start | bytes 196616 | tf_op jit(solution)/shard_map/ppermute | solution.py:148
  10.1 2.1 %copy-start = (bf16[1,2,2304]{2,1,0:T(2,128)(2,1)S(1)}, bf16[1,2,2304]{2,1,0:T(2,128)(2,1)}, u32[]{:S(2)}) copy-start(bf16[1,2,2304]{2,1,0:T(2,128)(2,1)} %param.7) | copy-start | bytes 27652
  60.7 5.2 %collective-permute-start.4 = (bf16[128,256]{1,0:T(8,128)(2,1)S(1)}, bf16[128,256]{1,0:T(8,128)(2,1)S(1)}, u32[]{:S(2)}, u32[]{:S(2)}) collective-permute-start(bf16[128,256]{1,0:T(8,128)(2,1)S(1)} %shard_map.87), channel_id=1, source_target_pairs={{0,1},{1,0},{2,3},{3,2},{4,5},{5,4},{6,7},{7,6},{8,9},{9,8},{10,11... | collective-permute-start | bytes 196616 | tf_op jit(solution)/shard_map/ppermute | solution.py:148
  65.3 2.4 %collective-permute-start.3 = (bf16[128,256]{1,0:T(8,128)(2,1)S(1)}, bf16[128,256]{1,0:T(8,128)(2,1)S(1)}, u32[]{:S(2)}, u32[]{:S(2)}) collective-permute-start(bf16[128,256]{1,0:T(8,128)(2,1)S(1)} %shard_map.85), channel_id=1, source_target_pairs={{0,1},{1,0},{2,3},{3,2},{4,5},{5,4},{6,7},{7,6},{8,9},{9,8},{10,11... | collective-permute-start | bytes 196616 | tf_op jit(solution)/shard_map/ppermute | solution.py:148
  65.9 3.2 %collective-permute-start.5 = (bf16[128,256]{1,0:T(8,128)(2,1)S(1)}, bf16[128,256]{1,0:T(8,128)(2,1)S(1)}, u32[]{:S(2)}, u32[]{:S(2)}) collective-permute-start(bf16[128,256]{1,0:T(8,128)(2,1)S(1)} %shard_map.88), channel_id=1, source_target_pairs={{0,2},{1,3},{2,0},{3,1},{4,6},{5,7},{6,4},{7,5},{8,10},{9,11},{10,... | collective-permute-start | bytes 196616 | tf_op jit(solution)/shard_map/ppermute | solution.py:148

commit v14 on v12

--- a/solution.py
+++ b/solution.py
@@ -9,9 +9,9 @@
 
 
 X, YH, ZH, ZL, TG = 4, 2, 4, 2, 4
-NEAR = ("x", "yh", "zl")
+NEAR = ("x", "zl")
 FEAT = ("x", "yh", "zh", "zl")
-GROUP = X * YH * ZL
+GROUP = X * ZL
 DOT = dict(preferred_element_type=jnp.float32)
 BF, F32 = jnp.bfloat16, jnp.float32
 VMEM = pl.BlockSpec(memory_space=pltpu.VMEM)
@@ -110,6 +110,10 @@
     for i in range(1, shares.shape[0]):
         total = total + shares[i].astype(F32)
     out[...] = total.astype(out.dtype)
+
+
+def pair_kernel(a, b, out):
+    out[...] = (a[...].astype(F32) + b[...].astype(F32)).astype(out.dtype)
 
 
 def spread_kernel(s0, s1, s2, s3, out):
@@ -218,6 +222,8 @@
     shares = shares.reshape(GROUP, rows, width)
     shares = lax.all_to_all(shares, NEAR, 0, 0, tiled=True)
     near = call(gather_sum_kernel, shape((rows, width), BF), [VMEM])(shares)
+    other = swap(near, "yh", 1)
+    near = call(pair_kernel, shape((rows, width), BF), [VMEM] * 2)(near, other)
     parts = [near] * ZH
     for flip in (2, 3, 1):
         parts[flip] = swap(near, "zh", flip)

time: 75.3 us -> 76.5 us (1.016)
  starting transfers between devices: 23.2 us -> 28.4 us
  blocking collectives: 18.7 us -> 13.8 us
  waiting for transfers between devices: 10.4 us -> 11.4 us
    ppermute x9 -> x10, starting transfers between devices: 18.9 us -> 24.2 us  [swap(): return lax.ppermute(value, name, [(i, i ^ flip) for i in range(size)])]
    all_to_all x1, blocking collectives: 18.7 us -> 13.8 us  [per_device(): shares = lax.all_to_all(shares, NEAR, 0, 0, tiled=True)]
    ppermute x9 -> x10, waiting for transfers between devices: 5.72 us -> 8.18 us  [swap(): return lax.ppermute(value, name, [(i, i ^ flip) for i in range(size)])]
    all_to_all x1, waiting for transfers between devices: 4.72 us -> 3.22 us  [per_device(): lax.all_to_all(copies, NEAR, 0, 0, tiled=True).reshape(tok, width)]
  transfers between devices with their start and end apart: 10 -> 11, of which waited for: 3 -> 4; matrix products, arithmetic and copies ran while one was open for 0% -> 0% of each run, Pallas kernels for 13% -> 13%
where the time goes in v14:
time: 76.5 us; the launch traced here: 75.9 us
  starting transfers between devices  28.4 us (37%)
  blocking collectives  13.8 us (18%)
  Pallas kernels  13.5 us (18%)
  waiting for transfers between devices  11.4 us (15%)
  local copies, waits for them, and re-layouts  7.38 us (10%)
  between operations  0.85 us (1%)
    ppermute x10, starting transfers between devices, swap(): return lax.ppermute(value, name, [(i, i ^ flip) for i in range(size)])  24.2 us
    all_to_all x1, blocking collectives, per_device(): shares = lax.all_to_all(shares, NEAR, 0, 0, tiled=True)  13.8 us
    ppermute x10, waiting for transfers between devices, swap(): return lax.ppermute(value, name, [(i, i ^ flip) for i in range(size)])  8.18 us
    unnamed x18, local copies, waits for them, and re-layouts  7.38 us
    pallas_call x4, Pallas kernels, term(): call(kernel, shape((tok, feats), kind), [VMEM] * 3, flops)  5.55 us
    all_to_all x1, starting transfers between devices, per_device(): lax.all_to_all(copies, NEAR, 0, 0, tiled=True).reshape(tok, width)  4.19 us
    all_to_all x1, waiting for transfers between devices, per_device(): lax.all_to_all(copies, NEAR, 0, 0, tiled=True).reshape(tok, width)  3.22 us
    pallas_call x1, Pallas kernels, per_device(): dec, own, keep = load(in_hbm(pair_mask), latent, mine, slabs)  2.03 us
  transfers between devices with their start and end apart: 11, of which 4 were waited for; matrix products, arithmetic and copies ran while one was open for 0% of the time, Pallas kernels for 13%

profile of v14, /device:TPU:1, one launch (start us, length us, event | category | flops | bytes accessed | tf_op | source)
XLA Modules:
  0.0 75.9 jit_solution(14477224492989426205)
XLA Ops:
  0.6 1.9 %shard_map.77 = (bf16[128,256]{1,0:T(8,128)(2,1)S(1)}, bf16[256,2304]{1,0:T(8,128)(2,1)S(1)}) custom-call(bf16[128,2304]{1,0:T(8,128)(2,1)} %bitcast.14, bf16[2304,256]{1,0:T(8,128)(2,1)} %bitcast.13, f32[1,256]{1,0:T(1,128)} %bias.1, bf16[4,256,2304]{2,1,0:T(8,128)(2,1)} %bitcast.11), custom_call_target="tpu_custom_call" | custom-call | flops 150994944 | bytes 1179648 | tf_op jit(solution)/shard_map/pallas_call | solution.py:183
  2.5 0.0 copy-start.2
  2.5 2.2 %collective-permute-start.1 = (bf16[128,256]{1,0:T(8,128)(2,1)S(1)}, bf16[128,256]{1,0:T(8,128)(2,1)S(1)}, u32[]{:S(2)}, u32[]{:S(2)}) collective-permute-start(bf16[128,256]{1,0:T(8,128)(2,1)S(1)} %get-tuple-element.7.latent), channel_id=1, source_target_pairs={{0,2},{1,3},{2,0},{3,1},{4,6},{5,7},{6,4},{7,5},{8,10},{9,11},{10,... | collective-permute-start | bytes 196616 | tf_op jit(solution)/shard_map/ppermute | solution.py:155
  4.7 1.2 %collective-permute-start = (bf16[128,256]{1,0:T(8,128)(2,1)S(1)}, bf16[128,256]{1,0:T(8,128)(2,1)S(1)}, u32[]{:S(2)}, u32[]{:S(2)}) collective-permute-start(bf16[128,256]{1,0:T(8,128)(2,1)S(1)} %get-tuple-element.7.latent), channel_id=1, source_target_pairs={{0,1},{1,0},{2,3},{3,2},{4,5},{5,4},{6,7},{7,6},{8,9},{9,8},{10,11... | collective-permute-start | bytes 196616 | tf_op jit(solution)/shard_map/ppermute | solution.py:155
  5.9 0.5 collective-permute-done.1.l2
  6.4 3.7 %collective-permute-start.2 = (bf16[128,256]{1,0:T(8,128)(2,1)S(1)}, bf16[128,256]{1,0:T(8,128)(2,1)S(1)}, u32[]{:S(2)}, u32[]{:S(2)}) collective-permute-start(bf16[128,256]{1,0:T(8,128)(2,1)S(1)} %collective-permute-done.1.l2), channel_id=1, source_target_pairs={{0,1},{1,0},{2,3},{3,2},{4,5},{5,4},{6,7},{7,6},{8,9},{9,8},{10,11... | collective-permute-start | bytes 196616 | tf_op jit(solution)/shard_map/ppermute | solution.py:155
  10.1 2.0 %shard_map.78 = (bf16[3,256,2304]{2,1,0:T(8,128)(2,1)S(1)}, f32[128,2304]{1,0:T(8,128)S(1)}, f32[4,8,256]{2,1,0:T(8,128)S(1)}) custom-call(s32[4,4]{1,0:T(4,128)} %mask.1, bf16[128,256]{1,0:T(8,128)(2,1)S(1)} %get-tuple-element.7.latent, bf16[256,2304]{1,0:T(8,128)(2,1)S(1)} %get-tuple-element.8.mine, bf16[4,256,2304]{2,1,0:T(8,128)(2,1)} %bitcast.12), custom_call_target="tpu_custom_call" | custom-call | flops 150994944 | bytes 4718592 | tf_op jit(solution)/shard_map/pallas_call | solution.py:213
  12.1 0.0 copy-done.2
  12.1 0.0 copy-start.5
  12.1 0.0 collective-permute-done.l1
  12.2 0.0 copy-done.8
  12.2 0.5 shard_map.79.most
  12.7 0.0 collective-permute-done.2.l3
  12.7 0.0 copy-done.5
  12.8 0.3 shard_map.80
  13.1 13.8 %all_to_all.10.shares = bf16[8,16,2304]{2,1,0:T(8,128)(2,1)S(1)} all-to-all(bf16[8,16,2304]{2,1,0:T(8,128)(2,1)S(1)} %bitcast.9), channel_id=1, replica_groups=mesh['x'=4,'yh'=2,'zh'=4,'zl'=2,'tgt'=4] {'x','zl'}, dimensions={0} | all-to-all | bytes 1179648 | tf_op jit(solution)/shard_map/all_to_all | solution.py:223
  26.9 0.1 shard_map.81.a
  26.9 3.0 %collective-permute-start.3 = (bf16[16,2304]{1,0:T(8,128)(2,1)S(1)}, bf16[16,2304]{1,0:T(8,128)(2,1)S(1)}, u32[]{:S(2)}, u32[]{:S(2)}) collective-permute-start(bf16[16,2304]{1,0:T(8,128)(2,1)S(1)} %shard_map.81.a), channel_id=1, source_target_pairs={{0,32},{32,0},{1,33},{33,1},{2,34},{34,2},{3,35},{35,3},{4,36},{36... | collective-permute-start | bytes 221192 | tf_op jit(solution)/shard_map/ppermute | solution.py:155
  29.9 1.8 %collective-permute-done.3.b = bf16[16,2304]{1,0:T(8,128)(2,1)S(1)} collective-permute-done((bf16[16,2304]{1,0:T(8,128)(2,1)S(1)}, bf16[16,2304]{1,0:T(8,128)(2,1)S(1)}, u32[]{:S(2)}, u32[]{:S(2)}) %collective-permute-start.3) | collective-permute-done | bytes 73760 | tf_op jit(solution)/shard_map/ppermute | solution.py:155
  31.8 5.2 %collective-permute-start.6 = (bf16[16,2304]{1,0:T(8,128)(2,1)S(1)}, bf16[16,2304]{1,0:T(8,128)(2,1)S(1)}, u32[]{:S(2)}, u32[]{:S(2)}) collective-permute-start(bf16[16,2304]{1,0:T(8,128)(2,1)S(1)} %shard_map.82.s0), channel_id=1, source_target_pairs={{0,24},{8,16},{16,8},{24,0},{1,25},{9,17},{17,9},{25,1},{2,26},{10... | collective-permute-start | bytes 221192 | tf_op jit(solution)/shard_map/ppermute | solution.py:155
  37.0 1.2 %collective-permute-start.5 = (bf16[16,2304]{1,0:T(8,128)(2,1)S(1)}, bf16[16,2304]{1,0:T(8,128)(2,1)S(1)}, u32[]{:S(2)}, u32[]{:S(2)}) collective-permute-start(bf16[16,2304]{1,0:T(8,128)(2,1)S(1)} %shard_map.82.s0), channel_id=1, source_target_pairs={{0,16},{8,24},{16,0},{24,8},{1,17},{9,25},{17,1},{25,9},{2,18},{10... | collective-permute-start | bytes 221192 | tf_op jit(solution)/shard_map/ppermute | solution.py:155
  38.1 1.0 %collective-permute-start.4 = (bf16[16,2304]{1,0:T(8,128)(2,1)S(1)}, bf16[16,2304]{1,0:T(8,128)(2,1)S(1)}, u32[]{:S(2)}, u32[]{:S(2)}) collective-permute-start(bf16[16,2304]{1,0:T(8,128)(2,1)S(1)} %shard_map.82.s0), channel_id=1, source_target_pairs={{0,8},{8,0},{16,24},{24,16},{1,9},{9,1},{17,25},{25,17},{2,10},{10... | collective-permute-start | bytes 221192 | tf_op jit(solution)/shard_map/ppermute | solution.py:155
  39.1 0.0 collective-permute-done.6.s3
  39.1 5.9 %collective-permute-done.5.s2 = bf16[16,2304]{1,0:T(8,128)(2,1)S(1)} collective-permute-done((bf16[16,2304]{1,0:T(8,128)(2,1)S(1)}, bf16[16,2304]{1,0:T(8,128)(2,1)S(1)}, u32[]{:S(2)}, u32[]{:S(2)}) %collective-permute-start.5) | collective-permute-done | bytes 73760 | tf_op jit(solution)/shard_map/ppermute | solution.py:155
  45.0 0.0 collective-permute-done.4.s1
  45.1 0.0 copy-start.4
  45.1 0.8 %copy-done.4 = bf16[8,16,2304]{2,1,0:T(8,128)(2,1)} copy-done((bf16[8,16,2304]{2,1,0:T(8,128)(2,1)}, bf16[8,16,2304]{2,1,0:T(8,128)(2,1)S(1)}, u32[]{:S(2)}) %copy-start.4) | copy-done | bytes 589848
  45.9 4.2 %all-to-all-start.1 = ((bf16[8,16,2304]{2,1,0:T(8,128)(2,1)}), bf16[8,16,2304]{2,1,0:T(8,128)(2,1)}, u32[]{:S(2)}, u32[]{:S(2)}) async-start(bf16[8,16,2304]{2,1,0:T(8,128)(2,1)} %copy-done.4), calls=%async_computation.1 | async-start | bytes 1179648 | tf_op jit(solution)/shard_map/all_to_all | solution.py:232
  50.1 1.3 %copy-done.3 = bf16[256,2304]{1,0:T(8,128)(2,1)S(1)} copy-done((bf16[256,2304]{1,0:T(8,128)(2,1)S(1)}, bf16[256,2304]{1,0:T(8,128)(2,1)}, u32[]{:S(2)}) %copy-start.3) | copy-done | bytes 1179672
  51.4 1.3 %shard_map.85.turned = bf16[4,2304,256]{2,1,0:T(8,128)(2,1)S(1)} custom-call(bf16[256,2304]{1,0:T(8,128)(2,1)S(1)} %copy-done.3, bf16[3,256,2304]{2,1,0:T(8,128)(2,1)S(1)} %get-tuple-element.11.dec), custom_call_target="tpu_custom_call" | custom-call | tf_op jit(solution)/shard_map/pallas_call | solution.py:230
  52.7 2.1 %copy-done = bf16[4,2304,256]{2,1,0:T(8,128)(2,1)} copy-done((bf16[4,2304,256]{2,1,0:T(8,128)(2,1)}, bf16[4,2304,256]{2,1,0:T(8,128)(2,1)S(1)}, u32[]{:S(2)}) %copy-start) | copy-done | bytes 4718616
  54.8 3.2 %all-to-all-done.1 = bf16[8,16,2304]{2,1,0:T(8,128)(2,1)} async-done(((bf16[8,16,2304]{2,1,0:T(8,128)(2,1)}), bf16[8,16,2304]{2,1,0:T(8,128)(2,1)}, u32[]{:S(2)}, u32[]{:S(2)}) %all-to-all-start.1) | async-done | bytes 589856 | tf_op jit(solution)/shard_map/all_to_all | solution.py:232
  58.0 2.3 %copy-done.1 = bf16[4,2304,256]{2,1,0:T(8,128)(2,1)S(1)} copy-done((bf16[4,2304,256]{2,1,0:T(8,128)(2,1)S(1)}, bf16[4,2304,256]{2,1,0:T(8,128)(2,1)}, u32[]{:S(2)}) %copy-start.1) | copy-done | bytes 4718616
  60.3 0.8 copy-done.6
  61.1 1.4 %shard_map.89 = bf16[128,256]{1,0:T(8,128)(2,1)S(1)} custom-call(f32[4,8,256]{2,1,0:T(8,128)S(1)} %copy-done.6, bf16[128,2304]{1,0:T(8,128)(2,1)} %bitcast.5.err, bf16[4,2304,256]{2,1,0:T(8,128)(2,1)S(1)} %copy-done.1), custom_call_target="tpu_custom_call" | custom-call | flops 150994944 | tf_op jit(solution)/shard_map/pallas_call | solution.py:236
  62.5 0.0 copy-start.7
  62.5 5.2 %collective-permute-start.8 = (bf16[128,256]{1,0:T(8,128)(2,1)S(1)}, bf16[128,256]{1,0:T(8,128)(2,1)S(1)}, u32[]{:S(2)}, u32[]{:S(2)}) collective-permute-start(bf16[128,256]{1,0:T(8,128)(2,1)S(1)} %shard_map.89), channel_id=1, source_target_pairs={{0,1},{1,0},{2,3},{3,2},{4,5},{5,4},{6,7},{7,6},{8,9},{9,8},{10,11... | collective-permute-start | bytes 196616 | tf_op jit(solution)/shard_map/ppermute | solution.py:155
  67.7 1.4 %shard_map.87 = bf16[128,256]{1,0:T(8,128)(2,1)S(1)} custom-call(f32[4,8,256]{2,1,0:T(8,128)S(1)} %copy-done.6, bf16[128,2304]{1,0:T(8,128)(2,1)} %bitcast.5.err, bf16[4,2304,256]{2,1,0:T(8,128)(2,1)S(1)} %copy-done.1), custom_call_target="tpu_custom_call" | custom-call | flops 150994944 | tf_op jit(solution)/shard_map/pallas_call | solution.py:236
  69.1 0.1 collective-permute-start.7
  69.2 0.0 copy-done.7
  69.2 1.4 %shard_map.88.a = f32[128,256]{1,0:T(8,128)S(1)} custom-call(f32[4,8,256]{2,1,0:T(8,128)S(1)} %copy-done.7, bf16[128,2304]{1,0:T(8,128)(2,1)} %bitcast.5.err, bf16[4,2304,256]{2,1,0:T(8,128)(2,1)S(1)} %copy-done.1), custom_call_target="tpu_custom_call" | custom-call | flops 150994944 | tf_op jit(solution)/shard_map/pallas_call | solution.py:236
  70.6 0.0 collective-permute-done.8.b
  70.7 1.4 %collective-permute-start.9 = (bf16[128,256]{1,0:T(8,128)(2,1)S(1)}, bf16[128,256]{1,0:T(8,128)(2,1)S(1)}, u32[]{:S(2)}, u32[]{:S(2)}) collective-permute-start(bf16[128,256]{1,0:T(8,128)(2,1)S(1)} %shard_map.90), channel_id=1, source_target_pairs={{0,2},{1,3},{2,0},{3,1},{4,6},{5,7},{6,4},{7,5},{8,10},{9,11},{10,... | collective-permute-start | bytes 196616 | tf_op jit(solution)/shard_map/ppermute | solution.py:155
  72.1 1.7 %shard_map.84 = bf16[2,2304]{1,0:T(2,128)(2,1)} custom-call(bf16[128,2304]{1,0:T(8,128)(2,1)} %bitcast.5.err), custom_call_target="tpu_custom_call" | custom-call | tf_op jit(solution)/shard_map/pallas_call | solution.py:248
  73.8 1.4 %shard_map.86 = f32[128,256]{1,0:T(8,128)S(1)} custom-call(f32[4,8,256]{2,1,0:T(8,128)S(1)} %copy-done.7, bf16[128,2304]{1,0:T(8,128)(2,1)} %bitcast.5.err, bf16[4,2304,256]{2,1,0:T(8,128)(2,1)S(1)} %copy-done.1), custom_call_target="tpu_custom_call" | custom-call | flops 150994944 | tf_op jit(solution)/shard_map/pallas_call | solution.py:236
  75.2 0.0 collective-permute-done.7
  75.2 0.0 collective-permute-done.9
  75.2 0.7 fusion
  (8 shorter events, 0.1 us)
Async XLA Ops:
  2.5 9.6 %copy-start.2 = (bf16[256,2304]{1,0:T(8,128)(2,1)}, bf16[256,2304]{1,0:T(8,128)(2,1)S(1)}, u32[]{:S(2)}) copy-start(bf16[256,2304]{1,0:T(8,128)(2,1)S(1)} %get-tuple-element.8.mine) | copy-start | bytes 3538948
  2.5 3.9 %collective-permute-start.1 = (bf16[128,256]{1,0:T(8,128)(2,1)S(1)}, bf16[128,256]{1,0:T(8,128)(2,1)S(1)}, u32[]{:S(2)}, u32[]{:S(2)}) collective-permute-start(bf16[128,256]{1,0:T(8,128)(2,1)S(1)} %get-tuple-element.7.latent), channel_id=1, source_target_pairs={{0,2},{1,3},{2,0},{3,1},{4,6},{5,7},{6,4},{7,5},{8,10},{9,11},{10,... | collective-permute-start | bytes 196616 | tf_op jit(solution)/shard_map/ppermute | solution.py:155
  4.7 7.4 %collective-permute-start = (bf16[128,256]{1,0:T(8,128)(2,1)S(1)}, bf16[128,256]{1,0:T(8,128)(2,1)S(1)}, u32[]{:S(2)}, u32[]{:S(2)}) collective-permute-start(bf16[128,256]{1,0:T(8,128)(2,1)S(1)} %get-tuple-element.7.latent), channel_id=1, source_target_pairs={{0,1},{1,0},{2,3},{3,2},{4,5},{5,4},{6,7},{7,6},{8,9},{9,8},{10,11... | collective-permute-start | bytes 196616 | tf_op jit(solution)/shard_map/ppermute | solution.py:155
  6.4 6.3 %collective-permute-start.2 = (bf16[128,256]{1,0:T(8,128)(2,1)S(1)}, bf16[128,256]{1,0:T(8,128)(2,1)S(1)}, u32[]{:S(2)}, u32[]{:S(2)}) collective-permute-start(bf16[128,256]{1,0:T(8,128)(2,1)S(1)} %collective-permute-done.1.l2), channel_id=1, source_target_pairs={{0,1},{1,0},{2,3},{3,2},{4,5},{5,4},{6,7},{7,6},{8,9},{9,8},{10,11... | collective-permute-start | bytes 196616 | tf_op jit(solution)/shard_map/ppermute | solution.py:155
  10.1 2.1 %copy-start.8 = (bf16[1,2,2304]{2,1,0:T(2,128)(2,1)S(1)}, bf16[1,2,2304]{2,1,0:T(2,128)(2,1)}, u32[]{:S(2)}) copy-start(bf16[1,2,2304]{2,1,0:T(2,128)(2,1)} %param.7) | copy-start | bytes 27652
  12.1 0.6 copy-start.5
  26.9 4.8 %collective-permute-start.3 = (bf16[16,2304]{1,0:T(8,128)(2,1)S(1)}, bf16[16,2304]{1,0:T(8,128)(2,1)S(1)}, u32[]{:S(2)}, u32[]{:S(2)}) collective-permute-start(bf16[16,2304]{1,0:T(8,128)(2,1)S(1)} %shard_map.81.a), channel_id=1, source_target_pairs={{0,32},{32,0},{1,33},{33,1},{2,34},{34,2},{3,35},{35,3},{4,36},{36... | collective-permute-start | bytes 221192 | tf_op jit(solution)/shard_map/ppermute | solution.py:155
  31.8 7.4 %collective-permute-start.6 = (bf16[16,2304]{1,0:T(8,128)(2,1)S(1)}, bf16[16,2304]{1,0:T(8,128)(2,1)S(1)}, u32[]{:S(2)}, u32[]{:S(2)}) collective-permute-start(bf16[16,2304]{1,0:T(8,128)(2,1)S(1)} %shard_map.82.s0), channel_id=1, source_target_pairs={{0,24},{8,16},{16,8},{24,0},{1,25},{9,17},{17,9},{25,1},{2,26},{10... | collective-permute-start | bytes 221192 | tf_op jit(solution)/shard_map/ppermute | solution.py:155
  37.0 8.1 %collective-permute-start.5 = (bf16[16,2304]{1,0:T(8,128)(2,1)S(1)}, bf16[16,2304]{1,0:T(8,128)(2,1)S(1)}, u32[]{:S(2)}, u32[]{:S(2)}) collective-permute-start(bf16[16,2304]{1,0:T(8,128)(2,1)S(1)} %shard_map.82.s0), channel_id=1, source_target_pairs={{0,16},{8,24},{16,0},{24,8},{1,17},{9,25},{17,1},{25,9},{2,18},{10... | collective-permute-start | bytes 221192 | tf_op jit(solution)/shard_map/ppermute | solution.py:155
  38.1 6.9 %collective-permute-start.4 = (bf16[16,2304]{1,0:T(8,128)(2,1)S(1)}, bf16[16,2304]{1,0:T(8,128)(2,1)S(1)}, u32[]{:S(2)}, u32[]{:S(2)}) collective-permute-start(bf16[16,2304]{1,0:T(8,128)(2,1)S(1)} %shard_map.82.s0), channel_id=1, source_target_pairs={{0,8},{8,0},{16,24},{24,16},{1,9},{9,1},{17,25},{25,17},{2,10},{10... | collective-permute-start | bytes 221192 | tf_op jit(solution)/shard_map/ppermute | solution.py:155
  45.1 0.8 %copy-start.4 = (bf16[8,16,2304]{2,1,0:T(8,128)(2,1)}, bf16[8,16,2304]{2,1,0:T(8,128)(2,1)S(1)}, u32[]{:S(2)}) copy-start(bf16[8,16,2304]{2,1,0:T(8,128)(2,1)S(1)} %shard_map.83) | copy-start | bytes 1769476
  45.9 12.1 %all-to-all-start.1 = ((bf16[8,16,2304]{2,1,0:T(8,128)(2,1)}), bf16[8,16,2304]{2,1,0:T(8,128)(2,1)}, u32[]{:S(2)}, u32[]{:S(2)}) async-start(bf16[8,16,2304]{2,1,0:T(8,128)(2,1)} %copy-done.4), calls=%async_computation.1 | async-start | bytes 1179648 | tf_op jit(solution)/shard_map/all_to_all | solution.py:232
  50.1 1.3 %copy-start.3 = (bf16[256,2304]{1,0:T(8,128)(2,1)S(1)}, bf16[256,2304]{1,0:T(8,128)(2,1)}, u32[]{:S(2)}) copy-start(bf16[256,2304]{1,0:T(8,128)(2,1)} %copy-done.2) | copy-start | bytes 3538948
  52.6 2.1 %copy-start = (bf16[4,2304,256]{2,1,0:T(8,128)(2,1)}, bf16[4,2304,256]{2,1,0:T(8,128)(2,1)S(1)}, u32[]{:S(2)}) copy-start(bf16[4,2304,256]{2,1,0:T(8,128)(2,1)S(1)} %shard_map.85.turned) | copy-start | bytes 14155780
  58.0 2.3 %copy-start.1 = (bf16[4,2304,256]{2,1,0:T(8,128)(2,1)S(1)}, bf16[4,2304,256]{2,1,0:T(8,128)(2,1)}, u32[]{:S(2)}) copy-start(bf16[4,2304,256]{2,1,0:T(8,128)(2,1)} %copy-done) | copy-start | bytes 14155780
  60.3 0.8 copy-start.6
  62.5 6.7 %copy-start.7 = (f32[4,8,256]{2,1,0:T(8,128)S(1)}, f32[4,8,256]{2,1,0:T(8,128)}, u32[]{:S(2)}) copy-start(f32[4,8,256]{2,1,0:T(8,128)} %copy-done.5) | copy-start | bytes 98308
  62.5 8.1 %collective-permute-start.8 = (bf16[128,256]{1,0:T(8,128)(2,1)S(1)}, bf16[128,256]{1,0:T(8,128)(2,1)S(1)}, u32[]{:S(2)}, u32[]{:S(2)}) collective-permute-start(bf16[128,256]{1,0:T(8,128)(2,1)S(1)} %shard_map.89), channel_id=1, source_target_pairs={{0,1},{1,0},{2,3},{3,2},{4,5},{5,4},{6,7},{7,6},{8,9},{9,8},{10,11... | collective-permute-start | bytes 196616 | tf_op jit(solution)/shard_map/ppermute | solution.py:155
  69.1 6.1 %collective-permute-start.7 = (bf16[128,256]{1,0:T(8,128)(2,1)S(1)}, bf16[128,256]{1,0:T(8,128)(2,1)S(1)}, u32[]{:S(2)}, u32[]{:S(2)}) collective-permute-start(bf16[128,256]{1,0:T(8,128)(2,1)S(1)} %shard_map.87), channel_id=1, source_target_pairs={{0,1},{1,0},{2,3},{3,2},{4,5},{5,4},{6,7},{7,6},{8,9},{9,8},{10,11... | collective-permute-start | bytes 196616 | tf_op jit(solution)/shard_map/ppermute | solution.py:155
  70.7 4.5 %collective-permute-start.9 = (bf16[128,256]{1,0:T(8,128)(2,1)S(1)}, bf16[128,256]{1,0:T(8,128)(2,1)S(1)}, u32[]{:S(2)}, u32[]{:S(2)}) collective-permute-start(bf16[128,256]{1,0:T(8,128)(2,1)S(1)} %shard_map.90), channel_id=1, source_target_pairs={{0,2},{1,3},{2,0},{3,1},{4,6},{5,7},{6,4},{7,5},{8,10},{9,11},{10,... | collective-permute-start | bytes 196616 | tf_op jit(solution)/shard_map/ppermute | solution.py:155
